TPU v7x, 32 devices: a whole 2x2x4 slice. The times are simulated.
32 devices in a mesh: dp: 2 (over core), expert: 4 (over y, x), mp: 4 (over z).
Axes of the slice: x: 2, y: 2, z: 4, core: 2. Of those that a mesh axis runs over, the one named last changes fastest.
Arguments:
- tokens: bfloat16 [512, 3072], P(('dp', 'expert')), may hold values from -6 to 6
- w_router: float32 [3072, 4], replicated, may hold values from -0.109375 to 0.109375
- expert_ids: int32 [512, 2], P(('dp', 'expert')), may hold values from 0 to 3, all different within a row; in each aligned block of 64 rows (0 to 63, 64 to 127, ...) at most 64 rows name the same one
- partner: int32 [4], replicated, may hold values from 0 to 3, as said below
- gate_weight: bfloat16 [4, 3072, 8192], P('expert', None, ('dp', 'mp')), may hold values from -0.109375 to 0.109375
- up_weight: bfloat16 [4, 3072, 8192], P('expert', None, ('dp', 'mp')), may hold values from -0.109375 to 0.109375
- down_weight: bfloat16 [4, 8192, 3072], P('expert', ('dp', 'mp')), may hold values from -0.0625 to 0.0625
- grad_out: bfloat16 [512, 3072], P(('dp', 'expert')), may hold values from -1.5 to 1.5
Outputs:
- mixed: bfloat16 [512, 3072], P(('dp', 'expert'))
- grad_tokens: bfloat16 [512, 3072], P(('dp', 'expert'))
- grad_router: float32 [3072, 4], replicated
- grad_gate: bfloat16 [4, 3072, 8192], P('expert', None, ('dp', 'mp'))
- grad_up: bfloat16 [4, 3072, 8192], P('expert', None, ('dp', 'mp'))
- grad_down: bfloat16 [4, 8192, 3072], P('expert', ('dp', 'mp'))
Inputs may be any that keep to these rules, and one draw needn't show every extreme that they name: `expert_ids`: each token names two different experts. Within each aligned block of 64 tokens no expert is named by more than 64 tokens, and in every draw some block names some expert exactly 64 times. A matching of the experts: partner[partner[e]] = e and partner[e] != e for every expert e.
All inputs are finite; a program needn't handle non-finite values.
Results may differ from a plain program's by a relative error of at most 0.019.
Values may be sent and summed in bfloat16 or wider, within the bound.
No kernel may reach another device: no remote copies, remote signals or barrier semaphores. Data moves between devices by JAX's collectives and lax.ppermute only.
A program may use at most 128 MiB of HBM per device.

v0:
```python
import jax
import jax.numpy as jnp
from jax import lax
from jax.sharding import PartitionSpec as P

exact_mode = lax.Precision.HIGHEST


def local(tokens, w_router, expert_ids, partner, gate_weight, up_weight, down_weight, grad_out):
    tok_rows, features = tokens.shape
    experts = w_router.shape[1]
    hid_part = gate_weight.shape[2]
    dp_count = lax.axis_size("dp")
    exp_count = lax.axis_size("expert")
    slot_count = min(tok_rows, 4 * tok_rows // experts)
    keep_count = 3 * slot_count // 4
    slot_total = experts * slot_count
    block_rows = exp_count * slot_count
    floats = tokens.astype(jnp.float32)
    logits = jnp.dot(floats, w_router, precision=exact_mode)
    chosen = (expert_ids[:, :, None] == lax.iota(jnp.int32, experts)[None, None, :]).astype(
        jnp.int32
    )
    chosen_float = chosen.astype(jnp.float32)
    picked = jnp.sum(logits[:, None, :] * chosen_float, axis=2)
    share_one = jax.nn.sigmoid(picked[:, 0] - picked[:, 1])
    shares = jnp.stack([share_one, 1.0 - share_one], axis=1)
    flat_choice = chosen.reshape(2 * tok_rows, experts)
    earlier = jnp.cumsum(flat_choice, axis=0) - flat_choice
    arrival = jnp.sum(earlier * flat_choice, axis=1).reshape(tok_rows, 2)
    partner_of = jnp.sum(chosen * partner[None, None, :], axis=2)
    target = jnp.where(arrival < keep_count, expert_ids, partner_of)
    slot_index = target * slot_count + arrival
    placing = (slot_index[:, :, None] == lax.iota(jnp.int32, slot_total)[None, None, :]).astype(
        jnp.bfloat16
    )
    send_tokens = jnp.einsum("tks,td->sd", placing, tokens, preferred_element_type=jnp.float32)
    send_tokens = send_tokens.astype(jnp.bfloat16).reshape(experts, slot_count, features)
    scaled = (shares[:, :, None] * grad_out.astype(jnp.float32)[:, None, :]).astype(jnp.bfloat16)
    send_cot = jnp.einsum("tks,tkd->sd", placing, scaled, preferred_element_type=jnp.float32)
    send_cot = send_cot.astype(jnp.bfloat16).reshape(experts, slot_count, features)

    def spread(buffer):
        arrived = lax.all_to_all(buffer, "expert", split_axis=0, concat_axis=0, tiled=True)
        return lax.all_gather(arrived, "dp", axis=0, tiled=True)

    rows_in = spread(send_tokens).reshape(-1, features)
    pieces = 1

    def combine(partial_value):
        summed = lax.psum(
            partial_value.reshape(dp_count, block_rows, features).astype(jnp.bfloat16), ("dp", "mp")
        ).astype(jnp.float32)
        own_rows = lax.dynamic_index_in_dim(summed, lax.axis_index("dp"), 0, keepdims=False)
        own_rows = own_rows.astype(jnp.bfloat16).reshape(exp_count, slot_count, features)
        restored = lax.all_to_all(own_rows, "expert", split_axis=0, concat_axis=0, tiled=True)
        return restored.reshape(slot_total, features)

    w_gate = gate_weight[0]
    w_up = up_weight[0]
    w_down = down_weight[0]
    pre_gate = jnp.dot(rows_in, w_gate, preferred_element_type=jnp.float32)
    pre_up = jnp.dot(rows_in, w_up, preferred_element_type=jnp.float32)
    sigmoid_gate = jax.nn.sigmoid(pre_gate)
    swished = pre_gate * sigmoid_gate
    hidden = (swished * pre_up).astype(jnp.bfloat16)
    down_split = w_down.reshape(hid_part, pieces, features // pieces)
    forward_terms = jnp.einsum(
        "prf,fqd->pqrd",
        hidden.reshape(dp_count, block_rows, hid_part),
        down_split,
        preferred_element_type=jnp.float32,
    )
    expert_out = combine(forward_terms)
    back_rows = jnp.einsum("tks,sd->tkd", placing, expert_out, preferred_element_type=jnp.float32)
    mixed = (shares[:, 0, None] * back_rows[:, 0] + shares[:, 1, None] * back_rows[:, 1]).astype(
        jnp.bfloat16
    )
    falling = grad_out.astype(jnp.float32)
    dshare = jnp.sum(falling[:, None, :] * back_rows, axis=2)
    dlogit = shares[:, 0] * shares[:, 1] * (dshare[:, 0] - dshare[:, 1])
    grad_logits = (chosen_float[:, 0] - chosen_float[:, 1]) * dlogit[:, None]
    router_term = lax.dot_general(
        floats, grad_logits, (((0,), (0,)), ((), ())), precision=exact_mode
    )
    grad_router = lax.psum(router_term.astype(jnp.bfloat16), ("dp", "expert")).astype(jnp.float32)
    router_back = jnp.dot(grad_logits, w_router.T, precision=exact_mode)
    cot_in = spread(send_cot).reshape(-1, features)
    dhidden = jnp.einsum("rd,fd->rf", cot_in, w_down, preferred_element_type=jnp.float32)
    up_grad = (dhidden * swished).astype(jnp.bfloat16)
    gate_grad = (dhidden * pre_up * sigmoid_gate * (1.0 + pre_gate * (1.0 - sigmoid_gate))).astype(
        jnp.bfloat16
    )
    grad_down = jnp.einsum("rf,rd->fd", hidden, cot_in, preferred_element_type=jnp.float32).astype(
        jnp.bfloat16
    )[None]
    grad_gate = jnp.einsum(
        "rd,rf->df", rows_in, gate_grad, preferred_element_type=jnp.float32
    ).astype(jnp.bfloat16)[None]
    grad_up = jnp.einsum("rd,rf->df", rows_in, up_grad, preferred_element_type=jnp.float32).astype(
        jnp.bfloat16
    )[None]
    gate_split = w_gate.reshape(pieces, features // pieces, hid_part)
    up_split = w_up.reshape(pieces, features // pieces, hid_part)
    backward_terms = jnp.einsum(
        "prf,qdf->pqrd",
        gate_grad.reshape(dp_count, block_rows, hid_part),
        gate_split,
        preferred_element_type=jnp.float32,
    )
    backward_terms = backward_terms + jnp.einsum(
        "prf,qdf->pqrd",
        up_grad.reshape(dp_count, block_rows, hid_part),
        up_split,
        preferred_element_type=jnp.float32,
    )
    row_grads = combine(backward_terms)
    grad_rows = jnp.einsum("tks,sd->tkd", placing, row_grads, preferred_element_type=jnp.float32)
    grad_tokens = (router_back + grad_rows[:, 0] + grad_rows[:, 1]).astype(jnp.bfloat16)
    return (mixed, grad_tokens, grad_router, grad_gate, grad_up, grad_down)


def solution(mesh):
    in_specs = (
        P(("dp", "expert"), None),
        P(),
        P(("dp", "expert"), None),
        P(),
        P("expert", None, ("dp", "mp")),
        P("expert", None, ("dp", "mp")),
        P("expert", ("dp", "mp"), None),
        P(("dp", "expert"), None),
    )
    out_specs = (
        P(("dp", "expert"), None),
        P(("dp", "expert"), None),
        P(),
        P("expert", None, ("dp", "mp")),
        P("expert", None, ("dp", "mp")),
        P("expert", ("dp", "mp"), None),
    )
    return jax.shard_map(local, mesh=mesh, in_specs=in_specs, out_specs=out_specs, check_vma=False)
```

profile of v0, /device:TPU:0, one launch (start us, length us, event | category | flops | bytes accessed | tf_op | source)
XLA Modules:
  0.0 329.6 jit_solution(508223752091180420)
XLA Ops:
  8.2 1.2 fusion.42
  14.2 24.8 %all_to_all.20 = bf16[4,64,3072]{2,1,0:T(8,128)(2,1)} all-to-all(bf16[4,64,3072]{2,1,0:T(8,128)(2,1)S(1)} %bitcast.108), channel_id=1, replica_groups=mesh['dp'=2,'expert'=4,'mp'=4] {'expert'}, dimensions={0} | all-to-all | bytes 3145728 | tf_op jit(solution)/shard_map/all_to_all | solution.py:44
  39.8 21.7 %all_to_all.21 = bf16[4,64,3072]{2,1,0:T(8,128)(2,1)} all-to-all(bf16[4,64,3072]{2,1,0:T(8,128)(2,1)S(1)} %bitcast.105), channel_id=1, replica_groups=mesh['dp'=2,'expert'=4,'mp'=4] {'expert'}, dimensions={0} | all-to-all | bytes 3145728 | tf_op jit(solution)/shard_map/all_to_all | solution.py:44
  61.6 6.5 %fusion.6 = f32[512,1024]{1,0:T(8,128)S(1)} fusion(bf16[512,3072]{1,0:T(8,128)(2,1)} %bitcast.120, bf16[1,1024,3072]{2,1,0:T(8,128)(2,1)} %param.14), kind=kOutput, calls=%fused_computation.6 | convolution fusion | flops 3221225472 | bytes 11534336 | tf_op jit(solution)/shard_map/rd,fd->rf/dot_general | solution.py:89
  68.1 5.4 %all-gather.3.cloned.1.call-done = bf16[8,64,3072]{2,1,0:T(8,128)(2,1)} async-done(((bf16[4,64,3072]{2,1,0:T(8,128)(2,1)}), bf16[8,64,3072]{2,1,0:T(8,128)(2,1)}) %all-gather.3.cloned.1.call-update) | async-done | bytes 3145744 | tf_op jit(solution)/shard_map/all_gather | solution.py:45
  73.5 6.6 %fusion.8 = f32[512,1024]{1,0:T(8,128)S(1)} fusion(bf16[512,3072]{1,0:T(8,128)(2,1)} %bitcast.116, bf16[1,3072,1024]{2,1,0:T(8,128)(2,1)} %param.13), kind=kOutput, calls=%fused_computation.8 | convolution fusion | flops 3221225472 | bytes 11534336 | tf_op jit(solution)/shard_map/dot_general | solution.py:63
  80.2 7.3 %multiply_convert_fusion.1 = (bf16[512,1024]{1,0:T(8,128)(2,1)S(1)}, bf16[512,1024]{1,0:T(8,128)(2,1)S(1)}, bf16[512,1024]{1,0:T(8,128)(2,1)S(1)}) fusion(f32[512,1024]{1,0:T(8,128)S(1)} %fusion.6, f32[512,1024]{1,0:T(8,128)S(1)} %fusion.8, bf16[512,3072]{1,0:T(8,128)(2,1)S(1)} %bitcast.118, bf16[1,3072,1024]{2,1,0:T(8,128)(2,1)} %param.12), kind=kOutput, calls=%fused_computation.28 | convolution fusion | flops 3229089792 | bytes 16777216 | tf_op jit(solution)/shard_map/dot_general | solution.py:62
  87.5 5.4 %fusion = f32[2,256,3072]{2,1,0:T(8,128)} fusion(bf16[2,256,1024]{2,1,0:T(8,128)(2,1)S(1)} %bitcast.123, bf16[1,3072,1024]{2,1,0:T(8,128)(2,1)S(1)} %bitcast.111), kind=kOutput, calls=%fused_computation | convolution fusion | flops 3221225472 | bytes 13631488 | tf_op jit(solution)/shard_map/prf,qdf->pqrd/dot_general | solution.py:111
  92.9 4.8 %fusion.14 = bf16[2,256,3072]{2,1,0:T(8,128)(2,1)} fusion(bf16[2,256,1024]{2,1,0:T(8,128)(2,1)S(1)} %bitcast.124, bf16[1,1024,3072]{2,1,0:T(8,128)(2,1)S(1)} %bitcast.113), kind=kOutput, calls=%fused_computation.16 | convolution fusion | flops 3222798336 | bytes 10485760 | tf_op jit(solution)/shard_map/prf,fqd->pqrd/dot_general | solution.py:68
  97.8 6.8 %add_convert_fusion = bf16[2,256,3072]{2,1,0:T(8,128)(2,1)} fusion(f32[2,256,3072]{2,1,0:T(8,128)} %fusion, bf16[2,256,1024]{2,1,0:T(8,128)(2,1)S(1)} %bitcast.122, bf16[1,3072,1024]{2,1,0:T(8,128)(2,1)S(1)} %bitcast.115), kind=kOutput, calls=%fused_computation.15 | convolution fusion | flops 3224371200 | bytes 16777216 | tf_op jit(solution)/shard_map/prf,qdf->pqrd/dot_general | solution.py:105
  104.6 137.8 %all-reduce.3.cloned.1.call-done = (bf16[2,256,3072]{2,1,0:T(8,128)(2,1)}, bf16[2,256,3072]{2,1,0:T(8,128)(2,1)}) async-done(((bf16[2,256,3072]{2,1,0:T(8,128)(2,1)}, bf16[2,256,3072]{2,1,0:T(8,128)(2,1)}), (bf16[2,256,3072]{2,1,0:T(8,128)(2,1)}, bf16[2,256,3072]{2,1,0:T(8,128)(2,1)})) %all-reduce.3.cloned.1.call-update) | async-done | bytes 6291472 | tf_op jit(solution)/shard_map/psum | solution.py:51
  242.4 2.7 convert_convert_fusion
  245.0 3.7 %all-to-all-start.3 = ((bf16[4,64,3072]{2,1,0:T(8,128)(2,1)}), bf16[4,64,3072]{2,1,0:T(8,128)(2,1)S(1)}, u32[]{:S(2)}, u32[]{:S(2)}) async-start(bf16[4,64,3072]{2,1,0:T(8,128)(2,1)} %bitcast.107), calls=%async_computation.3 | async-start | bytes 3145728 | tf_op jit(solution)/shard_map/all_to_all | solution.py:56
  248.8 8.5 %convert_bitcast_fusion = bf16[1,1024,3072]{2,1,0:T(8,128)(2,1)} fusion(bf16[512,1024]{1,0:T(8,128)(2,1)} %copy-done.10, bf16[512,3072]{1,0:T(8,128)(2,1)} %bitcast.121), kind=kOutput, calls=%fused_computation.12 | convolution fusion | flops 3224371200 | bytes 10485760 | tf_op jit(solution)/shard_map/rf,rd->fd/dot_general | solution.py:94
  257.4 1.3 convert_convert_fusion.1
  258.6 9.3 %all-to-all-done.3 = bf16[4,64,3072]{2,1,0:T(8,128)(2,1)S(1)} async-done(((bf16[4,64,3072]{2,1,0:T(8,128)(2,1)}), bf16[4,64,3072]{2,1,0:T(8,128)(2,1)S(1)}, u32[]{:S(2)}, u32[]{:S(2)}) %all-to-all-start.3) | async-done | bytes 1572896 | tf_op jit(solution)/shard_map/all_to_all | solution.py:56
  268.0 4.4 %all-to-all-start.1 = ((bf16[4,64,3072]{2,1,0:T(8,128)(2,1)}), bf16[4,64,3072]{2,1,0:T(8,128)(2,1)}, u32[]{:S(2)}, u32[]{:S(2)}) async-start(bf16[4,64,3072]{2,1,0:T(8,128)(2,1)} %bitcast.106), calls=%async_computation.1 | async-start | bytes 3145728 | tf_op jit(solution)/shard_map/all_to_all | solution.py:56
  272.4 8.5 %convert_bitcast_fusion.1 = bf16[1,3072,1024]{2,1,0:T(8,128)(2,1)} fusion(bf16[512,3072]{1,0:T(8,128)(2,1)} %bitcast.117, bf16[512,1024]{1,0:T(8,128)(2,1)} %copy-done.9), kind=kOutput, calls=%fused_computation.13 | convolution fusion | flops 3224371200 | bytes 10485760 | tf_op jit(solution)/shard_map/rd,rf->df/dot_general | solution.py:100
  280.9 5.4 %convert_bitcast_fusion.2 = bf16[1,3072,1024]{2,1,0:T(8,128)(2,1)} fusion(bf16[512,3072]{1,0:T(8,128)(2,1)S(1)} %bitcast.119, bf16[512,1024]{1,0:T(8,128)(2,1)S(1)} %copy-done.8), kind=kOutput, calls=%fused_computation.14 | convolution fusion | flops 3224371200 | bytes 10485760 | tf_op jit(solution)/shard_map/rd,rf->df/dot_general | solution.py:97
  286.3 1.6 fusion.28
  287.8 3.3 all-to-all-done.1
  291.1 2.1 multiply_reduce_fusion
  293.5 1.6 fusion.19
  295.1 26.4 %psum.23 = bf16[3072,4]{0,1:T(4,128)(2,1)S(1)} all-reduce(bf16[3072,4]{0,1:T(4,128)(2,1)S(1)} %fusion.20), channel_id=1, replica_groups=mesh['dp'=2,'expert'=4,'mp'=4] {'dp','expert'}, use_global_device_ids=true, to_apply=%region_8.9 | all-reduce | flops 12288 | bytes 49152 | tf_op jit(solution)/shard_map/psum | solution.py:86
  (66 shorter events, 8.5 us)
Async XLA Ops:
  7.2 1.0 copy-start
  7.2 54.4 %all-gather.5.cloned.1.call-start = ((), (), s32[]{:S(2)}) async-start(), calls=%async_computation.5 | async-start | bytes 4718592 | tf_op jit(solution)/shard_map/all_gather | solution.py:45
  39.0 34.5 %all-gather.3.cloned.1.call-start = ((), (), s32[]{:S(2)}) async-start(), calls=%async_computation.4 | async-start | bytes 4718592 | tf_op jit(solution)/shard_map/all_gather | solution.py:45
  61.5 180.9 %all-reduce.3.cloned.1.call-start = ((), (), s32[]{:S(2)}) async-start(), calls=%async_computation.6 | async-start | bytes 12582912 | tf_op jit(solution)/shard_map/psum | solution.py:51
  73.5 6.6 %copy-start.5 = (bf16[8,64,3072]{2,1,0:T(8,128)(2,1)S(1)}, bf16[8,64,3072]{2,1,0:T(8,128)(2,1)}, u32[]{:S(2)}) copy-start(bf16[8,64,3072]{2,1,0:T(8,128)(2,1)} %all-gather.3.cloned.1.call-done) | copy-start | bytes 9437188
  73.5 14.0 %slice-start = ((s8[6291456]{0:T(1024)(128)(4,1)}), s8[4194304]{0:T(1024)(128)(4,1)S(1)}, s32[]{:S(2)}) async-start(s8[6291456]{0:T(1024)(128)(4,1)} %bitcast.110), calls=%async_computation.7 | async-start | bytes 8388608
  73.5 19.4 %slice-start.2 = ((s8[6291456]{0:T(1024)(128)(4,1)}), s8[4194304]{0:T(1024)(128)(4,1)S(1)}, s32[]{:S(2)}) async-start(s8[6291456]{0:T(1024)(128)(4,1)} %bitcast.112), calls=%async_computation.9 | async-start | bytes 8388608
  80.1 7.4 %slice-start.1 = ((s8[6291456]{0:T(1024)(128)(4,1)}), s8[2097152]{0:T(1024)(128)(4,1)S(1)}, s32[]{:S(2)}) async-start(s8[6291456]{0:T(1024)(128)(4,1)} %bitcast.110), calls=%async_computation.8 | async-start | bytes 4194304
  80.1 12.8 %slice-start.3 = ((s8[6291456]{0:T(1024)(128)(4,1)}), s8[2097152]{0:T(1024)(128)(4,1)S(1)}, s32[]{:S(2)}) async-start(s8[6291456]{0:T(1024)(128)(4,1)} %bitcast.112), calls=%async_computation.10 | async-start | bytes 4194304
  80.1 17.6 %slice-start.4 = ((s8[6291456]{0:T(1024)(128)(4,1)}), s8[4194304]{0:T(1024)(128)(4,1)S(1)}, s32[]{:S(2)}) async-start(s8[6291456]{0:T(1024)(128)(4,1)} %bitcast.114), calls=%async_computation.11 | async-start | bytes 8388608
  87.5 5.4 %copy-start.9 = (bf16[512,1024]{1,0:T(8,128)(2,1)}, bf16[512,1024]{1,0:T(8,128)(2,1)S(1)}, u32[]{:S(2)}) copy-start(bf16[512,1024]{1,0:T(8,128)(2,1)S(1)} %get-tuple-element.11) | copy-start | bytes 3145732
  87.5 5.4 %copy-start.10 = (bf16[512,1024]{1,0:T(8,128)(2,1)}, bf16[512,1024]{1,0:T(8,128)(2,1)S(1)}, u32[]{:S(2)}) copy-start(bf16[512,1024]{1,0:T(8,128)(2,1)S(1)} %get-tuple-element.12) | copy-start | bytes 3145732
  87.5 10.3 %copy-start.7 = (bf16[512,1024]{1,0:T(8,128)(2,1)}, bf16[512,1024]{1,0:T(8,128)(2,1)S(1)}, u32[]{:S(2)}) copy-start(bf16[512,1024]{1,0:T(8,128)(2,1)S(1)} %get-tuple-element.10) | copy-start | bytes 3145732
  87.5 10.2 %slice-start.5 = ((s8[6291456]{0:T(1024)(128)(4,1)}), s8[2097152]{0:T(1024)(128)(4,1)S(1)}, s32[]{:S(2)}) async-start(s8[6291456]{0:T(1024)(128)(4,1)} %bitcast.114), calls=%async_computation.12 | async-start | bytes 4194304
  242.4 6.4 %copy-start.4 = (s32[64,2]{0,1:T(2,128)S(1)}, s32[64,2]{0,1:T(2,128)}, u32[]{:S(2)}) copy-start(s32[64,2]{0,1:T(2,128)} %param.10) | copy-start | bytes 1540
  245.0 23.0 %all-to-all-start.3 = ((bf16[4,64,3072]{2,1,0:T(8,128)(2,1)}), bf16[4,64,3072]{2,1,0:T(8,128)(2,1)S(1)}, u32[]{:S(2)}, u32[]{:S(2)}) async-start(bf16[4,64,3072]{2,1,0:T(8,128)(2,1)} %bitcast.107), calls=%async_computation.3 | async-start | bytes 3145728 | tf_op jit(solution)/shard_map/all_to_all | solution.py:56
  248.8 8.6 %copy-start.2 = (bf16[2,256,3072]{2,1,0:T(8,128)(2,1)S(1)}, bf16[2,256,3072]{2,1,0:T(8,128)(2,1)}, u32[]{:S(2)}) copy-start(bf16[2,256,3072]{2,1,0:T(8,128)(2,1)} %get-tuple-element.6) | copy-start | bytes 9437188
  268.0 23.1 %all-to-all-start.1 = ((bf16[4,64,3072]{2,1,0:T(8,128)(2,1)}), bf16[4,64,3072]{2,1,0:T(8,128)(2,1)}, u32[]{:S(2)}, u32[]{:S(2)}) async-start(bf16[4,64,3072]{2,1,0:T(8,128)(2,1)} %bitcast.106), calls=%async_computation.1 | async-start | bytes 3145728 | tf_op jit(solution)/shard_map/all_to_all | solution.py:56
  272.4 8.5 %copy-start.6 = (bf16[8,64,3072]{2,1,0:T(8,128)(2,1)S(1)}, bf16[8,64,3072]{2,1,0:T(8,128)(2,1)}, u32[]{:S(2)}) copy-start(bf16[8,64,3072]{2,1,0:T(8,128)(2,1)} %all-gather.3.cloned.1.call-done) | copy-start | bytes 9437188
  272.4 8.5 %copy-start.8 = (bf16[512,1024]{1,0:T(8,128)(2,1)S(1)}, bf16[512,1024]{1,0:T(8,128)(2,1)}, u32[]{:S(2)}) copy-start(bf16[512,1024]{1,0:T(8,128)(2,1)} %copy-done.7) | copy-start | bytes 3145732
  286.3 7.2 %copy-start.3 = (f32[3072,4]{0,1:T(4,128)S(1)}, f32[3072,4]{0,1:T(4,128)}, u32[]{:S(2)}) copy-start(f32[3072,4]{0,1:T(4,128)} %param.9) | copy-start | bytes 147460
  291.1 2.4 copy-start.1
Sparse Core Ops, SparseCore 0:
  39.1 11.8 all-gather.4
  61.6 11.8 all-gather.2
  104.7 137.5 all-reduce.2
where the time goes:
time: 330 us
  waiting for transfers between devices  156 us (47%)
  blocking collectives  73 us (22%)
  matrix products  67.8 us (21%)
  between operations  14.1 us (4%)
  other arithmetic  9.3 us (3%)
  starting transfers between devices  8.22 us (2%)
    psum x1, waiting for transfers between devices, combine(): lax.psum(partial_value.reshape(dp_count, block_rows, features).astype(jnp...  138 us
    all_to_all x2, blocking collectives, spread(): lax.all_to_all(buffer, 'expert', split_axis=0, concat_axis=0, tiled=True)  46.6 us
    psum x1, blocking collectives, local(): lax.psum(router_term.astype(jnp.bfloat16), ('dp', 'expert'))  26.4 us
    all_to_all x2, waiting for transfers between devices, combine(): lax.all_to_all(own_rows, 'expert', split_axis=0, concat_axis=0, tiled=True)  12.6 us
    dot_general x1, matrix products, local(): jnp.einsum('rf,rd->fd', hidden, cot_in, preferred_element_type=jnp.float32)  8.54 us
    dot_general x1, matrix products, local(): jnp.einsum('rd,rf->df', rows_in, up_grad, preferred_element_type=jnp.floa...  8.51 us
    all_to_all x2, starting transfers between devices, combine(): lax.all_to_all(own_rows, 'expert', split_axis=0, concat_axis=0, tiled=True)  8.1 us
    dot_general x1, matrix products, local(): pre_gate = jnp.dot(rows_in, w_gate, preferred_element_type=jnp.float32)  7.32 us
  transfers between devices with their start and end apart: 5, of which 4 were waited for; matrix products, arithmetic and copies ran while one was open for 10% of the time, Pallas kernels for 0%

commit v1 on v0

v1 whole, which is shorter than its diff:
```python
import jax
import jax.numpy as jnp
from jax import lax
from jax.sharding import PartitionSpec as P


def split3(values):
    high = values.astype(jnp.bfloat16)
    rest = values - high.astype(jnp.float32)
    middle = rest.astype(jnp.bfloat16)
    low = (rest - middle.astype(jnp.float32)).astype(jnp.bfloat16)
    return high, middle, low


def routing(tokens, w_router, expert_ids, partner):
    tok_rows = tokens.shape[0]
    experts = w_router.shape[1]
    slot_count = min(tok_rows, 4 * tok_rows // experts)
    keep_count = 3 * slot_count // 4
    pieces = jnp.concatenate(split3(w_router), axis=1)
    logits = jnp.dot(tokens, pieces, preferred_element_type=jnp.float32)
    logits = logits.reshape(tok_rows, 3, experts)
    logits = (logits[:, 2] + logits[:, 1]) + logits[:, 0]
    columns = lax.broadcasted_iota(jnp.int32, (tok_rows, experts), 1)
    first = expert_ids[:, :1] == columns
    second = expert_ids[:, 1:] == columns
    first_float = first.astype(jnp.float32)
    second_float = second.astype(jnp.float32)
    difference = jnp.sum(logits * (first_float - second_float), axis=1, keepdims=True)
    share_one = jax.nn.sigmoid(difference)
    share_two = 1.0 - share_one
    rows = lax.broadcasted_iota(jnp.int32, (tok_rows, tok_rows), 0)
    before = (lax.broadcasted_iota(jnp.int32, (tok_rows, tok_rows), 1) < rows).astype(jnp.bfloat16)
    named = (first_float + second_float).astype(jnp.bfloat16)
    earlier = jnp.dot(before, named, preferred_element_type=jnp.float32)
    arrival_one = jnp.sum(earlier * first_float, axis=1, keepdims=True)
    arrival_two = jnp.sum(earlier * second_float, axis=1, keepdims=True)
    mate = partner[None, :]
    mate_one = jnp.sum(jnp.where(first, mate, 0), axis=1, keepdims=True)
    mate_two = jnp.sum(jnp.where(second, mate, 0), axis=1, keepdims=True)
    target_one = jnp.where(arrival_one < keep_count, expert_ids[:, :1], mate_one)
    target_two = jnp.where(arrival_two < keep_count, expert_ids[:, 1:], mate_two)
    lands_one = (target_one == columns).astype(jnp.float32)
    lands_two = (target_two == columns).astype(jnp.float32)
    weight = share_one * lands_one + share_two * lands_two
    slope = share_one * share_two * (lands_one - lands_two)
    return weight, slope, first_float - second_float


def swap(values, axis, flip):
    size = lax.axis_size(axis)
    return lax.ppermute(values, axis, [(place, place ^ flip) for place in range(size)])


def bits(axis):
    return [1 << bit for bit in range(lax.axis_size(axis).bit_length() - 1)]


def few():
    return lax.axis_size("dp") * lax.axis_size("expert") <= 8


def own_place():
    if few():
        return 0
    return lax.axis_index("dp") * lax.axis_size("expert") + lax.axis_index("expert")


def spread(block):
    if not few():
        return [lax.all_gather(block, ("dp", "expert"), axis=0, tiled=True)]
    if lax.axis_size("expert") == 4:
        half = block.shape[1] // 2
        beside = swap(block, "expert", 1)
        above = swap(block, "expert", 2)
        across = jnp.concatenate(
            [swap(above[:, :half], "expert", 1), swap(beside[:, half:], "expert", 2)], axis=1
        )
        found = [block, beside, above, across]
    else:
        found = [block]
        for flip in bits("expert"):
            found = found + [swap(item, "expert", flip) for item in found]
    for flip in bits("dp"):
        found = found + [swap(item, "dp", flip) for item in found]
    return found


def spread_small(block):
    if not few():
        return lax.all_gather(block, ("dp", "expert"), axis=0, tiled=False)
    found = block[None]
    for axis in ("expert", "dp"):
        for flip in bits(axis):
            found = jnp.concatenate([found, swap(found, axis, flip)], axis=0)
    return found


def total(values):
    if not few():
        return lax.psum(values, ("dp", "expert", "mp"))
    experts = lax.axis_size("expert")
    for axis, scale in (("expert", 1), ("dp", experts), ("mp", 0)):
        for flip in bits(axis):
            arrived = swap(values, axis, flip)
            if scale:
                arrived = arrived.reshape(-1, 2, flip * scale, values.shape[1])
                arrived = jnp.flip(arrived, axis=1).reshape(values.shape)
            values = values + arrived
    return values


def sum_over_mp(values):
    if lax.axis_size("mp") == 1:
        return values.astype(jnp.bfloat16)
    half = values.shape[1] // 2
    odd = (lax.axis_index("mp") & 1) == 1
    left, right = values[:, :half], values[:, half:]
    kept = jnp.where(odd, right, left) + swap(
        jnp.where(odd, left, right).astype(jnp.bfloat16), "mp", 1
    ).astype(jnp.float32)
    kept = kept.astype(jnp.bfloat16)
    for flip in bits("mp")[1:]:
        kept = (kept.astype(jnp.float32) + swap(kept, "mp", flip).astype(jnp.float32)).astype(
            jnp.bfloat16
        )
    other = swap(kept, "mp", 1)
    return jnp.concatenate([jnp.where(odd, other, kept), jnp.where(odd, kept, other)], axis=1)


def collect(partial_value, tok_rows):
    if not few():
        own = lax.psum_scatter(
            partial_value.astype(jnp.bfloat16), ("dp", "expert"), scatter_dimension=0, tiled=True
        )
        return lax.psum(own, "mp")
    features = partial_value.shape[1]
    parts = partial_value.reshape(-1, tok_rows, features)
    blocks = lax.axis_size("expert")
    for flip in reversed(bits("dp")):
        grouped = parts.reshape(2, -1, tok_rows, features)
        parts = grouped[0] + swap(grouped[1].astype(jnp.bfloat16), "dp", flip).astype(jnp.float32)
    ways = bits("expert")
    width = features // len(ways)
    sums = []
    for turn in range(len(ways)):
        piece = parts[:, :, turn * width : (turn + 1) * width]
        done = []
        left = list(range(blocks))
        held = {place: piece[place] for place in left}
        for flip in ways[turn:] + ways[:turn]:
            sent = [place for place in held if place & flip]
            arrived = swap(
                jnp.stack([held[place] for place in sent]).astype(jnp.bfloat16), "expert", flip
            ).astype(jnp.float32)
            for number, place in enumerate(sent):
                held[place ^ flip] = held[place ^ flip] + arrived[number]
                del held[place]
        sums.append(sum_over_mp(held[0]))
    return jnp.concatenate(sums, axis=1)


def local(tokens, w_router, expert_ids, partner, gate_weight, up_weight, down_weight, grad_out):
    tok_rows = tokens.shape[0]
    experts = w_router.shape[1]
    all_tokens = jnp.concatenate(spread(tokens), axis=0)
    all_grads = jnp.concatenate(spread(grad_out), axis=0)
    weight, slope, sign = routing(tokens, w_router, expert_ids, partner)
    small = spread_small(jnp.concatenate([weight, slope, sign], axis=1))
    blocks = small.shape[0]
    small = small.reshape(blocks * tok_rows, 3 * experts)
    mine = (lax.iota(jnp.int32, experts) == lax.axis_index("expert")).astype(jnp.float32)
    weight_all = jnp.sum(small[:, :experts] * mine, axis=1, keepdims=True)
    slope_all = jnp.sum(small[:, experts : 2 * experts] * mine, axis=1)
    sign_all = small[:, 2 * experts :]

    w_gate = gate_weight[0]
    w_up = up_weight[0]
    w_down = down_weight[0]
    pre_gate = jnp.dot(all_tokens, w_gate, preferred_element_type=jnp.float32)
    pre_up = jnp.dot(all_tokens, w_up, preferred_element_type=jnp.float32)
    sigmoid_gate = jax.nn.sigmoid(pre_gate)
    swished = pre_gate * sigmoid_gate
    product = swished * pre_up
    hidden = (weight_all * product).astype(jnp.bfloat16)
    mixed = collect(jnp.dot(hidden, w_down, preferred_element_type=jnp.float32), tok_rows)

    back = jnp.einsum("rd,fd->rf", all_grads, w_down, preferred_element_type=jnp.float32)
    dshare = jnp.sum(product * back, axis=1)
    dhidden = weight_all * back
    up_grad = (dhidden * swished).astype(jnp.bfloat16)
    gate_grad = (dhidden * pre_up * sigmoid_gate * (1.0 + pre_gate * (1.0 - sigmoid_gate))).astype(
        jnp.bfloat16
    )
    dlogit = total((slope_all * dshare).reshape(blocks, tok_rows))
    row_grads = collect(
        jnp.einsum("rf,df->rd", gate_grad, w_gate, preferred_element_type=jnp.float32)
        + jnp.einsum("rf,df->rd", up_grad, w_up, preferred_element_type=jnp.float32),
        tok_rows,
    )
    grad_down = jnp.einsum("rf,rd->fd", hidden, all_grads, preferred_element_type=jnp.float32)
    grad_gate = jnp.einsum("rd,rf->df", all_tokens, gate_grad, preferred_element_type=jnp.float32)
    grad_up = jnp.einsum("rd,rf->df", all_tokens, up_grad, preferred_element_type=jnp.float32)

    grad_logits = sign_all * dlogit.reshape(-1, 1)
    pieces = jnp.concatenate(split3(grad_logits), axis=1)
    grad_router = jnp.einsum("rd,re->de", all_tokens, pieces, preferred_element_type=jnp.float32)
    grad_router = (
        grad_router[:, 2 * experts :] + grad_router[:, experts : 2 * experts]
    ) + grad_router[:, :experts]
    own_logits = lax.dynamic_slice_in_dim(grad_logits, own_place() * tok_rows, tok_rows, 0)
    router_back = jnp.dot(own_logits, w_router.T, precision=lax.Precision.HIGHEST)
    grad_tokens = (router_back + row_grads.astype(jnp.float32)).astype(jnp.bfloat16)
    return (
        mixed,
        grad_tokens,
        grad_router,
        grad_gate.astype(jnp.bfloat16)[None],
        grad_up.astype(jnp.bfloat16)[None],
        grad_down.astype(jnp.bfloat16)[None],
    )


def solution(mesh):
    in_specs = (
        P(("dp", "expert"), None),
        P(),
        P(("dp", "expert"), None),
        P(),
        P("expert", None, ("dp", "mp")),
        P("expert", None, ("dp", "mp")),
        P("expert", ("dp", "mp"), None),
        P(("dp", "expert"), None),
    )
    out_specs = (
        P(("dp", "expert"), None),
        P(("dp", "expert"), None),
        P(),
        P("expert", None, ("dp", "mp")),
        P("expert", None, ("dp", "mp")),
        P("expert", ("dp", "mp"), None),
    )
    return jax.shard_map(local, mesh=mesh, in_specs=in_specs, out_specs=out_specs, check_vma=False)
```

time: 330 us -> 188 us (0.57)
  waiting for transfers between devices: 156 us -> 44.2 us
  blocking collectives: 73 us -> 0 us
  starting transfers between devices: 8.22 us -> 42.2 us
  local copies, waits for them, and re-layouts: 1.39 us -> 18.8 us
  between operations: 14.1 us -> 1.31 us
  other arithmetic: 9.3 us -> 14.3 us
    psum x1 -> x0, waiting for transfers between devices: 138 us -> none  [combine(): lax.psum(partial_value.reshape(dp_count, block_rows, features).astype(jnp...]
    all_to_all x2 -> x0, blocking collectives: 46.6 us -> none  [spread(): lax.all_to_all(buffer, 'expert', split_axis=0, concat_axis=0, tiled=True)]
    ppermute x0 -> x46, waiting for transfers between devices: none -> 44.2 us  [swap(): lax.ppermute(values, axis, [(place, place ^ flip) for place in range(size)])]
    ppermute x0 -> x46, starting transfers between devices: none -> 42.2 us  [swap(): lax.ppermute(values, axis, [(place, place ^ flip) for place in range(size)])]
    psum x1 -> x0, blocking collectives: 26.4 us -> none  [local(): lax.psum(router_term.astype(jnp.bfloat16), ('dp', 'expert'))]
    all_to_all x2 -> x0, waiting for transfers between devices: 12.6 us -> none  [combine(): lax.all_to_all(own_rows, 'expert', split_axis=0, concat_axis=0, tiled=True)]
    unnamed x35 -> x48, local copies, waits for them, and re-layouts: 1.04 us -> 9.95 us
    all_to_all x2 -> x0, starting transfers between devices: 8.1 us -> none  [combine(): lax.all_to_all(own_rows, 'expert', split_axis=0, concat_axis=0, tiled=True)]
  transfers between devices with their start and end apart: 5 -> 46, of which waited for: 4 -> 24; matrix products, arithmetic and copies ran while one was open for 10% -> 44% of each run, Pallas kernels for 0% -> 0%
where the time goes in v1:
time: 188 us; the launch traced here: 187 us
  matrix products  66 us (35%)
  waiting for transfers between devices  44.2 us (24%)
  starting transfers between devices  42.2 us (22%)
  local copies, waits for them, and re-layouts  18.8 us (10%)
  other arithmetic  14.3 us (8%)
    ppermute x46, waiting for transfers between devices, swap(): lax.ppermute(values, axis, [(place, place ^ flip) for place in range(size)])  44.2 us
    ppermute x46, starting transfers between devices, swap(): lax.ppermute(values, axis, [(place, place ^ flip) for place in range(size)])  42.2 us
    dot_general x1, matrix products, local(): jnp.einsum('rf,df->rd', gate_grad, w_gate, preferred_element_type=jnp.flo...  11.1 us
    unnamed x48, local copies, waits for them, and re-layouts  9.95 us
    dot_general x1, matrix products, local(): jnp.einsum('rf,df->rd', up_grad, w_up, preferred_element_type=jnp.float32)  9.28 us
    dot_general x1, matrix products, local(): jnp.einsum('rd,fd->rf', all_grads, w_down, preferred_element_type=jnp.flo...  8.32 us
    dot_general x1, matrix products, local(): jnp.einsum('rd,rf->df', all_tokens, gate_grad, preferred_element_type=jnp...  6.83 us
    dot_general x1, matrix products, local(): jnp.einsum('rd,rf->df', all_tokens, up_grad, preferred_element_type=jnp.f...  6.74 us
  transfers between devices with their start and end apart: 46, of which 24 were waited for; matrix products, arithmetic and copies ran while one was open for 44% of the time, Pallas kernels for 0%

profile of v1, /device:TPU:0, one launch (start us, length us, event | category | flops | bytes accessed | tf_op | source)
XLA Modules:
  0.0 186.8 jit_solution(2988483725685028755)
XLA Ops:
  0.6 3.0 %collective-permute-start.3 = (bf16[64,3072]{1,0:T(8,128)(2,1)}, bf16[64,3072]{1,0:T(8,128)(2,1)}, u32[]{:S(2)}, u32[]{:S(2)}) collective-permute-start(bf16[64,3072]{1,0:T(8,128)(2,1)} %param.8), channel_id=1, source_target_pairs={{0,4},{4,0},{8,12},{12,8},{1,5},{5,1},{9,13},{13,9},{2,6},{6,2},{1... | collective-permute-start | bytes 1179656 | tf_op jit(solution)/shard_map/ppermute | solution.py:52
  14.2 2.5 %collective-permute-start.1 = (f32[2,64,12]{1,2,0:T(8,128)}, f32[2,64,12]{1,2,0:T(8,128)}, u32[]{:S(2)}, u32[]{:S(2)}) collective-permute-start(f32[2,64,12]{1,2,0:T(8,128)} %pad_maximum_fusion.7), channel_id=1, source_target_pairs={{0,8},{4,12},{8,0},{12,4},{1,9},{5,13},{9,1},{13,5},{2,10},{6,14},... | collective-permute-start | bytes 18440 | tf_op jit(solution)/shard_map/ppermute | solution.py:52
  30.9 2.4 %collective-permute-done.23 = bf16[64,3072]{1,0:T(8,128)(2,1)} collective-permute-done((bf16[64,3072]{1,0:T(8,128)(2,1)}, bf16[64,3072]{1,0:T(8,128)(2,1)}, u32[]{:S(2)}, u32[]{:S(2)}) %collective-permute-start.23) | collective-permute-done | bytes 393248 | tf_op jit(solution)/shard_map/ppermute | solution.py:52
  42.8 3.4 %collective-permute-done.25 = bf16[64,1536]{1,0:T(8,128)(2,1)S(1)} collective-permute-done((bf16[64,1536]{1,0:T(8,128)(2,1)S(1)}, bf16[64,1536]{1,0:T(8,128)(2,1)S(1)}, u32[]{:S(2)}, u32[]{:S(2)}) %collective-permute-start.25) | collective-permute-done | bytes 196640 | tf_op jit(solution)/shard_map/ppermute | solution.py:52
  48.6 4.8 %fusion.6 = f32[512,1024]{1,0:T(8,128)} fusion(bf16[512,3072]{1,0:T(8,128)(2,1)S(1)} %constant_dynamic-update-slice_fusion, bf16[1,3072,1024]{2,1,0:T(8,128)(2,1)S(1)} %copy-done.6), kind=kOutput, calls=%fused_computation.6 | convolution fusion | flops 3221225472 | bytes 11534336 | tf_op jit(solution)/shard_map/dot_general | solution.py:181
  53.4 4.8 %fusion.10 = f32[512,1024]{1,0:T(8,128)} fusion(bf16[512,3072]{1,0:T(8,128)(2,1)S(1)} %constant_dynamic-update-slice_fusion, bf16[1,3072,1024]{2,1,0:T(8,128)(2,1)S(1)} %bitcast.105), kind=kOutput, calls=%fused_computation.10 | convolution fusion | flops 3221225472 | bytes 11534336 | tf_op jit(solution)/shard_map/dot_general | solution.py:180
  58.2 8.3 %multiply_reduce_fusion = (f32[512]{0:T(512)S(1)}, bf16[512,1024]{1,0:T(8,128)(2,1)}, bf16[512,1024]{1,0:T(8,128)(2,1)S(1)}, bf16[512,1024]{1,0:T(8,128)(2,1)}) fusion(f32[512,1024]{1,0:T(8,128)S(1)} %copy-done.9, f32[512,1024]{1,0:T(8,128)} %fusion.10, f32[512]{0:T(512)S(1)} %get-tuple-element.7, ...), kind=kOutput, calls=%fused_computation.22 | convolution fusion | flops 3231186432 | bytes 16781312 | tf_op jit(solution)/shard_map/rd,fd->rf/dot_general | solution.py:188
  66.6 3.5 %fusion.2 = f32[512,3072]{1,0:T(8,128)S(1)} fusion(bf16[512,1024]{1,0:T(8,128)(2,1)S(1)} %get-tuple-element.23, bf16[1,1024,3072]{2,1,0:T(8,128)(2,1)S(1)} %bitcast.103), kind=kOutput, calls=%fused_computation.2 | convolution fusion | flops 3221225472 | bytes 13631488 | tf_op jit(solution)/shard_map/dot_general | solution.py:186
  70.0 2.6 %copy-done = f32[512,3072]{1,0:T(8,128)} copy-done((f32[512,3072]{1,0:T(8,128)}, f32[512,3072]{1,0:T(8,128)S(1)}, u32[]{:S(2)}) %copy-start) | copy-done | bytes 6291480
  75.0 9.3 %fusion.4 = f32[512,3072]{1,0:T(8,128)} fusion(bf16[512,1024]{1,0:T(8,128)(2,1)} %get-tuple-element.24, bf16[1,3072,1024]{2,1,0:T(8,128)(2,1)} %param.13), kind=kOutput, calls=%fused_computation.4 | convolution fusion | flops 3221225472 | bytes 13631488 | tf_op jit(solution)/shard_map/rf,df->rd/dot_general | solution.py:198
  84.9 11.1 %fusion.12 = f32[512,3072]{1,0:T(8,128)} fusion(f32[512,3072]{1,0:T(8,128)} %fusion.4, bf16[512,1024]{1,0:T(8,128)(2,1)} %get-tuple-element.22, bf16[1,3072,1024]{2,1,0:T(8,128)(2,1)} %param.12), kind=kOutput, calls=%fused_computation.15 | convolution fusion | flops 3222798336 | bytes 19922944 | tf_op jit(solution)/shard_map/rf,df->rd/dot_general | solution.py:197
  96.1 6.8 %convert_bitcast_fusion.2 = bf16[1,3072,1024]{2,1,0:T(8,128)(2,1)} fusion(bf16[512,3072]{1,0:T(8,128)(2,1)S(1)} %constant_dynamic-update-slice_fusion, bf16[512,1024]{1,0:T(8,128)(2,1)} %get-tuple-element.22), kind=kOutput, calls=%fused_computation.14 | convolution fusion | flops 3224371200 | bytes 10485760 | tf_op jit(solution)/shard_map/rd,rf->df/dot_general | solution.py:202
  104.4 6.7 %convert_bitcast_fusion.1 = bf16[1,3072,1024]{2,1,0:T(8,128)(2,1)} fusion(bf16[512,3072]{1,0:T(8,128)(2,1)S(1)} %constant_dynamic-update-slice_fusion, bf16[512,1024]{1,0:T(8,128)(2,1)} %get-tuple-element.24), kind=kOutput, calls=%fused_computation.13 | convolution fusion | flops 3224371200 | bytes 10485760 | tf_op jit(solution)/shard_map/rd,rf->df/dot_general | solution.py:203
  111.1 2.7 %collective-permute-start.34 = (f32[8,64]{1,0:T(8,128)S(1)}, f32[8,64]{1,0:T(8,128)S(1)}, u32[]{:S(2)}, u32[]{:S(2)}) collective-permute-start(f32[8,64]{1,0:T(8,128)S(1)} %add.172), channel_id=1, source_target_pairs={{0,2},{1,3},{2,0},{3,1},{4,6},{5,7},{6,4},{7,5},{8,10},{9,11},{10,... | collective-permute-start | bytes 6152 | tf_op jit(solution)/shard_map/ppermute | solution.py:52
  113.8 5.4 %convert_bitcast_fusion = bf16[1,1024,3072]{2,1,0:T(8,128)(2,1)} fusion(bf16[512,1024]{1,0:T(8,128)(2,1)S(1)} %copy-done.8, bf16[512,3072]{1,0:T(8,128)(2,1)S(1)} %copy-done.4), kind=kOutput, calls=%fused_computation.12 | convolution fusion | flops 3224371200 | bytes 10485760 | tf_op jit(solution)/shard_map/rf,rd->fd/dot_general | solution.py:201
  121.5 2.4 %fusion.35 = f32[3072,12]{0,1:T(8,128)S(1)} fusion(bf16[512,3072]{1,0:T(8,128)(2,1)} %copy-done.1, bf16[512,4]{0,1:T(4,128)(2,1)S(1)} %get-tuple-element.49, bf16[512,4]{0,1:T(4,128)(2,1)S(1)} %get-tuple-element.48, bf16[512,4]{0,1:T(4,128)(2,1)S(1)} %get-tuple-element.13), kind=kOutput, calls=%fused_computation.104 | convolution fusion | flops 37785600 | bytes 3305472 | tf_op jit(solution)/shard_map/rd,re->de/dot_general | solution.py:207
  124.6 2.1 %fusion.62 = (bf16[4,64,3072]{2,1,0:T(8,128)(2,1)S(1)}, f32[4,64,3072]{2,1,0:T(8,128)S(1)}) fusion(f32[4,64,3072]{2,1,0:T(8,128)S(1)} %bitcast.95, bf16[4,64,3072]{2,1,0:T(8,128)(2,1)} %collective-permute-done.11), kind=kLoop, calls=%fused_computation.157 | loop fusion | flops 2359296 | bytes 9437184 | tf_op jit(solution)/shard_map/convert.10
  129.9 2.1 %fusion.61 = (bf16[4,64,3072]{2,1,0:T(8,128)(2,1)S(1)}, f32[4,64,3072]{2,1,0:T(8,128)S(1)}) fusion(f32[4,64,3072]{2,1,0:T(8,128)S(1)} %bitcast.94, bf16[4,64,3072]{2,1,0:T(8,128)(2,1)} %collective-permute-done.35), kind=kLoop, calls=%fused_computation.156 | loop fusion | flops 2359296 | bytes 9437184 | tf_op jit(solution)/shard_map/convert.4
  133.2 5.6 %collective-permute-done.12 = bf16[2,64,1536]{2,1,0:T(8,128)(2,1)S(1)} collective-permute-done((bf16[2,64,1536]{2,1,0:T(8,128)(2,1)S(1)}, bf16[2,64,1536]{2,1,0:T(8,128)(2,1)S(1)}, u32[]{:S(2)}, u32[]{:S(2)}) %collective-permute-start.12) | collective-permute-done | bytes 393248 | tf_op jit(solution)/shard_map/ppermute | solution.py:52
  142.6 4.6 %collective-permute-done.36 = bf16[2,64,1536]{2,1,0:T(8,128)(2,1)S(1)} collective-permute-done((bf16[2,64,1536]{2,1,0:T(8,128)(2,1)S(1)}, bf16[2,64,1536]{2,1,0:T(8,128)(2,1)S(1)}, u32[]{:S(2)}, u32[]{:S(2)}) %collective-permute-start.36) | collective-permute-done | bytes 393248 | tf_op jit(solution)/shard_map/ppermute | solution.py:52
  159.3 2.5 %collective-permute-start.15 = (bf16[64,768]{1,0:T(8,128)(2,1)S(1)}, bf16[64,768]{1,0:T(8,128)(2,1)S(1)}, u32[]{:S(2)}, u32[]{:S(2)}) collective-permute-start(bf16[64,768]{1,0:T(8,128)(2,1)S(1)} %add_convert_fusion.8), channel_id=1, source_target_pairs={{0,2},{1,3},{2,0},{3,1},{4,6},{5,7},{6,4},{7,5},{8,10},{9,11},{10,... | collective-permute-start | bytes 294920 | tf_op jit(solution)/shard_map/ppermute | solution.py:52
  166.8 6.2 %collective-permute-done.20 = bf16[64,768]{1,0:T(8,128)(2,1)S(1)} collective-permute-done((bf16[64,768]{1,0:T(8,128)(2,1)S(1)}, bf16[64,768]{1,0:T(8,128)(2,1)S(1)}, u32[]{:S(2)}, u32[]{:S(2)}) %collective-permute-start.20) | collective-permute-done | bytes 98336 | tf_op jit(solution)/shard_map/ppermute | solution.py:52
  173.1 2.1 %collective-permute-done.15 = bf16[64,768]{1,0:T(8,128)(2,1)S(1)} collective-permute-done((bf16[64,768]{1,0:T(8,128)(2,1)S(1)}, bf16[64,768]{1,0:T(8,128)(2,1)S(1)}, u32[]{:S(2)}, u32[]{:S(2)}) %collective-permute-start.15) | collective-permute-done | bytes 98336 | tf_op jit(solution)/shard_map/ppermute | solution.py:52
  180.0 2.1 %collective-permute-done.16 = bf16[64,768]{1,0:T(8,128)(2,1)S(1)} collective-permute-done((bf16[64,768]{1,0:T(8,128)(2,1)S(1)}, bf16[64,768]{1,0:T(8,128)(2,1)S(1)}, u32[]{:S(2)}, u32[]{:S(2)}) %collective-permute-start.16) | collective-permute-done | bytes 98336 | tf_op jit(solution)/shard_map/ppermute | solution.py:52
  (209 shorter events, 78.7 us)
Async XLA Ops:
  0.6 27.0 %collective-permute-start.3 = (bf16[64,3072]{1,0:T(8,128)(2,1)}, bf16[64,3072]{1,0:T(8,128)(2,1)}, u32[]{:S(2)}, u32[]{:S(2)}) collective-permute-start(bf16[64,3072]{1,0:T(8,128)(2,1)} %param.8), channel_id=1, source_target_pairs={{0,4},{4,0},{8,12},{12,8},{1,5},{5,1},{9,13},{13,9},{2,6},{6,2},{1... | collective-permute-start | bytes 1179656 | tf_op jit(solution)/shard_map/ppermute | solution.py:52
  3.6 23.8 %collective-permute-start.4 = (bf16[64,3072]{1,0:T(8,128)(2,1)}, bf16[64,3072]{1,0:T(8,128)(2,1)S(1)}, u32[]{:S(2)}, u32[]{:S(2)}) collective-permute-start(bf16[64,3072]{1,0:T(8,128)(2,1)} %param.8), channel_id=1, source_target_pairs={{0,8},{4,12},{8,0},{12,4},{1,9},{5,13},{9,1},{13,5},{2,10},{6,14},... | collective-permute-start | bytes 1179656 | tf_op jit(solution)/shard_map/ppermute | solution.py:52
  5.2 35.8 %collective-permute-start.7 = (bf16[64,3072]{1,0:T(8,128)(2,1)}, bf16[64,3072]{1,0:T(8,128)(2,1)}, u32[]{:S(2)}, u32[]{:S(2)}) collective-permute-start(bf16[64,3072]{1,0:T(8,128)(2,1)} %param.8), channel_id=1, source_target_pairs={{0,16},{16,0},{1,17},{17,1},{2,18},{18,2},{3,19},{19,3},{4,20},{20... | collective-permute-start | bytes 1179656 | tf_op jit(solution)/shard_map/ppermute | solution.py:52
  10.3 25.7 %collective-permute-start.22 = (bf16[64,3072]{1,0:T(8,128)(2,1)}, bf16[64,3072]{1,0:T(8,128)(2,1)}, u32[]{:S(2)}, u32[]{:S(2)}) collective-permute-start(bf16[64,3072]{1,0:T(8,128)(2,1)} %param.15), channel_id=1, source_target_pairs={{0,4},{4,0},{8,12},{12,8},{1,5},{5,1},{9,13},{13,9},{2,6},{6,2},{1... | collective-permute-start | bytes 1179656 | tf_op jit(solution)/shard_map/ppermute | solution.py:52
  21.6 11.8 %collective-permute-start.23 = (bf16[64,3072]{1,0:T(8,128)(2,1)}, bf16[64,3072]{1,0:T(8,128)(2,1)}, u32[]{:S(2)}, u32[]{:S(2)}) collective-permute-start(bf16[64,3072]{1,0:T(8,128)(2,1)} %param.15), channel_id=1, source_target_pairs={{0,8},{4,12},{8,0},{12,4},{1,9},{5,13},{9,1},{13,5},{2,10},{6,14},... | collective-permute-start | bytes 1179656 | tf_op jit(solution)/shard_map/ppermute | solution.py:52
  27.5 18.8 %collective-permute-start.26 = (bf16[64,3072]{1,0:T(8,128)(2,1)}, bf16[64,3072]{1,0:T(8,128)(2,1)S(1)}, u32[]{:S(2)}, u32[]{:S(2)}) collective-permute-start(bf16[64,3072]{1,0:T(8,128)(2,1)} %param.15), channel_id=1, source_target_pairs={{0,16},{16,0},{1,17},{17,1},{2,18},{18,2},{3,19},{19,3},{4,20},{20... | collective-permute-start | bytes 1179656 | tf_op jit(solution)/shard_map/ppermute | solution.py:52
  27.6 12.9 %collective-permute-start.5 = (bf16[64,1536]{1,0:T(8,128)(2,1)S(1)}, bf16[64,1536]{1,0:T(8,128)(2,1)S(1)}, u32[]{:S(2)}, u32[]{:S(2)}) collective-permute-start(bf16[64,1536]{1,0:T(8,128)(2,1)S(1)} %slice.232), channel_id=1, source_target_pairs={{0,4},{4,0},{8,12},{12,8},{1,5},{5,1},{9,13},{13,9},{2,6},{6,2},{1... | collective-permute-start | bytes 589832 | tf_op jit(solution)/shard_map/ppermute | solution.py:52
  46.9 11.3 %collective-permute-start.29 = (bf16[64,3072]{1,0:T(8,128)(2,1)S(1)}, bf16[64,3072]{1,0:T(8,128)(2,1)S(1)}, u32[]{:S(2)}, u32[]{:S(2)}) collective-permute-start(bf16[64,3072]{1,0:T(8,128)(2,1)S(1)} %pad_maximum_fusion.3), channel_id=1, source_target_pairs={{0,16},{16,0},{1,17},{17,1},{2,18},{18,2},{3,19},{19,3},{4,20},{20... | collective-permute-start | bytes 1179656 | tf_op jit(solution)/shard_map/ppermute | solution.py:52
  74.1 50.5 %collective-permute-start.11 = (bf16[4,64,3072]{2,1,0:T(8,128)(2,1)}, bf16[4,64,3072]{2,1,0:T(8,128)(2,1)}, u32[]{:S(2)}, u32[]{:S(2)}) collective-permute-start(bf16[4,64,3072]{2,1,0:T(8,128)(2,1)} %bitcast.15), channel_id=1, source_target_pairs={{0,16},{16,0},{1,17},{17,1},{2,18},{18,2},{3,19},{19,3},{4,20},{20... | collective-permute-start | bytes 4718600 | tf_op jit(solution)/shard_map/ppermute | solution.py:52
  74.3 10.0 %collective-permute-start.30 = (f32[8,64]{1,0:T(8,128)S(1)}, f32[8,64]{1,0:T(8,128)S(1)}, u32[]{:S(2)}, u32[]{:S(2)}) collective-permute-start(f32[8,64]{1,0:T(8,128)S(1)} %mul.129), channel_id=1, source_target_pairs={{0,4},{4,0},{8,12},{12,8},{1,5},{5,1},{9,13},{13,9},{2,6},{6,2},{1... | collective-permute-start | bytes 6152 | tf_op jit(solution)/shard_map/ppermute | solution.py:52
  84.3 11.6 %collective-permute-start.31 = (f32[8,64]{1,0:T(8,128)S(1)}, f32[8,64]{1,0:T(8,128)S(1)}, u32[]{:S(2)}, u32[]{:S(2)}) collective-permute-start(f32[8,64]{1,0:T(8,128)S(1)} %add.169), channel_id=1, source_target_pairs={{0,8},{4,12},{8,0},{12,4},{1,9},{5,13},{9,1},{13,5},{2,10},{6,14},... | collective-permute-start | bytes 6152 | tf_op jit(solution)/shard_map/ppermute | solution.py:52
  102.9 8.2 %collective-permute-start.33 = (f32[8,64]{1,0:T(8,128)S(1)}, f32[8,64]{1,0:T(8,128)S(1)}, u32[]{:S(2)}, u32[]{:S(2)}) collective-permute-start(f32[8,64]{1,0:T(8,128)S(1)} %add.171), channel_id=1, source_target_pairs={{0,1},{1,0},{2,3},{3,2},{4,5},{5,4},{6,7},{7,6},{8,9},{9,8},{10,11... | collective-permute-start | bytes 6152 | tf_op jit(solution)/shard_map/ppermute | solution.py:52
  111.1 9.4 %collective-permute-start.34 = (f32[8,64]{1,0:T(8,128)S(1)}, f32[8,64]{1,0:T(8,128)S(1)}, u32[]{:S(2)}, u32[]{:S(2)}) collective-permute-start(f32[8,64]{1,0:T(8,128)S(1)} %add.172), channel_id=1, source_target_pairs={{0,2},{1,3},{2,0},{3,1},{4,6},{5,7},{6,4},{7,5},{8,10},{9,11},{10,... | collective-permute-start | bytes 6152 | tf_op jit(solution)/shard_map/ppermute | solution.py:52
  120.5 9.4 %collective-permute-start.35 = (bf16[4,64,3072]{2,1,0:T(8,128)(2,1)}, bf16[4,64,3072]{2,1,0:T(8,128)(2,1)}, u32[]{:S(2)}, u32[]{:S(2)}) collective-permute-start(bf16[4,64,3072]{2,1,0:T(8,128)(2,1)} %bitcast.25), channel_id=1, source_target_pairs={{0,16},{16,0},{1,17},{17,1},{2,18},{18,2},{3,19},{19,3},{4,20},{20... | collective-permute-start | bytes 4718600 | tf_op jit(solution)/shard_map/ppermute | solution.py:52
  126.8 12.0 %collective-permute-start.12 = (bf16[2,64,1536]{2,1,0:T(8,128)(2,1)S(1)}, bf16[2,64,1536]{2,1,0:T(8,128)(2,1)S(1)}, u32[]{:S(2)}, u32[]{:S(2)}) collective-permute-start(bf16[2,64,1536]{2,1,0:T(8,128)(2,1)S(1)} %pad_maximum_fusion.1), channel_id=1, source_target_pairs={{0,4},{4,0},{8,12},{12,8},{1,5},{5,1},{9,13},{13,9},{2,6},{6,2},{1... | collective-permute-start | bytes 1179656 | tf_op jit(solution)/shard_map/ppermute | solution.py:52
  128.4 12.0 %collective-permute-start.17 = (bf16[2,64,1536]{2,1,0:T(8,128)(2,1)S(1)}, bf16[2,64,1536]{2,1,0:T(8,128)(2,1)S(1)}, u32[]{:S(2)}, u32[]{:S(2)}) collective-permute-start(bf16[2,64,1536]{2,1,0:T(8,128)(2,1)S(1)} %stack.22), channel_id=1, source_target_pairs={{0,8},{4,12},{8,0},{12,4},{1,9},{5,13},{9,1},{13,5},{2,10},{6,14},... | collective-permute-start | bytes 1179656 | tf_op jit(solution)/shard_map/ppermute | solution.py:52
  132.1 15.1 %collective-permute-start.36 = (bf16[2,64,1536]{2,1,0:T(8,128)(2,1)S(1)}, bf16[2,64,1536]{2,1,0:T(8,128)(2,1)S(1)}, u32[]{:S(2)}, u32[]{:S(2)}) collective-permute-start(bf16[2,64,1536]{2,1,0:T(8,128)(2,1)S(1)} %pad_maximum_fusion.4), channel_id=1, source_target_pairs={{0,4},{4,0},{8,12},{12,8},{1,5},{5,1},{9,13},{13,9},{2,6},{6,2},{1... | collective-permute-start | bytes 1179656 | tf_op jit(solution)/shard_map/ppermute | solution.py:52
  132.7 16.1 %collective-permute-start.41 = (bf16[2,64,1536]{2,1,0:T(8,128)(2,1)S(1)}, bf16[2,64,1536]{2,1,0:T(8,128)(2,1)S(1)}, u32[]{:S(2)}, u32[]{:S(2)}) collective-permute-start(bf16[2,64,1536]{2,1,0:T(8,128)(2,1)S(1)} %stack.23), channel_id=1, source_target_pairs={{0,8},{4,12},{8,0},{12,4},{1,9},{5,13},{9,1},{13,5},{2,10},{6,14},... | collective-permute-start | bytes 1179656 | tf_op jit(solution)/shard_map/ppermute | solution.py:52
  140.5 12.5 %collective-permute-start.13 = (bf16[1,64,1536]{2,1,0:T(8,128)(2,1)S(1)}, bf16[1,64,1536]{2,1,0:T(8,128)(2,1)S(1)}, u32[]{:S(2)}, u32[]{:S(2)}) collective-permute-start(bf16[1,64,1536]{2,1,0:T(8,128)(2,1)S(1)} %get-tuple-element.31), channel_id=1, source_target_pairs={{0,8},{4,12},{8,0},{12,4},{1,9},{5,13},{9,1},{13,5},{2,10},{6,14},... | collective-permute-start | bytes 589832 | tf_op jit(solution)/shard_map/ppermute | solution.py:52
  142.1 10.9 %collective-permute-start.18 = (bf16[1,64,1536]{2,1,0:T(8,128)(2,1)S(1)}, bf16[1,64,1536]{2,1,0:T(8,128)(2,1)S(1)}, u32[]{:S(2)}, u32[]{:S(2)}) collective-permute-start(bf16[1,64,1536]{2,1,0:T(8,128)(2,1)S(1)} %get-tuple-element.32), channel_id=1, source_target_pairs={{0,4},{4,0},{8,12},{12,8},{1,5},{5,1},{9,13},{13,9},{2,6},{6,2},{1... | collective-permute-start | bytes 589832 | tf_op jit(solution)/shard_map/ppermute | solution.py:52
  158.7 14.3 %collective-permute-start.20 = (bf16[64,768]{1,0:T(8,128)(2,1)S(1)}, bf16[64,768]{1,0:T(8,128)(2,1)S(1)}, u32[]{:S(2)}, u32[]{:S(2)}) collective-permute-start(bf16[64,768]{1,0:T(8,128)(2,1)S(1)} %add_convert_fusion.6), channel_id=1, source_target_pairs={{0,2},{1,3},{2,0},{3,1},{4,6},{5,7},{6,4},{7,5},{8,10},{9,11},{10,... | collective-permute-start | bytes 294920 | tf_op jit(solution)/shard_map/ppermute | solution.py:52
  159.3 15.9 %collective-permute-start.15 = (bf16[64,768]{1,0:T(8,128)(2,1)S(1)}, bf16[64,768]{1,0:T(8,128)(2,1)S(1)}, u32[]{:S(2)}, u32[]{:S(2)}) collective-permute-start(bf16[64,768]{1,0:T(8,128)(2,1)S(1)} %add_convert_fusion.8), channel_id=1, source_target_pairs={{0,2},{1,3},{2,0},{3,1},{4,6},{5,7},{6,4},{7,5},{8,10},{9,11},{10,... | collective-permute-start | bytes 294920 | tf_op jit(solution)/shard_map/ppermute | solution.py:52
  163.7 13.1 %collective-permute-start.44 = (bf16[64,768]{1,0:T(8,128)(2,1)S(1)}, bf16[64,768]{1,0:T(8,128)(2,1)S(1)}, u32[]{:S(2)}, u32[]{:S(2)}) collective-permute-start(bf16[64,768]{1,0:T(8,128)(2,1)S(1)} %add_convert_fusion.2), channel_id=1, source_target_pairs={{0,2},{1,3},{2,0},{3,1},{4,6},{5,7},{6,4},{7,5},{8,10},{9,11},{10,... | collective-permute-start | bytes 294920 | tf_op jit(solution)/shard_map/ppermute | solution.py:52
  165.1 12.8 %collective-permute-start.39 = (bf16[64,768]{1,0:T(8,128)(2,1)S(1)}, bf16[64,768]{1,0:T(8,128)(2,1)S(1)}, u32[]{:S(2)}, u32[]{:S(2)}) collective-permute-start(bf16[64,768]{1,0:T(8,128)(2,1)S(1)} %add_convert_fusion.4), channel_id=1, source_target_pairs={{0,2},{1,3},{2,0},{3,1},{4,6},{5,7},{6,4},{7,5},{8,10},{9,11},{10,... | collective-permute-start | bytes 294920 | tf_op jit(solution)/shard_map/ppermute | solution.py:52
  (40 other events, 325.9 us)

commit v2 on v1

v2 whole, which is shorter than its diff:
```python
import functools

import jax
import jax.numpy as jnp
from jax import lax
from jax.experimental import pallas as pl
from jax.experimental.pallas import tpu as pltpu
from jax.sharding import PartitionSpec as P


def split3(values):
    high = values.astype(jnp.bfloat16)
    rest = values - high.astype(jnp.float32)
    middle = rest.astype(jnp.bfloat16)
    low = (rest - middle.astype(jnp.float32)).astype(jnp.bfloat16)
    return high, middle, low


def routing(tokens, w_router, expert_ids, partner):
    tok_rows = tokens.shape[0]
    experts = w_router.shape[1]
    slot_count = min(tok_rows, 4 * tok_rows // experts)
    keep_count = 3 * slot_count // 4
    pieces = jnp.concatenate(split3(w_router), axis=1)
    logits = jnp.dot(tokens, pieces, preferred_element_type=jnp.float32)
    logits = logits.reshape(tok_rows, 3, experts)
    logits = (logits[:, 2] + logits[:, 1]) + logits[:, 0]
    columns = lax.broadcasted_iota(jnp.int32, (tok_rows, experts), 1)
    first = expert_ids[:, :1] == columns
    second = expert_ids[:, 1:] == columns
    first_float = first.astype(jnp.float32)
    second_float = second.astype(jnp.float32)
    difference = jnp.sum(logits * (first_float - second_float), axis=1, keepdims=True)
    share_one = jax.nn.sigmoid(difference)
    share_two = 1.0 - share_one
    rows = lax.broadcasted_iota(jnp.int32, (tok_rows, tok_rows), 0)
    before = (lax.broadcasted_iota(jnp.int32, (tok_rows, tok_rows), 1) < rows).astype(jnp.bfloat16)
    named = (first_float + second_float).astype(jnp.bfloat16)
    earlier = jnp.dot(before, named, preferred_element_type=jnp.float32)
    arrival_one = jnp.sum(earlier * first_float, axis=1, keepdims=True)
    arrival_two = jnp.sum(earlier * second_float, axis=1, keepdims=True)
    mate = partner[None, :]
    mate_one = jnp.sum(jnp.where(first, mate, 0), axis=1, keepdims=True)
    mate_two = jnp.sum(jnp.where(second, mate, 0), axis=1, keepdims=True)
    target_one = jnp.where(arrival_one < keep_count, expert_ids[:, :1], mate_one)
    target_two = jnp.where(arrival_two < keep_count, expert_ids[:, 1:], mate_two)
    lands_one = (target_one == columns).astype(jnp.float32)
    lands_two = (target_two == columns).astype(jnp.float32)
    weight = share_one * lands_one + share_two * lands_two
    slope = share_one * share_two * (lands_one - lands_two)
    return weight, slope, first_float - second_float


def swap(values, axis, flip):
    size = lax.axis_size(axis)
    return lax.ppermute(values, axis, [(place, place ^ flip) for place in range(size)])


NT = (((1,), (1,)), ((), ()))
TN = (((0,), (0,)), ((), ()))
WHOLE = pl.BlockSpec(memory_space=pltpu.VMEM)
LEFT = pl.BlockSpec(memory_space=pl.ANY)


def settings():
    return pltpu.CompilerParams(vmem_limit_bytes=40 << 20)


def after(values, pins):
    if not pins:
        return values
    return lax.optimization_barrier((values, *pins))[0]


def on_hbm(*arrays):
    return tuple(pltpu.with_memory_space_constraint(array, pltpu.HBM) for array in arrays)


def in_hbm(shape, dtype=jnp.bfloat16):
    return pltpu.HBM(shape, dtype)


def in_vmem(shape, dtype=jnp.bfloat16):
    return pltpu.VMEM(shape, dtype)


def cost(flops, moved):
    return pl.CostEstimate(flops=flops, bytes_accessed=moved, transcendentals=0)


def once(shape):
    return pl.BlockSpec(shape, lambda i: (0,) * len(shape), pipeline_mode=pl.Buffered(1))


def shaped(shape, dtype=jnp.bfloat16):
    return jax.ShapeDtypeStruct(shape, dtype)


def routing_kernel(experts, keep_count, tokens, w_router, ids, partner, out):
    tok_rows = tokens.shape[0]
    high, middle, low = split3(w_router[...])

    def product(piece):
        return lax.dot_general(piece, tokens[...], NT, preferred_element_type=jnp.float32)

    logits = (product(low) + product(middle)) + product(high)
    names = lax.broadcasted_iota(jnp.int32, (experts, tok_rows), 0)
    first = (ids[0:1, :] == names).astype(jnp.float32)
    second = (ids[1:2, :] == names).astype(jnp.float32)
    difference = jnp.sum(logits * (first - second), axis=0, keepdims=True)
    share_one = jax.nn.sigmoid(difference)
    share_two = 1.0 - share_one
    source = lax.broadcasted_iota(jnp.int32, (tok_rows, tok_rows), 0)
    before = source < lax.broadcasted_iota(jnp.int32, (tok_rows, tok_rows), 1)
    earlier = jnp.dot(first + second, before.astype(jnp.float32), preferred_element_type=jnp.float32)
    arrival_one = jnp.sum(earlier * first, axis=0, keepdims=True)
    arrival_two = jnp.sum(earlier * second, axis=0, keepdims=True)
    mates = jnp.zeros(names.shape, jnp.int32)
    for expert in range(experts):
        mates = jnp.where(names == expert, partner[expert], mates)
    mates = mates.astype(jnp.float32)
    place = names.astype(jnp.float32)

    def lands(chosen, arrival):
        own = jnp.sum(chosen * place, axis=0, keepdims=True)
        mate = jnp.sum(chosen * mates, axis=0, keepdims=True)
        target = jnp.where(arrival < keep_count, own, mate)
        return (target == place).astype(jnp.float32)

    lands_one = lands(first, arrival_one)
    lands_two = lands(second, arrival_two)
    out[0:experts, :] = share_one * lands_one + share_two * lands_two
    out[experts : 2 * experts, :] = share_one * share_two * (lands_one - lands_two)
    out[2 * experts :, :] = first - second


def route(tokens, w_router, expert_ids, partner):
    tok_rows = tokens.shape[0]
    experts = w_router.shape[1]
    slot_count = min(tok_rows, 4 * tok_rows // experts)
    return pl.pallas_call(
        functools.partial(routing_kernel, experts, 3 * slot_count // 4),
        out_shape=shaped((3 * experts, tok_rows), jnp.float32),
        in_specs=[WHOLE] * 3 + [pl.BlockSpec(memory_space=pltpu.SMEM)],
        out_specs=WHOLE,
        name="route",
        cost_estimate=cost(1 << 20, 1 << 20),
    )(tokens, w_router.T, expert_ids.T, partner)


def tile_of(number, size):
    return pl.ds(pl.multiple_of(number * size, size), size)


class Mover:
    def __init__(self, sems):
        self.sems = sems
        self.used = 0

    def start(self, source, target):
        copy = pltpu.make_async_copy(source, target, self.sems.at[self.used])
        self.used += 1
        copy.start()
        return copy


def fetch_rows(mover, blocks, rows):
    count = blocks[0].shape[0]
    return [
        mover.start(block, rows.at[pl.ds(number * count, count), :])
        for number, block in enumerate(blocks)
    ]


def forward(blocks, w_gate, w_up, tile):
    number = len(blocks)
    tok_rows, features = blocks[0].shape
    count = number * tok_rows
    width = w_gate.shape[1]

    def body(*refs):
        pieces, refs = refs[:number], refs[number:]
        wg, wu, hid, sw, sg, everything, x, bg, bu, gates, h, a, b, sems_in, sems_out = refs
        mover, outward = Mover(sems_in), Mover(sems_out)
        copies = [mover.start(wg, bg)]
        for copy in fetch_rows(mover, pieces, x):
            copy.wait()
        copies.append(mover.start(wu, bu))
        copies[0].wait()
        tiles = [pl.ds(step * tile, tile) for step in range(width // tile)]
        for place in tiles:
            gates[:, place] = jnp.dot(x[...], bg[:, place], preferred_element_type=jnp.float32)
        done = [outward.start(x, everything)]
        copies[1].wait()
        for place in tiles:
            up = jnp.dot(x[...], bu[:, place], preferred_element_type=jnp.float32)
            gate = gates[:, place]
            sigmoid_gate = jax.nn.sigmoid(gate)
            swished = gate * sigmoid_gate
            h[:, place] = (swished * up).astype(jnp.bfloat16)
            a[:, place] = swished.astype(jnp.bfloat16)
            b[:, place] = (up * sigmoid_gate * (1.0 + gate * (1.0 - sigmoid_gate))).astype(
                jnp.bfloat16
            )
        done += [outward.start(h, hid), outward.start(a, sw), outward.start(b, sg)]
        for copy in done:
            copy.wait()

    flat = pltpu.VMEM((count, width), jnp.bfloat16)
    weights = pltpu.VMEM((features, width), jnp.bfloat16)
    return pl.pallas_call(
        body,
        out_shape=(in_hbm((count, width)),) * 3 + (in_hbm((count, features)),),
        in_specs=[LEFT] * (number + 2),
        out_specs=(LEFT,) * 4,
        scratch_shapes=[
            pltpu.VMEM((count, features), jnp.bfloat16),
            weights,
            weights,
            pltpu.VMEM((count, width), jnp.float32),
            flat,
            flat,
            flat,
            pltpu.SemaphoreType.DMA((number + 2,)),
            pltpu.SemaphoreType.DMA((4,)),
        ],
        compiler_params=pltpu.CompilerParams(vmem_limit_bytes=40 << 20),
        name="forward",
        cost_estimate=cost(4 * count * features * width, 6 * features * width),
    )(*on_hbm(*blocks, w_gate, w_up))


def down(core, hidden, w_down, tile, pins):
    count, width = hidden.shape
    half = w_down.shape[1] // 2
    steps = half // tile
    hidden = after(hidden, pins)

    def body(core_ref, hid, wd, keep, send, h, bd, k, s, sems_in, sems_out):
        mover, outward = Mover(sems_in), Mover(sems_out)
        copies = [mover.start(hid, h), mover.start(wd, bd)]
        for copy in copies:
            copy.wait()
        me = core_ref[0]
        done = []
        for side, target, out in ((1 - me, s, send), (me, k, keep)):
            for step in range(steps):
                source = pl.ds(pl.multiple_of(side * half + step * tile, tile), tile)
                columns = pl.ds(step * tile, tile)
                target[:, columns] = jnp.dot(
                    h[...], bd[:, source], preferred_element_type=jnp.float32
                ).astype(jnp.bfloat16)
                done.append(outward.start(target.at[:, columns], out.at[:, columns]))
        for copy in done:
            copy.wait()

    part = pltpu.VMEM((count, half), jnp.bfloat16)
    return pl.pallas_call(
        body,
        out_shape=(in_hbm((count, half)),) * 2,
        in_specs=[pl.BlockSpec(memory_space=pltpu.SMEM)] + [LEFT] * 2,
        out_specs=(LEFT,) * 2,
        scratch_shapes=[
            pltpu.VMEM((count, width), jnp.bfloat16),
            pltpu.VMEM((width, 2 * half), jnp.bfloat16),
            part,
            part,
            pltpu.SemaphoreType.DMA((2,)),
            pltpu.SemaphoreType.DMA((2 * steps,)),
        ],
        compiler_params=pltpu.CompilerParams(vmem_limit_bytes=24 << 20),
        name="down",
        cost_estimate=cost(4 * count * half * width, 4 * half * width),
    )(core, *on_hbm(hidden, w_down))


def backward(blocks, w_down, hidden, sw, sg, weight, slope, tile):
    number = len(blocks)
    tok_rows, features = blocks[0].shape
    count = number * tok_rows
    width = w_down.shape[0]

    def body(*refs):
        pieces, refs = refs[:number], refs[number:]
        wd, hid, swished, slopes, c, v, up_out, gate_out, hidden_out, ds, everything = refs[:11]
        x, bd, h, a, b, ug, gg, hc, sems_in, sems_out = refs[11:]
        mover, outward = Mover(sems_in), Mover(sems_out)
        moves = fetch_rows(mover, pieces, x)
        tiles = [pl.ds(step * tile, tile) for step in range(width // tile)]
        copies = [mover.start(wd.at[tiles[0], :], bd.at[tiles[0], :])]
        for copy in moves:
            copy.wait()
        rest = [mover.start(hid, h), mover.start(swished, a), mover.start(slopes, b)]
        ds[...] = jnp.zeros_like(ds)
        scale = c[...]
        for step, place in enumerate(tiles):
            if step + 1 < len(tiles):
                following = tiles[step + 1]
                copies.append(mover.start(wd.at[following, :], bd.at[following, :]))
            copies[step].wait()
            if step == 0:
                done = [outward.start(x, everything)]
            back = lax.dot_general(x[...], bd[place, :], NT, preferred_element_type=jnp.float32)
            if step == 0:
                for copy in rest:
                    copy.wait()
            value = h[:, place].astype(jnp.float32)
            ds[...] += jnp.sum(value * back, axis=1, keepdims=True) * v[...]
            hc[:, place] = (value * scale).astype(jnp.bfloat16)
            back = back * scale
            ug[:, place] = (back * a[:, place].astype(jnp.float32)).astype(jnp.bfloat16)
            gg[:, place] = (back * b[:, place].astype(jnp.float32)).astype(jnp.bfloat16)
        done += [
            outward.start(ug, up_out),
            outward.start(gg, gate_out),
            outward.start(hc, hidden_out),
        ]
        for copy in done:
            copy.wait()

    flat = pltpu.VMEM((count, width), jnp.bfloat16)
    return pl.pallas_call(
        body,
        out_shape=(in_hbm((count, width)),) * 3
        + (shaped((count, 1), jnp.float32), in_hbm((count, features))),
        in_specs=[LEFT] * (number + 4) + [WHOLE] * 2,
        out_specs=(LEFT,) * 3 + (WHOLE, LEFT),
        scratch_shapes=[
            pltpu.VMEM((count, features), jnp.bfloat16),
            pltpu.VMEM((width, features), jnp.bfloat16),
        ]
        + [flat] * 6
        + [
            pltpu.SemaphoreType.DMA((number + width // tile + 3,)),
            pltpu.SemaphoreType.DMA((4,)),
        ],
        compiler_params=pltpu.CompilerParams(vmem_limit_bytes=40 << 20),
        name="backward",
        cost_estimate=cost(2 * count * features * width, 2 * features * width),
    )(*on_hbm(*blocks, w_down, hidden, sw, sg), weight, slope)


def rows_back(core, gate_grad, up_grad, w_gate, w_up, first, last, tile, pins):
    count, width = gate_grad.shape
    half = w_gate.shape[0] // 2
    gate_grad = after(gate_grad, pins)
    steps = (last - first) // tile

    def body(core_ref, gate_in, up_in, wg, wu, keep, send, gg, ug, bg, bu, k, s, sems_in, sems_out):
        mover, outward = Mover(sems_in), Mover(sems_out)
        me = core_ref[0]
        pieces = []
        for side, target, out in ((1 - me, s, send), (me, k, keep)):
            for step in range(steps):
                source = pl.ds(pl.multiple_of(side * half + first + step * tile, tile), tile)
                pieces.append((source, target, pl.ds(step * tile, tile), out))
        copies = []

        def load(number):
            if number < len(pieces):
                source, place = pieces[number][0], pl.ds(number * tile, tile)
                copies.append(mover.start(wg.at[source, :], bg.at[place, :]))
                copies.append(mover.start(wu.at[source, :], bu.at[place, :]))

        rows = [mover.start(gate_in, gg), mover.start(up_in, ug)]
        load(0)
        for copy in rows:
            copy.wait()
        done = []
        for number, (_, target, columns, out) in enumerate(pieces):
            load(number + 1)
            place = pl.ds(number * tile, tile)
            copies[2 * number].wait()
            total = lax.dot_general(gg[...], bg[place, :], NT, preferred_element_type=jnp.float32)
            copies[2 * number + 1].wait()
            total = total + lax.dot_general(
                ug[...], bu[place, :], NT, preferred_element_type=jnp.float32
            )
            target[:, columns] = total.astype(jnp.bfloat16)
            done.append(outward.start(target.at[:, columns], out.at[:, columns]))
        for copy in done:
            copy.wait()

    flat = pltpu.VMEM((count, width), jnp.bfloat16)
    weights = pltpu.VMEM((2 * (last - first), width), jnp.bfloat16)
    part = pltpu.VMEM((count, last - first), jnp.bfloat16)
    return pl.pallas_call(
        body,
        out_shape=(in_hbm((count, last - first)),) * 2,
        in_specs=[pl.BlockSpec(memory_space=pltpu.SMEM)] + [LEFT] * 4,
        out_specs=(LEFT,) * 2,
        scratch_shapes=[flat, flat, weights, weights, part, part]
        + [pltpu.SemaphoreType.DMA((4 * steps + 2,)), pltpu.SemaphoreType.DMA((2 * steps,))],
        compiler_params=pltpu.CompilerParams(vmem_limit_bytes=40 << 20),
        name="rows_back",
        cost_estimate=cost(8 * count * (last - first) * width, 8 * (last - first) * width),
    )(core, *on_hbm(gate_grad, up_grad, w_gate, w_up))


def outer(left, right, pins):
    left = after(left, pins)
    return lax.dot_general(left, right, TN, preferred_element_type=jnp.float32).astype(jnp.bfloat16)


def small_call(body, outs, args, pins, name):
    first = after(args[0], pins)
    return pl.pallas_call(
        body,
        out_shape=tuple(outs),
        in_specs=[WHOLE] * len(args),
        out_specs=(WHOLE,) * len(outs),
        compiler_params=settings(),
        name=name,
        cost_estimate=cost(1 << 20, 1 << 20),
    )(first, *args[1:])


def add(one, two):
    return (one.astype(jnp.float32) + two.astype(jnp.float32)).astype(jnp.bfloat16)


def trade(values, kind):
    cores, experts = lax.axis_size("dp"), lax.axis_size("expert")
    pairs = []
    for core in range(cores):
        for place in range(experts):
            flip = {"peer": 0, "first": 1 + core, "second": 2 - core, "both": 3}[kind]
            other = core ^ 1 if kind == "peer" else core
            pairs.append((core * experts + place, other * experts + (place ^ flip)))
    return lax.ppermute(values, ("dp", "expert"), pairs)


TAIL = 16


def pack(values):
    high, middle, low = split3(values)
    shape = (TAIL, values.shape[1])
    row = lax.broadcasted_iota(jnp.int32, shape, 0)
    out = jnp.zeros(shape, jnp.float32)
    for number, piece in enumerate((high, middle, low)):
        out = jnp.where(row == number, piece.astype(jnp.float32), out)
    return out.astype(jnp.bfloat16)


def unpack(block):
    return jnp.sum(block.astype(jnp.float32), axis=0, keepdims=True)


class Reduction:
    def __init__(self, keep, send, tok_rows, odd, rider=None):
        self.rows = tok_rows
        self.width = keep.shape[1]
        self.keep = (keep,)
        self.odd = odd
        self.rider = rider
        self.arrived = (trade(send, "peer"),)

    def spread_part(self, number, pins):
        rows = self.rows

        def body(inputs, sent, kept):
            keep, arrived = inputs
            for side in range(2):
                for place, there in enumerate((0, 2, 1, 3)):
                    away = place in ((1, 3), (2, 3))[number]
                    slot = 2 * side + (place // 2, place % 2)[number]
                    (sent if away else kept)[0][pl.ds(slot * rows, rows), :] = add(
                        keep[pl.ds((4 * side + place) * rows, rows), :],
                        arrived[pl.ds((4 * (1 - side) + there) * rows, rows), :],
                    )

        shape = (4 * rows, self.width)
        sent = self.run(body, [shape], [shape], [], pins, "spread_part", False)
        self.arrived = (trade(sent[0], ("first", "second")[number]),)
        return list(self.keep)

    def cross_part(self, number, pins):
        rows = self.rows

        def body(inputs, sent, kept):
            keep, arrived = inputs
            for place in range(4):
                out = (sent if place % 2 else kept)[0]
                source = pl.ds(place * rows, rows)
                out[pl.ds(place // 2 * rows, rows), :] = add(keep[source, :], arrived[source, :])

        shape = (2 * rows, self.width)
        sent = self.run(body, [shape], [shape], [], pins, "cross_part", True)
        self.arrived = (trade(sent[0], ("second", "first")[number]),)
        return list(self.keep)

    def halve_part(self, pins):
        rows, half = 2 * self.rows, self.width // 2

        def body(inputs, sent, kept):
            one = add(inputs[0][:, :half], inputs[1][:, :half])
            two = add(inputs[0][:, half:], inputs[1][:, half:])
            flag = inputs[2][...] > 0
            sent[0][...] = jnp.where(flag, one, two)
            kept[0][...] = jnp.where(flag, two, one)

        shape = (rows, half)
        sent = self.run(body, [shape], [shape], [self.odd], pins, "halve_part", True)
        self.arrived = (swap(sent[0], "mp", 1),)
        return list(self.keep)

    def run(self, body, sent, kept, extra, pins, name, rides):
        riding = self.rider is not None
        outs = [
            shaped((rows + (TAIL if riding and number == 0 else 0), width))
            for number, (rows, width) in enumerate(sent)
        ]
        outs += [shaped(shape) for shape in kept]
        args = [*self.keep, *self.arrived, *extra]
        tail_at = len(self.keep)
        if riding:
            args.append(self.rider)
            outs.append(shaped(self.rider.shape, jnp.float32))

        def whole(*refs):
            inputs, outputs = refs[: len(args)], refs[len(args) :]
            body(inputs, outputs[: len(sent)], outputs[len(sent) : len(sent) + len(kept)])
            if riding:
                total = inputs[-1][...]
                length = total.shape[1]
                if rides:
                    arrived = inputs[tail_at]
                    total = total + unpack(arrived[arrived.shape[0] - TAIL :, :length])
                outputs[-1][...] = total
                outputs[0][sent[0][0] :, :length] = pack(total)

        outs = small_call(whole, outs, args, pins, name)
        if riding:
            self.rider = outs[-1]
        self.keep = outs[len(sent) : len(sent) + len(kept)] if kept else (outs[0],)
        return outs[: len(sent)]

    def spread(self, pins, scale=None):
        rows, half = self.rows, self.width // 2

        def body(inputs, sent, kept):
            keep, arrived = inputs[0], inputs[1]
            for side in range(2):
                for place, there in enumerate((0, 2, 1, 3)):
                    source = pl.ds((4 * side + place) * rows, rows)
                    total = keep[source, :].astype(jnp.float32) + arrived[
                        pl.ds((4 * (1 - side) + there) * rows, rows), :
                    ].astype(jnp.float32)
                    if scale is not None:
                        total = total * inputs[2][source, :]
                    total = total.astype(jnp.bfloat16)
                    left = pl.ds((2 * side + place // 2) * rows, rows)
                    right = pl.ds((2 * side + place % 2) * rows, rows)
                    (sent if place in (1, 3) else kept)[0][left, :] = total[:, :half]
                    (sent if place in (2, 3) else kept)[1][right, :] = total[:, half:]

        extra = [] if scale is None else [scale]
        shape = (4 * rows, half)
        sent = self.run(body, [shape] * 2, [shape] * 2, extra, pins, "spread", False)
        self.arrived = (trade(sent[0], "first"), trade(sent[1], "second"))
        return list(self.keep[:1])

    def cross(self, pins):
        rows, half = self.rows, self.width // 2

        def body(inputs, sent, kept):
            for part in range(2):
                keep, arrived = inputs[part], inputs[2 + part]
                for place in range(4):
                    out = (sent if place % 2 else kept)[part]
                    source = pl.ds(place * rows, rows)
                    out[pl.ds(place // 2 * rows, rows), :] = add(
                        keep[source, :], arrived[source, :]
                    )

        shape = (2 * rows, half)
        sent = self.run(body, [shape] * 2, [shape] * 2, [], pins, "cross", True)
        self.arrived = (trade(sent[0], "second"), trade(sent[1], "first"))
        return list(self.keep[:1])

    def halve(self, pins):
        rows, half = 2 * self.rows, self.width // 2

        def body(inputs, sent, kept):
            one = add(inputs[0][...], inputs[2][:rows, :])
            two = add(inputs[1][...], inputs[3][...])
            flag = inputs[4][...] > 0
            sent[0][:rows, :] = jnp.where(flag, one, two)
            kept[0][...] = jnp.where(flag, two, one)

        shape = (rows, half)
        sent = self.run(body, [shape], [shape], [self.odd], pins, "halve", True)
        self.arrived = (swap(sent[0], "mp", 1),)
        return list(self.keep)

    def step(self, flip, pins):
        rows, half = 2 * self.rows, self.width // 2

        def body(inputs, sent, kept):
            sent[0][:rows, :] = add(inputs[0][:rows, :], inputs[1][:rows, :])

        sent = self.run(body, [(rows, half)], [], [], pins, "step", True)
        self.arrived = (swap(sent[0], "mp", flip),)
        return list(self.keep)

    def join(self, pins):
        rows, half = self.rows, self.width // 2

        def body(inputs, sent, kept):
            keep, arrived = inputs[0], inputs[1]
            flag = inputs[2][...] > 0
            for out, place in ((kept[0], pl.ds(0, rows)), (sent[0], pl.ds(rows, rows))):
                out[:rows, :half] = jnp.where(flag, arrived[place, :], keep[place, :])
                out[:rows, half:] = jnp.where(flag, keep[place, :], arrived[place, :])

        shape = (rows, self.width)
        sent = self.run(body, [shape], [shape], [self.odd], pins, "join", False)
        self.arrived = (trade(sent[0], "peer"),)
        return list(self.keep)


def finish(parts, core, extra, pins, name):
    rows, width = parts[0].keep[0].shape
    features = 2 * width * len(parts)
    rider = parts[0].rider
    riding = rider is not None
    args = [item for part in parts for item in (part.keep[0], part.arrived[0])]
    at = len(args)
    args += [core, *extra] + ([rider] if riding else [])
    outs = [shaped((rows, features))]
    if riding:
        outs.append(shaped(rider.shape, jnp.float32))

    def body(*refs):
        out = refs[len(args)]
        flag = refs[at][...] > 0
        for number in range(len(parts)):
            keep, arrived = refs[2 * number][...], refs[2 * number + 1][:rows, :]
            sides = (jnp.where(flag, arrived, keep), jnp.where(flag, keep, arrived))
            for side, values in enumerate(sides):
                columns = pl.ds(side * features // 2 + number * width, width)
                if extra:
                    values = values.astype(jnp.float32)
                    logits, router = refs[at + 1], refs[at + 2]
                    for expert in range(router.shape[0]):
                        values = values + logits[:, expert : expert + 1] * (
                            router[expert : expert + 1, columns]
                        )
                out[:, columns] = values.astype(jnp.bfloat16)
        if riding:
            own = refs[len(args) - 1][...]
            refs[-1][...] = own + unpack(refs[1][rows:, : own.shape[1]])

    return small_call(body, outs, args, pins, name)


def gather_rows(block, peer, near, second, far):
    near_peer, second_peer = trade(second, "peer"), trade(near, "peer")
    return [block, near, second, far, peer, near_peer, second_peer, trade(far, "peer")]


def swapped(blocks):
    return jnp.stack([blocks[0], blocks[2], blocks[1], blocks[3]])


def gather_small(small):
    found = jnp.stack([small, trade(small, "first")])
    return jnp.concatenate([found, trade(found, "second")], axis=0)


def order():
    core, expert = lax.axis_index("dp"), lax.axis_index("expert")
    flips = (0, 1 + core, 2 - core, 3)
    places = [(core ^ side) * 4 + (expert ^ flip) for side in range(2) for flip in flips]
    places = jnp.stack([jnp.asarray(place, jnp.int32) for place in places])
    return (lax.iota(jnp.int32, 8)[:, None] == places[None, :]).astype(jnp.float32)


def local_pairs(tokens, w_router, expert_ids, partner, gate_weight, up_weight, down_weight, grad_out):
    tok_rows, features = tokens.shape
    experts = w_router.shape[1]
    width = gate_weight.shape[2]
    w_gate, w_up, w_down = gate_weight[0], up_weight[0], down_weight[0]
    odd = (lax.axis_index("mp") & 1).astype(jnp.int32).reshape(1, 1)
    core = lax.axis_index("dp").astype(jnp.int32).reshape(1)

    tok_near = trade(tokens, "first")
    tok_second = trade(tokens, "second")
    tok_peer = trade(tokens, "peer")
    small = route(tokens, w_router, expert_ids, partner)
    tok_far = trade(after(tok_near, [small]), "second")
    small = gather_small(small)
    small_peer = trade(small, "peer")
    token_blocks = gather_rows(tokens, tok_peer, tok_near, tok_second, after(tok_far, [small]))
    later = after(grad_out, [tok_far])
    out_near = trade(later, "first")
    out_second = trade(later, "second")
    out_far = trade(later, "both")
    out_peer = trade(grad_out, "peer")
    hidden, sw, sg, all_tokens = forward(token_blocks, w_gate, w_up, width // 4)
    small = jnp.concatenate([small, swapped(after(small_peer, [hidden]))], axis=0)
    mine = (lax.iota(jnp.int32, experts) == lax.axis_index("expert")).astype(jnp.float32)
    mine = mine[None, :, None]
    weight = jnp.sum(small[:, :experts] * mine, axis=1).reshape(-1, 1)
    slope = jnp.sum(small[:, experts : 2 * experts] * mine, axis=1).reshape(-1, 1)
    keep, send = down(core, hidden, w_down, features // 4, [])
    out_near, out_second, out_far = (
        after(item, [keep]) for item in (out_near, out_second, out_far)
    )
    grad_blocks = gather_rows(grad_out, out_peer, out_near, out_second, out_far)
    send = after(send, [out_near, out_second, out_far])
    mixed = Reduction(keep, send, tok_rows, odd)
    up_grad, gate_grad, hidden, dshare, all_grads = backward(
        grad_blocks, w_down, hidden, sw, sg, weight, slope, width // 2
    )
    places = order()
    dlogit = jnp.sum(places[:, :, None] * dshare.reshape(1, -1, tok_rows), axis=1)
    mixed.rider = dlogit.reshape(1, -1)
    pins = mixed.spread([gate_grad], weight)
    half = features // 2
    middle = half // 2
    tile = middle
    keep, send = rows_back(core, gate_grad, up_grad, w_gate, w_up, 0, middle, tile, pins)
    pins = mixed.cross([keep])
    left = Reduction(keep, after(send, pins), tok_rows, odd)
    keep, send = rows_back(core, gate_grad, up_grad, w_gate, w_up, middle, half, tile, pins)
    pins = mixed.halve([keep])
    left.spread_part(0, pins)
    right = Reduction(keep, after(send, left.keep), tok_rows, odd)
    pins = right.spread_part(1, [])
    grad_down = outer(hidden, all_grads, pins)
    pins = left.cross_part(0, [grad_down])
    pins = pins + mixed.step(2, [grad_down])
    pins = pins + right.cross_part(1, [grad_down])
    grad_gate = outer(all_tokens, gate_grad, pins)
    pins = left.halve_part([grad_gate])
    pins = pins + mixed.step(1, [grad_gate])
    pins = pins + right.halve_part([grad_gate])
    grad_up = outer(all_tokens, up_grad, pins)
    pins = left.step(2, [grad_up])
    pins = pins + mixed.join([grad_up])
    pins = pins + right.step(2, [grad_up])
    side = core.reshape(1, 1)
    mixed_out, dlogit = finish([mixed], side, (), pins, "finish_mixed")
    dlogit = dlogit.reshape(-1, tok_rows)

    dlogit = jnp.sum(places[:, :, None] * dlogit[:, None, :], axis=0)
    sign = jnp.swapaxes(small[:, 2 * experts :], 1, 2)
    grad_logits = (sign * dlogit[:, :, None]).reshape(-1, experts)
    pieces = jnp.concatenate(split3(grad_logits), axis=1)
    grad_router = jnp.einsum("rd,re->de", all_tokens, pieces, preferred_element_type=jnp.float32)
    grad_router = (
        grad_router[:, 2 * experts :] + grad_router[:, experts : 2 * experts]
    ) + grad_router[:, :experts]
    left.step(1, [grad_router])
    right.step(1, left.keep)
    left.join(right.keep)
    right.join([])
    extra = (grad_logits[:tok_rows], w_router.T)
    (grad_tokens,) = finish([left, right], side, extra, [], "finish_tokens")
    return mixed_out, grad_tokens, grad_router, grad_gate[None], grad_up[None], grad_down[None]


def in_pairs():
    return (
        lax.axis_size("dp") == 2 and lax.axis_size("expert") == 4 and lax.axis_size("mp") == 4
    )


def local(tokens, w_router, expert_ids, partner, gate_weight, up_weight, down_weight, grad_out):
    if in_pairs():
        return local_pairs(
            tokens, w_router, expert_ids, partner, gate_weight, up_weight, down_weight, grad_out
        )
    experts = w_router.shape[1]
    blocks = ("dp", "expert")
    all_tokens = lax.all_gather(tokens, blocks, axis=0, tiled=True)
    all_grads = lax.all_gather(grad_out, blocks, axis=0, tiled=True)
    weight, slope, sign = routing(tokens, w_router, expert_ids, partner)
    small = lax.all_gather(
        jnp.concatenate([weight, slope, sign], axis=1), blocks, axis=0, tiled=True
    )
    mine = (lax.iota(jnp.int32, experts) == lax.axis_index("expert")).astype(jnp.float32)
    weight_all = jnp.sum(small[:, :experts] * mine, axis=1, keepdims=True)
    slope_all = jnp.sum(small[:, experts : 2 * experts] * mine, axis=1)
    sign_all = small[:, 2 * experts :]

    w_gate = gate_weight[0]
    w_up = up_weight[0]
    w_down = down_weight[0]
    pre_gate = jnp.dot(all_tokens, w_gate, preferred_element_type=jnp.float32)
    pre_up = jnp.dot(all_tokens, w_up, preferred_element_type=jnp.float32)
    back = jnp.einsum("rd,fd->rf", all_grads, w_down, preferred_element_type=jnp.float32)
    sigmoid_gate = jax.nn.sigmoid(pre_gate)
    swished = pre_gate * sigmoid_gate
    hidden = swished * pre_up
    dshare = jnp.sum(hidden * back, axis=1)
    hidden = (weight_all * hidden).astype(jnp.bfloat16)
    dhidden = weight_all * back
    up_grad = (dhidden * swished).astype(jnp.bfloat16)
    gate_grad = (dhidden * pre_up * sigmoid_gate * (1.0 + pre_gate * (1.0 - sigmoid_gate))).astype(
        jnp.bfloat16
    )
    dlogit = lax.psum(slope_all * dshare, ("dp", "expert", "mp"))

    def collect(partial_value):
        own = lax.psum_scatter(
            partial_value.astype(jnp.bfloat16), blocks, scatter_dimension=0, tiled=True
        )
        return lax.psum(own, "mp")

    mixed = collect(jnp.dot(hidden, w_down, preferred_element_type=jnp.float32))
    row_grads = collect(
        jnp.einsum("rf,df->rd", gate_grad, w_gate, preferred_element_type=jnp.float32)
        + jnp.einsum("rf,df->rd", up_grad, w_up, preferred_element_type=jnp.float32)
    )
    grad_down = jnp.einsum("rf,rd->fd", hidden, all_grads, preferred_element_type=jnp.float32)
    grad_gate = jnp.einsum("rd,rf->df", all_tokens, gate_grad, preferred_element_type=jnp.float32)
    grad_up = jnp.einsum("rd,rf->df", all_tokens, up_grad, preferred_element_type=jnp.float32)

    grad_logits = sign_all * dlogit[:, None]
    pieces = jnp.concatenate(split3(grad_logits), axis=1)
    grad_router = jnp.einsum("rd,re->de", all_tokens, pieces, preferred_element_type=jnp.float32)
    grad_router = (
        grad_router[:, 2 * experts :] + grad_router[:, experts : 2 * experts]
    ) + grad_router[:, :experts]
    tok_rows = tokens.shape[0]
    block = lax.axis_index("dp") * lax.axis_size("expert") + lax.axis_index("expert")
    own_logits = lax.dynamic_slice_in_dim(grad_logits, block * tok_rows, tok_rows, 0)
    router_back = jnp.dot(own_logits, w_router.T, precision=lax.Precision.HIGHEST)
    grad_tokens = (router_back + row_grads.astype(jnp.float32)).astype(jnp.bfloat16)
    return (
        mixed,
        grad_tokens,
        grad_router,
        grad_gate.astype(jnp.bfloat16)[None],
        grad_up.astype(jnp.bfloat16)[None],
        grad_down.astype(jnp.bfloat16)[None],
    )


def solution(mesh):
    in_specs = (
        P(("dp", "expert"), None),
        P(),
        P(("dp", "expert"), None),
        P(),
        P("expert", None, ("dp", "mp")),
        P("expert", None, ("dp", "mp")),
        P("expert", ("dp", "mp"), None),
        P(("dp", "expert"), None),
    )
    out_specs = (
        P(("dp", "expert"), None),
        P(("dp", "expert"), None),
        P(),
        P("expert", None, ("dp", "mp")),
        P("expert", None, ("dp", "mp")),
        P("expert", ("dp", "mp"), None),
    )
    return jax.shard_map(local, mesh=mesh, in_specs=in_specs, out_specs=out_specs, check_vma=False)
```

time: 188 us -> 150 us (0.80)
  Pallas kernels: 0 us -> 54.3 us
  matrix products: 66 us -> 16.9 us
  waiting for transfers between devices: 44.2 us -> 26.9 us
  other arithmetic: 14.3 us -> 4.16 us
  local copies, waits for them, and re-layouts: 18.8 us -> 9.33 us
  starting transfers between devices: 42.2 us -> 37 us
    pallas_call x0 -> x26, Pallas kernels: none -> 54.3 us  [the longest x2 17 us: rows_back(): pl.pallas_call(body, out_shape=(in_hbm((count, last - first)),) * 2, in_s...]
    dot_general x13 -> x4, matrix products: 66 us -> 16.9 us  [the longest x3 16.4 us: outer(): lax.dot_general(left, right, TN, preferred_element_type=jnp.float32)]
    ppermute x46 -> x9, waiting for transfers between devices: 44.2 us -> 10.8 us  [swap(): lax.ppermute(values, axis, [(place, place ^ flip) for place in range(size)])]
    ppermute x46 -> x9, starting transfers between devices: 42.2 us -> 13.9 us  [swap(): lax.ppermute(values, axis, [(place, place ^ flip) for place in range(size)])]
    ppermute x0 -> x31, starting transfers between devices: none -> 23.1 us  [trade(): return lax.ppermute(values, ('dp', 'expert'), pairs)]
    ppermute x0 -> x31, waiting for transfers between devices: none -> 16 us  [trade(): return lax.ppermute(values, ('dp', 'expert'), pairs)]
    unnamed x48 -> x40, local copies, waits for them, and re-layouts: 9.95 us -> 3.26 us
    slice x12 -> x2, local copies, waits for them, and re-layouts: 5.65 us -> 0.78 us  [the longest x1 0.76 us: local_pairs(): extra = (grad_logits[:tok_rows], w_router.T)]
  transfers between devices with their start and end apart: 46 -> 40, of which waited for: 24 -> 15; matrix products, arithmetic and copies ran while one was open for 44% -> 18% of each run, Pallas kernels for 0% -> 35%
where the time goes in v2:
time: 150 us
  Pallas kernels  54.3 us (36%)
  starting transfers between devices  37 us (25%)
  waiting for transfers between devices  26.9 us (18%)
  matrix products  16.9 us (11%)
  local copies, waits for them, and re-layouts  9.33 us (6%)
  other arithmetic  4.16 us (3%)
    ppermute x31, starting transfers between devices, trade(): return lax.ppermute(values, ('dp', 'expert'), pairs)  23.1 us
    pallas_call x2, Pallas kernels, rows_back(): pl.pallas_call(body, out_shape=(in_hbm((count, last - first)),) * 2, in_s...  17 us
    dot_general x3, matrix products, outer(): lax.dot_general(left, right, TN, preferred_element_type=jnp.float32)  16.4 us
    ppermute x31, waiting for transfers between devices, trade(): return lax.ppermute(values, ('dp', 'expert'), pairs)  16 us
    ppermute x9, starting transfers between devices, swap(): lax.ppermute(values, axis, [(place, place ^ flip) for place in range(size)])  13.9 us
    pallas_call x1, Pallas kernels, forward(): pl.pallas_call(body, out_shape=(in_hbm((count, width)),) * 3 + (in_hbm((c...  13.2 us
    ppermute x9, waiting for transfers between devices, swap(): lax.ppermute(values, axis, [(place, place ^ flip) for place in range(size)])  10.8 us
    pallas_call x1, Pallas kernels, backward(): pl.pallas_call(body, out_shape=(in_hbm((count, width)),) * 3 + (shaped((c...  10.2 us
  transfers between devices with their start and end apart: 40, of which 15 were waited for; matrix products, arithmetic and copies ran while one was open for 18% of the time, Pallas kernels for 35%

profile of v2, /device:TPU:0, one launch (start us, length us, event | category | flops | bytes accessed | tf_op | source)
XLA Modules:
  0.0 149.7 jit_solution(9691011139855899793)
XLA Ops:
  0.6 3.0 %collective-permute-start = (bf16[64,3072]{1,0:T(8,128)(2,1)}, bf16[64,3072]{1,0:T(8,128)(2,1)S(1)}, u32[]{:S(2)}, u32[]{:S(2)}) collective-permute-start(bf16[64,3072]{1,0:T(8,128)(2,1)} %refs_0_.2), channel_id=1, source_target_pairs={{0,4},{4,0},{8,12},{12,8},{16,24},{20,28},{24,16},{28,20},{1,5},{5... | collective-permute-start | bytes 1179656 | tf_op jit(solution)/shard_map/ppermute | solution.py:430
  3.6 1.5 %collective-permute-start.1 = (bf16[64,3072]{1,0:T(8,128)(2,1)}, bf16[64,3072]{1,0:T(8,128)(2,1)S(1)}, u32[]{:S(2)}, u32[]{:S(2)}) collective-permute-start(bf16[64,3072]{1,0:T(8,128)(2,1)} %refs_0_.2), channel_id=1, source_target_pairs={{0,8},{4,12},{8,0},{12,4},{16,20},{20,16},{24,28},{28,24},{1,9},{5... | collective-permute-start | bytes 1179656 | tf_op jit(solution)/shard_map/ppermute | solution.py:430
  5.2 2.1 %route.1 = f32[12,64]{1,0:T(8,128)} custom-call(bf16[64,3072]{1,0:T(8,128)(2,1)} %refs_0_.2, f32[4,3072]{1,0:T(4,128)} %bitcast.33, s32[2,64]{1,0:T(2,128)} %bitcast.47, s32[4]{0:T(128)} %partner.1), custom_call_target="tpu_custom_call" | custom-call | flops 1048576 | bytes 1048576 | tf_op jit(solution)/shard_map/route/pallas_call | solution.py:141
  7.2 6.1 %collective-permute-done.refs_1_ = bf16[64,3072]{1,0:T(8,128)(2,1)S(1)} collective-permute-done((bf16[64,3072]{1,0:T(8,128)(2,1)}, bf16[64,3072]{1,0:T(8,128)(2,1)S(1)}, u32[]{:S(2)}, u32[]{:S(2)}) %collective-permute-start) | collective-permute-done | bytes 393248 | tf_op jit(solution)/shard_map/ppermute | solution.py:430
  14.8 1.6 %collective-permute-start.3 = (f32[12,64]{1,0:T(8,128)}, f32[12,64]{1,0:T(8,128)S(1)}, u32[]{:S(2)}, u32[]{:S(2)}) collective-permute-start(f32[12,64]{1,0:T(8,128)} %route.1), channel_id=1, source_target_pairs={{0,4},{4,0},{8,12},{12,8},{16,24},{20,28},{24,16},{28,20},{1,5},{5... | collective-permute-start | bytes 9224 | tf_op jit(solution)/shard_map/ppermute | solution.py:430
  17.2 1.5 %collective-permute-done.3 = f32[12,64]{1,0:T(8,128)S(1)} collective-permute-done((f32[12,64]{1,0:T(8,128)}, f32[12,64]{1,0:T(8,128)S(1)}, u32[]{:S(2)}, u32[]{:S(2)}) %collective-permute-start.3) | collective-permute-done | bytes 3104 | tf_op jit(solution)/shard_map/ppermute | solution.py:430
  19.8 2.7 %collective-permute-done.4 = f32[2,12,64]{2,0,1:T(2,128)S(1)} collective-permute-done((f32[2,12,64]{2,0,1:T(2,128)S(1)}, f32[2,12,64]{2,0,1:T(2,128)S(1)}, u32[]{:S(2)}, u32[]{:S(2)}) %collective-permute-start.4) | collective-permute-done | bytes 6176 | tf_op jit(solution)/shard_map/ppermute | solution.py:430
  23.2 2.3 %collective-permute-start.11 = (bf16[64,3072]{1,0:T(8,128)(2,1)}, bf16[64,3072]{1,0:T(8,128)(2,1)S(1)}, u32[]{:S(2)}, u32[]{:S(2)}) collective-permute-start(bf16[64,3072]{1,0:T(8,128)(2,1)} %refs_0_.3), channel_id=1, source_target_pairs={{0,12},{4,8},{8,4},{12,0},{16,28},{20,24},{24,20},{28,16},{1,13},{... | collective-permute-start | bytes 1179656 | tf_op jit(solution)/shard_map/ppermute | solution.py:430
  27.2 13.2 %forward.1 = (bf16[512,1024]{1,0:T(8,128)(2,1)}, bf16[512,1024]{1,0:T(8,128)(2,1)}, bf16[512,1024]{1,0:T(8,128)(2,1)}, bf16[512,3072]{1,0:T(8,128)(2,1)}) custom-call(bf16[64,3072]{1,0:T(8,128)(2,1)} %refs_0_.2, bf16[64,3072]{1,0:T(8,128)(2,1)} %copy-done.15, bf16[64,3072]{1,0:T(8,128)(2,1)} %copy-done.16, bf16[64,3072]{1,0:T(8,128)(2,1)} %copy-done.17, ...), custom_call_target="tpu_custom_call" | custom-call | flops 6442450944 | bytes 18874368 | tf_op jit(solution)/shard_map/forward/pallas_call | solution.py:211
  40.4 7.6 %down.1 = (bf16[512,1536]{1,0:T(8,128)(2,1)}, bf16[512,1536]{1,0:T(8,128)(2,1)}) custom-call(s32[1]{0:T(128)} %bitcast.core_ref, bf16[512,1024]{1,0:T(8,128)(2,1)} %get-tuple-element.93.hid.refs_9_, bf16[1024,3072]{1,0:T(8,128)(2,1)} %bitcast.41), custom_call_target="tpu_custom_call" | custom-call | flops 3221225472 | bytes 6291456 | tf_op jit(solution)/shard_map/down/pallas_call | solution.py:258
  49.3 2.1 %collective-permute-done.16 = f32[4,12,64]{2,0,1:T(4,128)S(1)} collective-permute-done((f32[4,12,64]{2,0,1:T(4,128)S(1)}, f32[4,12,64]{2,0,1:T(4,128)S(1)}, u32[]{:S(2)}, u32[]{:S(2)}) %collective-permute-start.16) | collective-permute-done | bytes 12320 | tf_op jit(solution)/shard_map/ppermute | solution.py:430
  55.3 10.2 %backward.1 = (bf16[512,1024]{1,0:T(8,128)(2,1)}, bf16[512,1024]{1,0:T(8,128)(2,1)}, bf16[512,1024]{1,0:T(8,128)(2,1)}, f32[512,1]{1,0:T(8,128)S(1)}, bf16[512,3072]{1,0:T(8,128)(2,1)}) custom-call(bf16[64,3072]{1,0:T(8,128)(2,1)} %refs_0_.3, bf16[64,3072]{1,0:T(8,128)(2,1)} %copy-done.12, bf16[64,3072]{1,0:T(8,128)(2,1)} %copy-done.11, ...), custom_call_target="tpu_custom_call" | custom-call | flops 3221225472 | bytes 6291456 | tf_op jit(solution)/shard_map/backward/pallas_call | solution.py:322
  70.6 8.4 %rows_back.2 = (bf16[512,768]{1,0:T(8,128)(2,1)}, bf16[512,768]{1,0:T(8,128)(2,1)}) custom-call(s32[1]{0:T(128)} %bitcast.core_ref, bf16[512,1024]{1,0:T(8,128)(2,1)} %get-tuple-element.117.gate_in, bf16[512,1024]{1,0:T(8,128)(2,1)} %get-tuple-element.109.up_in, bf16[3072,1024]{1,0:T(8,128)(2,1)} %bitcast.36, bf16[3072,1024]{1,0:T(8,128)(2,1)} %bitcast.39), custom_call_target="tpu_custom_call" | custom-call | flops 3221225472 | bytes 6291456 | tf_op jit(solution)/shard_map/rows_back/pallas_call | solution.py:387
  83.2 8.6 %rows_back.3 = (bf16[512,768]{1,0:T(8,128)(2,1)}, bf16[512,768]{1,0:T(8,128)(2,1)}) custom-call(s32[1]{0:T(128)} %bitcast.core_ref, bf16[512,1024]{1,0:T(8,128)(2,1)} %get-tuple-element.117.gate_in, bf16[512,1024]{1,0:T(8,128)(2,1)} %get-tuple-element.109.up_in, bf16[3072,1024]{1,0:T(8,128)(2,1)} %bitcast.37, bf16[3072,1024]{1,0:T(8,128)(2,1)} %bitcast.40), custom_call_target="tpu_custom_call" | custom-call | flops 3221225472 | bytes 6291456 | tf_op jit(solution)/shard_map/rows_back/pallas_call | solution.py:387
  97.2 5.6 %convolution_convert_fusion.2 = bf16[1024,3072]{1,0:T(8,128)(2,1)} fusion(bf16[512,1024]{1,0:T(8,128)(2,1)S(1)} %copy-done.14, bf16[512,3072]{1,0:T(8,128)(2,1)S(1)} %copy-done.13), kind=kOutput, calls=%fused_computation.2 | convolution fusion | flops 3224371200 | bytes 10485760 | tf_op jit(solution)/shard_map/dot_general | solution.py:402
  105.4 2.8 %collective-permute-start.27 = (bf16[144,768]{1,0:T(8,128)(2,1)S(1)}, bf16[144,768]{1,0:T(8,128)(2,1)S(1)}, u32[]{:S(2)}, u32[]{:S(2)}) collective-permute-start(bf16[144,768]{1,0:T(8,128)(2,1)S(1)} %get-tuple-element.147.refs_0_), channel_id=1, source_target_pairs={{0,2},{1,3},{2,0},{3,1},{4,6},{5,7},{6,4},{7,5},{8,10},{9,11},{10,... | collective-permute-start | bytes 663560 | tf_op jit(solution)/shard_map/ppermute | solution.py:56
  109.1 5.4 %convolution_convert_fusion.1 = bf16[3072,1024]{1,0:T(8,128)(2,1)} fusion(bf16[512,3072]{1,0:T(8,128)(2,1)S(1)} %copy-done.6, bf16[512,1024]{1,0:T(8,128)(2,1)S(1)} %copy-done.8), kind=kOutput, calls=%fused_computation.1 | convolution fusion | flops 3224371200 | bytes 10485760 | tf_op jit(solution)/shard_map/dot_general | solution.py:402
  114.5 2.2 %collective-permute-done.27.refs_1_ = bf16[144,768]{1,0:T(8,128)(2,1)S(1)} collective-permute-done((bf16[144,768]{1,0:T(8,128)(2,1)S(1)}, bf16[144,768]{1,0:T(8,128)(2,1)S(1)}, u32[]{:S(2)}, u32[]{:S(2)}) %collective-permute-start.27) | collective-permute-done | bytes 221216 | tf_op jit(solution)/shard_map/ppermute | solution.py:56
  117.6 5.4 %convolution_convert_fusion = bf16[3072,1024]{1,0:T(8,128)(2,1)} fusion(bf16[512,3072]{1,0:T(8,128)(2,1)S(1)} %copy-done.6, bf16[512,1024]{1,0:T(8,128)(2,1)S(1)} %copy-done.7), kind=kOutput, calls=%fused_computation | convolution fusion | flops 3224371200 | bytes 10485760 | tf_op jit(solution)/shard_map/dot_general | solution.py:402
  123.5 1.5 %collective-permute-start.31 = (bf16[128,384]{1,0:T(8,128)(2,1)S(1)}, bf16[128,384]{1,0:T(8,128)(2,1)S(1)}, u32[]{:S(2)}, u32[]{:S(2)}) collective-permute-start(bf16[128,384]{1,0:T(8,128)(2,1)S(1)} %get-tuple-element.161), channel_id=1, source_target_pairs={{0,1},{1,0},{2,3},{3,2},{4,5},{5,4},{6,7},{7,6},{8,9},{9,8},{10,11... | collective-permute-start | bytes 294920 | tf_op jit(solution)/shard_map/ppermute | solution.py:56
  125.6 3.6 %collective-permute-done.31.refs_1_ = bf16[128,384]{1,0:T(8,128)(2,1)S(1)} collective-permute-done((bf16[128,384]{1,0:T(8,128)(2,1)S(1)}, bf16[128,384]{1,0:T(8,128)(2,1)S(1)}, u32[]{:S(2)}, u32[]{:S(2)}) %collective-permute-start.31) | collective-permute-done | bytes 98336 | tf_op jit(solution)/shard_map/ppermute | solution.py:56
  129.2 3.2 %collective-permute-start.34 = (bf16[128,384]{1,0:T(8,128)(2,1)S(1)}, bf16[128,384]{1,0:T(8,128)(2,1)S(1)}, u32[]{:S(2)}, u32[]{:S(2)}) collective-permute-start(bf16[128,384]{1,0:T(8,128)(2,1)S(1)} %step.8.refs_0_), channel_id=1, source_target_pairs={{0,2},{1,3},{2,0},{3,1},{4,6},{5,7},{6,4},{7,5},{8,10},{9,11},{10,... | collective-permute-start | bytes 294920 | tf_op jit(solution)/shard_map/ppermute | solution.py:56
  132.4 1.6 %collective-permute-start.35 = (bf16[128,384]{1,0:T(8,128)(2,1)S(1)}, bf16[128,384]{1,0:T(8,128)(2,1)S(1)}, u32[]{:S(2)}, u32[]{:S(2)}) collective-permute-start(bf16[128,384]{1,0:T(8,128)(2,1)S(1)} %step.9.refs_0_), channel_id=1, source_target_pairs={{0,2},{1,3},{2,0},{3,1},{4,6},{5,7},{6,4},{7,5},{8,10},{9,11},{10,... | collective-permute-start | bytes 294920 | tf_op jit(solution)/shard_map/ppermute | solution.py:56
  143.0 3.0 %collective-permute-done.38.refs_1_ = bf16[128,384]{1,0:T(8,128)(2,1)S(1)} collective-permute-done((bf16[128,384]{1,0:T(8,128)(2,1)S(1)}, bf16[128,384]{1,0:T(8,128)(2,1)S(1)}, u32[]{:S(2)}, u32[]{:S(2)}) %collective-permute-start.38) | collective-permute-done | bytes 98336 | tf_op jit(solution)/shard_map/ppermute | solution.py:56
  (152 shorter events, 43.3 us)
Async XLA Ops:
  0.6 12.7 %collective-permute-start = (bf16[64,3072]{1,0:T(8,128)(2,1)}, bf16[64,3072]{1,0:T(8,128)(2,1)S(1)}, u32[]{:S(2)}, u32[]{:S(2)}) collective-permute-start(bf16[64,3072]{1,0:T(8,128)(2,1)} %refs_0_.2), channel_id=1, source_target_pairs={{0,4},{4,0},{8,12},{12,8},{16,24},{20,28},{24,16},{28,20},{1,5},{5... | collective-permute-start | bytes 1179656 | tf_op jit(solution)/shard_map/ppermute | solution.py:430
  3.6 19.0 %collective-permute-start.1 = (bf16[64,3072]{1,0:T(8,128)(2,1)}, bf16[64,3072]{1,0:T(8,128)(2,1)S(1)}, u32[]{:S(2)}, u32[]{:S(2)}) collective-permute-start(bf16[64,3072]{1,0:T(8,128)(2,1)} %refs_0_.2), channel_id=1, source_target_pairs={{0,8},{4,12},{8,0},{12,4},{16,20},{20,16},{24,28},{28,24},{1,9},{5... | collective-permute-start | bytes 1179656 | tf_op jit(solution)/shard_map/ppermute | solution.py:430
  13.4 9.8 %collective-permute-start.2 = (bf16[64,3072]{1,0:T(8,128)(2,1)S(1)}, bf16[64,3072]{1,0:T(8,128)(2,1)S(1)}, u32[]{:S(2)}, u32[]{:S(2)}) collective-permute-start(bf16[64,3072]{1,0:T(8,128)(2,1)S(1)} %collective-permute-done.refs_1_), channel_id=1, source_target_pairs={{0,8},{4,12},{8,0},{12,4},{16,20},{20,16},{24,28},{28,24},{1,9},{5... | collective-permute-start | bytes 1179656 | tf_op jit(solution)/shard_map/ppermute | solution.py:430
  23.2 24.8 %collective-permute-start.11 = (bf16[64,3072]{1,0:T(8,128)(2,1)}, bf16[64,3072]{1,0:T(8,128)(2,1)S(1)}, u32[]{:S(2)}, u32[]{:S(2)}) collective-permute-start(bf16[64,3072]{1,0:T(8,128)(2,1)} %refs_0_.3), channel_id=1, source_target_pairs={{0,12},{4,8},{8,4},{12,0},{16,28},{20,24},{24,20},{28,16},{1,13},{... | collective-permute-start | bytes 1179656 | tf_op jit(solution)/shard_map/ppermute | solution.py:430
  25.6 22.5 %collective-permute-start.10 = (bf16[64,3072]{1,0:T(8,128)(2,1)}, bf16[64,3072]{1,0:T(8,128)(2,1)S(1)}, u32[]{:S(2)}, u32[]{:S(2)}) collective-permute-start(bf16[64,3072]{1,0:T(8,128)(2,1)} %refs_0_.3), channel_id=1, source_target_pairs={{0,8},{4,12},{8,0},{12,4},{16,20},{20,16},{24,28},{28,24},{1,9},{5... | collective-permute-start | bytes 1179656 | tf_op jit(solution)/shard_map/ppermute | solution.py:430
  26.4 21.6 %collective-permute-start.9 = (bf16[64,3072]{1,0:T(8,128)(2,1)}, bf16[64,3072]{1,0:T(8,128)(2,1)S(1)}, u32[]{:S(2)}, u32[]{:S(2)}) collective-permute-start(bf16[64,3072]{1,0:T(8,128)(2,1)} %refs_0_.3), channel_id=1, source_target_pairs={{0,4},{4,0},{8,12},{12,8},{16,24},{20,28},{24,16},{28,20},{1,5},{5... | collective-permute-start | bytes 1179656 | tf_op jit(solution)/shard_map/ppermute | solution.py:430
  48.1 19.5 %collective-permute-start.17 = (bf16[512,1536]{1,0:T(8,128)(2,1)}, bf16[512,1536]{1,0:T(8,128)(2,1)S(1)}, u32[]{:S(2)}, u32[]{:S(2)}) collective-permute-start(bf16[512,1536]{1,0:T(8,128)(2,1)} %get-tuple-element.105), channel_id=1, source_target_pairs={{0,16},{4,20},{8,24},{12,28},{16,0},{20,4},{24,8},{28,12},{1,17},{... | collective-permute-start | bytes 4718600 | tf_op jit(solution)/shard_map/ppermute | solution.py:430
  48.2 6.1 %collective-permute-start.12 = (bf16[64,3072]{1,0:T(8,128)(2,1)S(1)}, bf16[64,3072]{1,0:T(8,128)(2,1)}, u32[]{:S(2)}, u32[]{:S(2)}) collective-permute-start(bf16[64,3072]{1,0:T(8,128)(2,1)S(1)} %copy-done.9), channel_id=1, source_target_pairs={{0,16},{4,20},{8,24},{12,28},{16,0},{20,4},{24,8},{28,12},{1,17},{... | collective-permute-start | bytes 1179656 | tf_op jit(solution)/shard_map/ppermute | solution.py:430
  68.1 12.3 %collective-permute-start.18 = (bf16[272,768]{1,0:T(8,128)(2,1)S(1)}, bf16[272,768]{1,0:T(8,128)(2,1)S(1)}, u32[]{:S(2)}, u32[]{:S(2)}) collective-permute-start(bf16[272,768]{1,0:T(8,128)(2,1)S(1)} %get-tuple-element.113), channel_id=1, source_target_pairs={{0,4},{4,0},{8,12},{12,8},{16,24},{20,28},{24,16},{28,20},{1,5},{5... | collective-permute-start | bytes 1253384 | tf_op jit(solution)/shard_map/ppermute | solution.py:430
  69.5 10.2 %collective-permute-start.19 = (bf16[256,768]{1,0:T(8,128)(2,1)S(1)}, bf16[256,768]{1,0:T(8,128)(2,1)S(1)}, u32[]{:S(2)}, u32[]{:S(2)}) collective-permute-start(bf16[256,768]{1,0:T(8,128)(2,1)S(1)} %get-tuple-element.114), channel_id=1, source_target_pairs={{0,8},{4,12},{8,0},{12,4},{16,20},{20,16},{24,28},{28,24},{1,9},{5... | collective-permute-start | bytes 1179656 | tf_op jit(solution)/shard_map/ppermute | solution.py:430
  80.6 11.4 %collective-permute-start.22 = (bf16[512,768]{1,0:T(8,128)(2,1)}, bf16[512,768]{1,0:T(8,128)(2,1)S(1)}, u32[]{:S(2)}, u32[]{:S(2)}) collective-permute-start(bf16[512,768]{1,0:T(8,128)(2,1)} %get-tuple-element.129), channel_id=1, source_target_pairs={{0,16},{4,20},{8,24},{12,28},{16,0},{20,4},{24,8},{28,12},{1,17},{... | collective-permute-start | bytes 2359304 | tf_op jit(solution)/shard_map/ppermute | solution.py:430
  80.7 11.0 %collective-permute-start.20 = (bf16[144,768]{1,0:T(8,128)(2,1)S(1)}, bf16[144,768]{1,0:T(8,128)(2,1)S(1)}, u32[]{:S(2)}, u32[]{:S(2)}) collective-permute-start(bf16[144,768]{1,0:T(8,128)(2,1)S(1)} %get-tuple-element.121), channel_id=1, source_target_pairs={{0,8},{4,12},{8,0},{12,4},{16,20},{20,16},{24,28},{28,24},{1,9},{5... | collective-permute-start | bytes 663560 | tf_op jit(solution)/shard_map/ppermute | solution.py:430
  81.8 9.9 %collective-permute-start.21 = (bf16[128,768]{1,0:T(8,128)(2,1)S(1)}, bf16[128,768]{1,0:T(8,128)(2,1)S(1)}, u32[]{:S(2)}, u32[]{:S(2)}) collective-permute-start(bf16[128,768]{1,0:T(8,128)(2,1)S(1)} %get-tuple-element.122), channel_id=1, source_target_pairs={{0,4},{4,0},{8,12},{12,8},{16,24},{20,28},{24,16},{28,20},{1,5},{5... | collective-permute-start | bytes 589832 | tf_op jit(solution)/shard_map/ppermute | solution.py:430
  92.3 13.0 %collective-permute-start.24 = (bf16[144,768]{1,0:T(8,128)(2,1)S(1)}, bf16[144,768]{1,0:T(8,128)(2,1)S(1)}, u32[]{:S(2)}, u32[]{:S(2)}) collective-permute-start(bf16[144,768]{1,0:T(8,128)(2,1)S(1)} %get-tuple-element.136), channel_id=1, source_target_pairs={{0,1},{1,0},{2,3},{3,2},{4,5},{5,4},{6,7},{7,6},{8,9},{9,8},{10,11... | collective-permute-start | bytes 663560 | tf_op jit(solution)/shard_map/ppermute | solution.py:56
  93.8 10.4 %collective-permute-start.25 = (bf16[256,768]{1,0:T(8,128)(2,1)S(1)}, bf16[256,768]{1,0:T(8,128)(2,1)S(1)}, u32[]{:S(2)}, u32[]{:S(2)}) collective-permute-start(bf16[256,768]{1,0:T(8,128)(2,1)S(1)} %get-tuple-element.141), channel_id=1, source_target_pairs={{0,4},{4,0},{8,12},{12,8},{16,24},{20,28},{24,16},{28,20},{1,5},{5... | collective-permute-start | bytes 1179656 | tf_op jit(solution)/shard_map/ppermute | solution.py:430
  96.1 12.1 %collective-permute-start.26 = (bf16[256,768]{1,0:T(8,128)(2,1)S(1)}, bf16[256,768]{1,0:T(8,128)(2,1)S(1)}, u32[]{:S(2)}, u32[]{:S(2)}) collective-permute-start(bf16[256,768]{1,0:T(8,128)(2,1)S(1)} %get-tuple-element.144), channel_id=1, source_target_pairs={{0,8},{4,12},{8,0},{12,4},{16,20},{20,16},{24,28},{28,24},{1,9},{5... | collective-permute-start | bytes 1179656 | tf_op jit(solution)/shard_map/ppermute | solution.py:430
  104.3 13.1 %collective-permute-start.28 = (bf16[128,768]{1,0:T(8,128)(2,1)S(1)}, bf16[128,768]{1,0:T(8,128)(2,1)S(1)}, u32[]{:S(2)}, u32[]{:S(2)}) collective-permute-start(bf16[128,768]{1,0:T(8,128)(2,1)S(1)} %get-tuple-element.151), channel_id=1, source_target_pairs={{0,8},{4,12},{8,0},{12,4},{16,20},{20,16},{24,28},{28,24},{1,9},{5... | collective-permute-start | bytes 589832 | tf_op jit(solution)/shard_map/ppermute | solution.py:430
  105.4 11.3 %collective-permute-start.27 = (bf16[144,768]{1,0:T(8,128)(2,1)S(1)}, bf16[144,768]{1,0:T(8,128)(2,1)S(1)}, u32[]{:S(2)}, u32[]{:S(2)}) collective-permute-start(bf16[144,768]{1,0:T(8,128)(2,1)S(1)} %get-tuple-element.147.refs_0_), channel_id=1, source_target_pairs={{0,2},{1,3},{2,0},{3,1},{4,6},{5,7},{6,4},{7,5},{8,10},{9,11},{10,... | collective-permute-start | bytes 663560 | tf_op jit(solution)/shard_map/ppermute | solution.py:56
  108.4 9.1 %collective-permute-start.29 = (bf16[128,768]{1,0:T(8,128)(2,1)S(1)}, bf16[128,768]{1,0:T(8,128)(2,1)S(1)}, u32[]{:S(2)}, u32[]{:S(2)}) collective-permute-start(bf16[128,768]{1,0:T(8,128)(2,1)S(1)} %get-tuple-element.154), channel_id=1, source_target_pairs={{0,4},{4,0},{8,12},{12,8},{16,24},{20,28},{24,16},{28,20},{1,5},{5... | collective-permute-start | bytes 589832 | tf_op jit(solution)/shard_map/ppermute | solution.py:430
  116.8 6.5 %collective-permute-start.30 = (bf16[144,768]{1,0:T(8,128)(2,1)S(1)}, bf16[144,768]{1,0:T(8,128)(2,1)S(1)}, u32[]{:S(2)}, u32[]{:S(2)}) collective-permute-start(bf16[144,768]{1,0:T(8,128)(2,1)S(1)} %get-tuple-element.157.refs_0_), channel_id=1, source_target_pairs={{0,1},{1,0},{2,3},{3,2},{4,5},{5,4},{6,7},{7,6},{8,9},{9,8},{10,11... | collective-permute-start | bytes 663560 | tf_op jit(solution)/shard_map/ppermute | solution.py:56
  123.4 10.6 %collective-permute-start.33 = (bf16[80,1536]{1,0:T(8,128)(2,1)S(1)}, bf16[80,1536]{1,0:T(8,128)(2,1)S(1)}, u32[]{:S(2)}, u32[]{:S(2)}) collective-permute-start(bf16[80,1536]{1,0:T(8,128)(2,1)S(1)} %get-tuple-element.165), channel_id=1, source_target_pairs={{0,16},{4,20},{8,24},{12,28},{16,0},{20,4},{24,8},{28,12},{1,17},{... | collective-permute-start | bytes 737288 | tf_op jit(solution)/shard_map/ppermute | solution.py:430
  125.0 7.4 %collective-permute-start.32 = (bf16[128,384]{1,0:T(8,128)(2,1)S(1)}, bf16[128,384]{1,0:T(8,128)(2,1)S(1)}, u32[]{:S(2)}, u32[]{:S(2)}) collective-permute-start(bf16[128,384]{1,0:T(8,128)(2,1)S(1)} %get-tuple-element.163), channel_id=1, source_target_pairs={{0,1},{1,0},{2,3},{3,2},{4,5},{5,4},{6,7},{7,6},{8,9},{9,8},{10,11... | collective-permute-start | bytes 294920 | tf_op jit(solution)/shard_map/ppermute | solution.py:56
  129.2 10.9 %collective-permute-start.34 = (bf16[128,384]{1,0:T(8,128)(2,1)S(1)}, bf16[128,384]{1,0:T(8,128)(2,1)S(1)}, u32[]{:S(2)}, u32[]{:S(2)}) collective-permute-start(bf16[128,384]{1,0:T(8,128)(2,1)S(1)} %step.8.refs_0_), channel_id=1, source_target_pairs={{0,2},{1,3},{2,0},{3,1},{4,6},{5,7},{6,4},{7,5},{8,10},{9,11},{10,... | collective-permute-start | bytes 294920 | tf_op jit(solution)/shard_map/ppermute | solution.py:56
  132.4 8.5 %collective-permute-start.35 = (bf16[128,384]{1,0:T(8,128)(2,1)S(1)}, bf16[128,384]{1,0:T(8,128)(2,1)S(1)}, u32[]{:S(2)}, u32[]{:S(2)}) collective-permute-start(bf16[128,384]{1,0:T(8,128)(2,1)S(1)} %step.9.refs_0_), channel_id=1, source_target_pairs={{0,2},{1,3},{2,0},{3,1},{4,6},{5,7},{6,4},{7,5},{8,10},{9,11},{10,... | collective-permute-start | bytes 294920 | tf_op jit(solution)/shard_map/ppermute | solution.py:56
  (36 other events, 200.1 us)

commit v3 on v2

--- a/solution.py
+++ b/solution.py
@@ -180,21 +180,27 @@
 
     def body(*refs):
         pieces, refs = refs[:number], refs[number:]
-        wg, wu, hid, sw, sg, everything, x, bg, bu, gates, h, a, b, sems_in, sems_out = refs
+        wg, wu, hid, sw, sg, everything, x, bg, bu, h, a, b, sems_in, sems_out = refs
         mover, outward = Mover(sems_in), Mover(sems_out)
-        copies = [mover.start(wg, bg)]
-        for copy in fetch_rows(mover, pieces, x):
+        moves = fetch_rows(mover, pieces, x)
+        tiles = [pl.ds(step * tile, tile) for step in range(width // tile)]
+        copies = [
+            (
+                mover.start(wg.at[:, place], bg.at[:, place]),
+                mover.start(wu.at[:, place], bu.at[:, place]),
+            )
+            for place in tiles
+        ]
+        for copy in moves:
             copy.wait()
-        copies.append(mover.start(wu, bu))
-        copies[0].wait()
-        tiles = [pl.ds(step * tile, tile) for step in range(width // tile)]
-        for place in tiles:
-            gates[:, place] = jnp.dot(x[...], bg[:, place], preferred_element_type=jnp.float32)
-        done = [outward.start(x, everything)]
-        copies[1].wait()
-        for place in tiles:
+        done = []
+        for place, pair in zip(tiles, copies):
+            for copy in pair:
+                copy.wait()
+            if pair is copies[-1]:
+                done.append(outward.start(x, everything))
+            gate = jnp.dot(x[...], bg[:, place], preferred_element_type=jnp.float32)
             up = jnp.dot(x[...], bu[:, place], preferred_element_type=jnp.float32)
-            gate = gates[:, place]
             sigmoid_gate = jax.nn.sigmoid(gate)
             swished = gate * sigmoid_gate
             h[:, place] = (swished * up).astype(jnp.bfloat16)
@@ -217,11 +223,10 @@
             pltpu.VMEM((count, features), jnp.bfloat16),
             weights,
             weights,
-            pltpu.VMEM((count, width), jnp.float32),
             flat,
             flat,
             flat,
-            pltpu.SemaphoreType.DMA((number + 2,)),
+            pltpu.SemaphoreType.DMA((number + 2 * (width // tile),)),
             pltpu.SemaphoreType.DMA((4,)),
         ],
         compiler_params=pltpu.CompilerParams(vmem_limit_bytes=40 << 20),
@@ -340,13 +345,19 @@
     )(*on_hbm(*blocks, w_down, hidden, sw, sg), weight, slope)
 
 
-def rows_back(core, gate_grad, up_grad, w_gate, w_up, first, last, tile, pins):
+def rows_back(core, gate_grad, up_grad, w_gate, w_up, first, last, tile, pins, rider=None):
     count, width = gate_grad.shape
     half = w_gate.shape[0] // 2
     gate_grad = after(gate_grad, pins)
     steps = (last - first) // tile
 
-    def body(core_ref, gate_in, up_in, wg, wu, keep, send, gg, ug, bg, bu, k, s, sems_in, sems_out):
+    riders = [] if rider is None else [rider]
+    tail = TAIL * len(riders)
+
+    def body(core_ref, gate_in, up_in, wg, wu, *refs):
+        keep, send, gg, ug, bg, bu, k, s, sems_in, sems_out = refs[len(riders) :]
+        if riders:
+            s[count:, : rider.shape[1]] = pack(refs[0][...])
         mover, outward = Mover(sems_in), Mover(sems_out)
         me = core_ref[0]
         pieces = []
@@ -376,7 +387,7 @@
             total = total + lax.dot_general(
                 ug[...], bu[place, :], NT, preferred_element_type=jnp.float32
             )
-            target[:, columns] = total.astype(jnp.bfloat16)
+            target[:count, columns] = total.astype(jnp.bfloat16)
             done.append(outward.start(target.at[:, columns], out.at[:, columns]))
         for copy in done:
             copy.wait()
@@ -384,17 +395,18 @@
     flat = pltpu.VMEM((count, width), jnp.bfloat16)
     weights = pltpu.VMEM((2 * (last - first), width), jnp.bfloat16)
     part = pltpu.VMEM((count, last - first), jnp.bfloat16)
+    sent = (count + tail, last - first)
     return pl.pallas_call(
         body,
-        out_shape=(in_hbm((count, last - first)),) * 2,
-        in_specs=[pl.BlockSpec(memory_space=pltpu.SMEM)] + [LEFT] * 4,
+        out_shape=(in_hbm((count, last - first)), in_hbm(sent)),
+        in_specs=[pl.BlockSpec(memory_space=pltpu.SMEM)] + [LEFT] * 4 + [WHOLE] * len(riders),
         out_specs=(LEFT,) * 2,
-        scratch_shapes=[flat, flat, weights, weights, part, part]
+        scratch_shapes=[flat, flat, weights, weights, part, pltpu.VMEM(sent, jnp.bfloat16)]
         + [pltpu.SemaphoreType.DMA((4 * steps + 2,)), pltpu.SemaphoreType.DMA((2 * steps,))],
         compiler_params=pltpu.CompilerParams(vmem_limit_bytes=40 << 20),
         name="rows_back",
         cost_estimate=cost(8 * count * (last - first) * width, 8 * (last - first) * width),
-    )(core, *on_hbm(gate_grad, up_grad, w_gate, w_up))
+    )(core, *on_hbm(gate_grad, up_grad, w_gate, w_up), *riders)
 
 
 def outer(left, right, pins):
@@ -434,17 +446,26 @@
 
 
 def pack(values):
-    high, middle, low = split3(values)
-    shape = (TAIL, values.shape[1])
-    row = lax.broadcasted_iota(jnp.int32, shape, 0)
-    out = jnp.zeros(shape, jnp.float32)
-    for number, piece in enumerate((high, middle, low)):
-        out = jnp.where(row == number, piece.astype(jnp.float32), out)
+    count, length = values.shape
+    row = lax.broadcasted_iota(jnp.int32, (TAIL, length), 0)
+    out = jnp.zeros((TAIL, length), jnp.float32)
+    for number, piece in enumerate(split3(values)):
+        for place in range(count):
+            line = piece[place : place + 1, :].astype(jnp.float32)
+            out = jnp.where(row == number * count + place, line, out)
     return out.astype(jnp.bfloat16)
 
 
-def unpack(block):
-    return jnp.sum(block.astype(jnp.float32), axis=0, keepdims=True)
+def unpack(block, count):
+    block = block.astype(jnp.float32)
+    row = lax.broadcasted_iota(jnp.int32, block.shape, 0)
+    line = lax.broadcasted_iota(jnp.int32, (count, block.shape[1]), 0)
+    out = jnp.zeros((count, block.shape[1]), jnp.float32)
+    for place in range(count):
+        picked = (row == place) | (row == count + place) | (row == 2 * count + place)
+        total = jnp.sum(jnp.where(picked, block, 0.0), axis=0, keepdims=True)
+        out = jnp.where(line == place, total, out)
+    return out
 
 
 class Reduction:
@@ -471,7 +492,7 @@
                     )
 
         shape = (4 * rows, self.width)
-        sent = self.run(body, [shape], [shape], [], pins, "spread_part", False)
+        sent = self.run(body, [shape], [shape], [], pins, "spread_part", True)
         self.arrived = (trade(sent[0], ("first", "second")[number]),)
         return list(self.keep)
 
@@ -494,10 +515,10 @@
         rows, half = 2 * self.rows, self.width // 2
 
         def body(inputs, sent, kept):
-            one = add(inputs[0][:, :half], inputs[1][:, :half])
-            two = add(inputs[0][:, half:], inputs[1][:, half:])
+            one = add(inputs[0][:, :half], inputs[1][:rows, :half])
+            two = add(inputs[0][:, half:], inputs[1][:rows, half:])
             flag = inputs[2][...] > 0
-            sent[0][...] = jnp.where(flag, one, two)
+            sent[0][:rows, :] = jnp.where(flag, one, two)
             kept[0][...] = jnp.where(flag, two, one)
 
         shape = (rows, half)
@@ -520,13 +541,15 @@
 
         def whole(*refs):
             inputs, outputs = refs[: len(args)], refs[len(args) :]
-            body(inputs, outputs[: len(sent)], outputs[len(sent) : len(sent) + len(kept)])
+            given = inputs[:-1] if riding else inputs
+            body(given, outputs[: len(sent)], outputs[len(sent) : len(sent) + len(kept)])
             if riding:
                 total = inputs[-1][...]
                 length = total.shape[1]
                 if rides:
                     arrived = inputs[tail_at]
-                    total = total + unpack(arrived[arrived.shape[0] - TAIL :, :length])
+                    block = arrived[arrived.shape[0] - TAIL :, :length]
+                    total = total + unpack(block, total.shape[0])
                 outputs[-1][...] = total
                 outputs[0][sent[0][0] :, :length] = pack(total)
 
@@ -620,17 +643,21 @@
         return list(self.keep)
 
 
+def meet(sums, pins):
+    sizes = [len(item.arrived) for item in sums]
+    held = lax.optimization_barrier(
+        (*[array for item in sums for array in item.arrived], *pins)
+    )
+    for item, size in zip(sums, sizes):
+        item.arrived, held = held[:size], held[size:]
+
+
 def finish(parts, core, extra, pins, name):
     rows, width = parts[0].keep[0].shape
     features = 2 * width * len(parts)
-    rider = parts[0].rider
-    riding = rider is not None
     args = [item for part in parts for item in (part.keep[0], part.arrived[0])]
     at = len(args)
-    args += [core, *extra] + ([rider] if riding else [])
-    outs = [shaped((rows, features))]
-    if riding:
-        outs.append(shaped(rider.shape, jnp.float32))
+    args += [core, *extra]
 
     def body(*refs):
         out = refs[len(args)]
@@ -648,11 +675,8 @@
                             router[expert : expert + 1, columns]
                         )
                 out[:, columns] = values.astype(jnp.bfloat16)
-        if riding:
-            own = refs[len(args) - 1][...]
-            refs[-1][...] = own + unpack(refs[1][rows:, : own.shape[1]])
-
-    return small_call(body, outs, args, pins, name)
+
+    return small_call(body, [shaped((rows, features))], args, pins, name)[0]
 
 
 def gather_rows(block, peer, near, second, far):
@@ -698,12 +722,13 @@
     out_second = trade(later, "second")
     out_far = trade(later, "both")
     out_peer = trade(grad_out, "peer")
-    hidden, sw, sg, all_tokens = forward(token_blocks, w_gate, w_up, width // 4)
-    small = jnp.concatenate([small, swapped(after(small_peer, [hidden]))], axis=0)
+    small = jnp.concatenate([small, swapped(small_peer)], axis=0)
     mine = (lax.iota(jnp.int32, experts) == lax.axis_index("expert")).astype(jnp.float32)
     mine = mine[None, :, None]
     weight = jnp.sum(small[:, :experts] * mine, axis=1).reshape(-1, 1)
     slope = jnp.sum(small[:, experts : 2 * experts] * mine, axis=1).reshape(-1, 1)
+    token_blocks[0] = after(token_blocks[0], [weight, slope])
+    hidden, sw, sg, all_tokens = forward(token_blocks, w_gate, w_up, width // 4)
     keep, send = down(core, hidden, w_down, features // 4, [])
     out_near, out_second, out_far = (
         after(item, [keep]) for item in (out_near, out_second, out_far)
@@ -711,40 +736,48 @@
     grad_blocks = gather_rows(grad_out, out_peer, out_near, out_second, out_far)
     send = after(send, [out_near, out_second, out_far])
     mixed = Reduction(keep, send, tok_rows, odd)
+    grad_blocks[0] = after(grad_blocks[0], mixed.spread([], weight))
     up_grad, gate_grad, hidden, dshare, all_grads = backward(
         grad_blocks, w_down, hidden, sw, sg, weight, slope, width // 2
     )
     places = order()
     dlogit = jnp.sum(places[:, :, None] * dshare.reshape(1, -1, tok_rows), axis=1)
-    mixed.rider = dlogit.reshape(1, -1)
-    pins = mixed.spread([gate_grad], weight)
+    dlogit = dlogit.reshape(2, -1)
+    meet([mixed], [gate_grad])
+    pins = mixed.cross([])
     half = features // 2
     middle = half // 2
     tile = middle
-    keep, send = rows_back(core, gate_grad, up_grad, w_gate, w_up, 0, middle, tile, pins)
-    pins = mixed.cross([keep])
-    left = Reduction(keep, after(send, pins), tok_rows, odd)
+    keep, send = rows_back(
+        core, gate_grad, up_grad, w_gate, w_up, 0, middle, tile, pins, dlogit
+    )
+    meet([mixed], [keep])
+    pins = mixed.halve([])
+    left = Reduction(keep, after(send, pins), tok_rows, odd, dlogit)
     keep, send = rows_back(core, gate_grad, up_grad, w_gate, w_up, middle, half, tile, pins)
-    pins = mixed.halve([keep])
-    left.spread_part(0, pins)
-    right = Reduction(keep, after(send, left.keep), tok_rows, odd)
-    pins = right.spread_part(1, [])
+    meet([mixed, left], [keep])
+    pins = left.spread_part(0, [])
+    right = Reduction(keep, after(send, pins), tok_rows, odd)
+    pins = mixed.step(2, pins)
+    pins = pins + right.spread_part(1, [])
     grad_down = outer(hidden, all_grads, pins)
-    pins = left.cross_part(0, [grad_down])
-    pins = pins + mixed.step(2, [grad_down])
-    pins = pins + right.cross_part(1, [grad_down])
+    meet([left, right, mixed], [grad_down])
+    pins = left.cross_part(0, []) + right.cross_part(1, [])
+    pins = mixed.step(1, pins)
     grad_gate = outer(all_tokens, gate_grad, pins)
-    pins = left.halve_part([grad_gate])
-    pins = pins + mixed.step(1, [grad_gate])
-    pins = pins + right.halve_part([grad_gate])
+    meet([left, right, mixed], [grad_gate])
+    pins = left.halve_part([]) + right.halve_part([])
+    pins = mixed.join(pins)
     grad_up = outer(all_tokens, up_grad, pins)
-    pins = left.step(2, [grad_up])
-    pins = pins + mixed.join([grad_up])
-    pins = pins + right.step(2, [grad_up])
+    meet([left, right], [grad_up])
+    pins = left.step(2, []) + right.step(2, [])
     side = core.reshape(1, 1)
-    mixed_out, dlogit = finish([mixed], side, (), pins, "finish_mixed")
-    dlogit = dlogit.reshape(-1, tok_rows)
-
+    mixed_out = finish([mixed], side, (), pins, "finish_mixed")
+    meet([left, right], [mixed_out])
+    left.step(1, [])
+    right.step(1, [])
+    dlogit = left.rider.reshape(-1, tok_rows)
+    left.rider = None
     dlogit = jnp.sum(places[:, :, None] * dlogit[:, None, :], axis=0)
     sign = jnp.swapaxes(small[:, 2 * experts :], 1, 2)
     grad_logits = (sign * dlogit[:, :, None]).reshape(-1, experts)
@@ -753,12 +786,11 @@
     grad_router = (
         grad_router[:, 2 * experts :] + grad_router[:, experts : 2 * experts]
     ) + grad_router[:, :experts]
-    left.step(1, [grad_router])
-    right.step(1, left.keep)
-    left.join(right.keep)
+    meet([left, right], [grad_router])
+    left.join([])
     right.join([])
     extra = (grad_logits[:tok_rows], w_router.T)
-    (grad_tokens,) = finish([left, right], side, extra, [], "finish_tokens")
+    grad_tokens = finish([left, right], side, extra, [], "finish_tokens")
     return mixed_out, grad_tokens, grad_router, grad_gate[None], grad_up[None], grad_down[None]
 
 

time: 150 us -> 146 us (0.973)
  local copies, waits for them, and re-layouts: 9.33 us -> 5.16 us
  other arithmetic: 4.16 us -> 1.1 us
  matrix products: 16.9 us -> 18.8 us
  starting transfers between devices: 37 us -> 38.6 us
    ppermute x31, starting transfers between devices: 23.1 us -> 26 us  [trade(): return lax.ppermute(values, ('dp', 'expert'), pairs)]
    dot_general x1, matrix products: 0.52 us -> 2.41 us  [local_pairs(): jnp.einsum('rd,re->de', all_tokens, pieces, preferred_element_type=jnp.fl...]
    unnamed x40 -> x30, local copies, waits for them, and re-layouts: 3.26 us -> 3.3 us
  transfers between devices with their start and end apart: 40 -> 40, of which waited for: 15 -> 12; matrix products, arithmetic and copies ran while one was open for 18% -> 15% of each run, Pallas kernels for 35% -> 35%
where the time goes in v3:
time: 146 us
  Pallas kernels  53.7 us (37%)
  starting transfers between devices  38.6 us (26%)
  waiting for transfers between devices  27.3 us (19%)
  matrix products  18.8 us (13%)
  local copies, waits for them, and re-layouts  5.16 us (4%)
    ppermute x31, starting transfers between devices, trade(): return lax.ppermute(values, ('dp', 'expert'), pairs)  26 us
    pallas_call x2, Pallas kernels, rows_back(): pl.pallas_call(body, out_shape=(in_hbm((count, last - first)), in_hbm(sen...  17 us
    ppermute x31, waiting for transfers between devices, trade(): return lax.ppermute(values, ('dp', 'expert'), pairs)  16.6 us
    dot_general x3, matrix products, outer(): lax.dot_general(left, right, TN, preferred_element_type=jnp.float32)  16.4 us
    ppermute x9, starting transfers between devices, swap(): lax.ppermute(values, axis, [(place, place ^ flip) for place in range(size)])  12.6 us
    pallas_call x1, Pallas kernels, forward(): pl.pallas_call(body, out_shape=(in_hbm((count, width)),) * 3 + (in_hbm((c...  12.2 us
    ppermute x9, waiting for transfers between devices, swap(): lax.ppermute(values, axis, [(place, place ^ flip) for place in range(size)])  10.7 us
    pallas_call x1, Pallas kernels, backward(): pl.pallas_call(body, out_shape=(in_hbm((count, width)),) * 3 + (shaped((c...  9.87 us
  transfers between devices with their start and end apart: 40, of which 12 were waited for; matrix products, arithmetic and copies ran while one was open for 15% of the time, Pallas kernels for 35%

profile of v3, /device:TPU:0, one launch (start us, length us, event | category | flops | bytes accessed | tf_op | source)
XLA Modules:
  0.0 145.7 jit_solution(13140884126525746641)
XLA Ops:
  0.6 3.0 %collective-permute-start.3 = (bf16[64,3072]{1,0:T(8,128)(2,1)}, bf16[64,3072]{1,0:T(8,128)(2,1)S(1)}, u32[]{:S(2)}, u32[]{:S(2)}) collective-permute-start(bf16[64,3072]{1,0:T(8,128)(2,1)} %refs_0_), channel_id=1, source_target_pairs={{0,4},{4,0},{8,12},{12,8},{16,24},{20,28},{24,16},{28,20},{1,5},{5... | collective-permute-start | bytes 1179656 | tf_op jit(solution)/shard_map/ppermute | solution.py:442
  5.2 2.1 %route.1 = f32[12,64]{1,0:T(8,128)} custom-call(bf16[64,3072]{1,0:T(8,128)(2,1)} %refs_0_, f32[4,3072]{1,0:T(4,128)} %bitcast.33, s32[2,64]{1,0:T(2,128)} %bitcast.47, s32[4]{0:T(128)} %partner.1), custom_call_target="tpu_custom_call" | custom-call | flops 1048576 | bytes 1048576 | tf_op jit(solution)/shard_map/route/pallas_call | solution.py:141
  7.2 6.1 %collective-permute-done.3.refs_1_ = bf16[64,3072]{1,0:T(8,128)(2,1)S(1)} collective-permute-done((bf16[64,3072]{1,0:T(8,128)(2,1)}, bf16[64,3072]{1,0:T(8,128)(2,1)S(1)}, u32[]{:S(2)}, u32[]{:S(2)}) %collective-permute-start.3) | collective-permute-done | bytes 393248 | tf_op jit(solution)/shard_map/ppermute | solution.py:442
  14.8 1.6 %collective-permute-start = (f32[12,64]{1,0:T(8,128)}, f32[12,64]{1,0:T(8,128)S(1)}, u32[]{:S(2)}, u32[]{:S(2)}) collective-permute-start(f32[12,64]{1,0:T(8,128)} %route.1), channel_id=1, source_target_pairs={{0,4},{4,0},{8,12},{12,8},{16,24},{20,28},{24,16},{28,20},{1,5},{5... | collective-permute-start | bytes 9224 | tf_op jit(solution)/shard_map/ppermute | solution.py:442
  17.2 1.5 %collective-permute-done = f32[12,64]{1,0:T(8,128)S(1)} collective-permute-done((f32[12,64]{1,0:T(8,128)}, f32[12,64]{1,0:T(8,128)S(1)}, u32[]{:S(2)}, u32[]{:S(2)}) %collective-permute-start) | collective-permute-done | bytes 3104 | tf_op jit(solution)/shard_map/ppermute | solution.py:442
  19.8 2.7 %collective-permute-done.1 = f32[2,12,64]{2,0,1:T(2,128)S(1)} collective-permute-done((f32[2,12,64]{2,0,1:T(2,128)S(1)}, f32[2,12,64]{2,0,1:T(2,128)S(1)}, u32[]{:S(2)}, u32[]{:S(2)}) %collective-permute-start.1) | collective-permute-done | bytes 6176 | tf_op jit(solution)/shard_map/ppermute | solution.py:442
  24.1 2.3 %collective-permute-start.12 = (bf16[64,3072]{1,0:T(8,128)(2,1)}, bf16[64,3072]{1,0:T(8,128)(2,1)}, u32[]{:S(2)}, u32[]{:S(2)}) collective-permute-start(bf16[64,3072]{1,0:T(8,128)(2,1)} %refs_0_.1), channel_id=1, source_target_pairs={{0,12},{4,8},{8,4},{12,0},{16,28},{20,24},{24,20},{28,16},{1,13},{... | collective-permute-start | bytes 1179656 | tf_op jit(solution)/shard_map/ppermute | solution.py:442
  28.4 12.2 %forward.1 = (bf16[512,1024]{1,0:T(8,128)(2,1)}, bf16[512,1024]{1,0:T(8,128)(2,1)}, bf16[512,1024]{1,0:T(8,128)(2,1)}, bf16[512,3072]{1,0:T(8,128)(2,1)}) custom-call(bf16[64,3072]{1,0:T(8,128)(2,1)} %refs_0_, bf16[64,3072]{1,0:T(8,128)(2,1)} %copy-done.9, bf16[64,3072]{1,0:T(8,128)(2,1)} %copy-done.10, bf16[64,3072]{1,0:T(8,128)(2,1)} %copy-done.11, ...), custom_call_target="tpu_custom_call" | custom-call | flops 6442450944 | bytes 18874368 | tf_op jit(solution)/shard_map/forward/pallas_call | solution.py:217
  40.7 7.6 %down.1 = (bf16[512,1536]{1,0:T(8,128)(2,1)}, bf16[512,1536]{1,0:T(8,128)(2,1)}) custom-call(s32[1]{0:T(128)} %bitcast.core_ref, bf16[512,1024]{1,0:T(8,128)(2,1)} %get-tuple-element.97.hid.refs_9_, bf16[1024,3072]{1,0:T(8,128)(2,1)} %bitcast.41), custom_call_target="tpu_custom_call" | custom-call | flops 3221225472 | bytes 6291456 | tf_op jit(solution)/shard_map/down/pallas_call | solution.py:263
  49.8 3.6 %collective-permute-done.13.refs_1_ = bf16[512,1536]{1,0:T(8,128)(2,1)S(1)} collective-permute-done((bf16[512,1536]{1,0:T(8,128)(2,1)}, bf16[512,1536]{1,0:T(8,128)(2,1)S(1)}, u32[]{:S(2)}, u32[]{:S(2)}) %collective-permute-start.13) | collective-permute-done | bytes 1572896 | tf_op jit(solution)/shard_map/ppermute | solution.py:442
  56.0 1.7 %collective-permute-start.14 = (bf16[256,768]{1,0:T(8,128)(2,1)}, bf16[256,768]{1,0:T(8,128)(2,1)S(1)}, u32[]{:S(2)}, u32[]{:S(2)}) collective-permute-start(bf16[256,768]{1,0:T(8,128)(2,1)} %get-tuple-element.107), channel_id=1, source_target_pairs={{0,4},{4,0},{8,12},{12,8},{16,24},{20,28},{24,16},{28,20},{1,5},{5... | collective-permute-start | bytes 1179656 | tf_op jit(solution)/shard_map/ppermute | solution.py:442
  58.9 9.9 %backward.1 = (bf16[512,1024]{1,0:T(8,128)(2,1)}, bf16[512,1024]{1,0:T(8,128)(2,1)}, bf16[512,1024]{1,0:T(8,128)(2,1)}, f32[512,1]{1,0:T(8,128)S(1)}, bf16[512,3072]{1,0:T(8,128)(2,1)}) custom-call(bf16[64,3072]{1,0:T(8,128)(2,1)} %refs_0_.1, bf16[64,3072]{1,0:T(8,128)(2,1)} %collective-permute-done.10.refs_1_, ...), custom_call_target="tpu_custom_call" | custom-call | flops 3221225472 | bytes 6291456 | tf_op jit(solution)/shard_map/backward/pallas_call | solution.py:327
  70.9 8.4 %rows_back.2 = (bf16[512,768]{1,0:T(8,128)(2,1)}, bf16[528,768]{1,0:T(8,128)(2,1)}) custom-call(s32[1]{0:T(128)} %bitcast.core_ref, bf16[512,1024]{1,0:T(8,128)(2,1)} %get-tuple-element.129.gate_in, bf16[512,1024]{1,0:T(8,128)(2,1)} %get-tuple-element.120.up_in, bf16[3072,1024]{1,0:T(8,128)(2,1)} %bitcast.36, bf16[3072,1024]{1,0:T(8,128)(2,1)} %bitcast.39, ...), custom_call_target="tpu_custom_call" | custom-call | flops 3221225472 | bytes 6291456 | tf_op jit(solution)/shard_map/rows_back/pallas_call | solution.py:399
  81.1 8.6 %rows_back.3 = (bf16[512,768]{1,0:T(8,128)(2,1)}, bf16[512,768]{1,0:T(8,128)(2,1)}) custom-call(s32[1]{0:T(128)} %bitcast.core_ref, bf16[512,1024]{1,0:T(8,128)(2,1)} %get-tuple-element.129.gate_in, bf16[512,1024]{1,0:T(8,128)(2,1)} %get-tuple-element.120.up_in, bf16[3072,1024]{1,0:T(8,128)(2,1)} %bitcast.37, bf16[3072,1024]{1,0:T(8,128)(2,1)} %bitcast.40), custom_call_target="tpu_custom_call" | custom-call | flops 3221225472 | bytes 6291456 | tf_op jit(solution)/shard_map/rows_back/pallas_call | solution.py:399
  90.3 2.6 %collective-permute-start.27 = (bf16[128,768]{1,0:T(8,128)(2,1)S(1)}, bf16[128,768]{1,0:T(8,128)(2,1)S(1)}, u32[]{:S(2)}, u32[]{:S(2)}) collective-permute-start(bf16[128,768]{1,0:T(8,128)(2,1)S(1)} %step.6.refs_0_), channel_id=1, source_target_pairs={{0,2},{1,3},{2,0},{3,1},{4,6},{5,7},{6,4},{7,5},{8,10},{9,11},{10,... | collective-permute-start | bytes 589832 | tf_op jit(solution)/shard_map/ppermute | solution.py:56
  97.1 5.6 %convolution_convert_fusion.2 = bf16[1024,3072]{1,0:T(8,128)(2,1)} fusion(bf16[512,1024]{1,0:T(8,128)(2,1)S(1)} %copy-done.8, bf16[512,3072]{1,0:T(8,128)(2,1)S(1)} %copy-done.7), kind=kOutput, calls=%fused_computation.2 | convolution fusion | flops 3224371200 | bytes 10485760 | tf_op jit(solution)/shard_map/dot_general | solution.py:414
  107.3 2.0 %collective-permute-start.28 = (bf16[144,768]{1,0:T(8,128)(2,1)S(1)}, bf16[144,768]{1,0:T(8,128)(2,1)S(1)}, u32[]{:S(2)}, u32[]{:S(2)}) collective-permute-start(bf16[144,768]{1,0:T(8,128)(2,1)S(1)} %get-tuple-element.150), channel_id=1, source_target_pairs={{0,8},{4,12},{8,0},{12,4},{16,20},{20,16},{24,28},{28,24},{1,9},{5... | collective-permute-start | bytes 663560 | tf_op jit(solution)/shard_map/ppermute | solution.py:442
  109.2 5.4 %convolution_convert_fusion.1 = bf16[3072,1024]{1,0:T(8,128)(2,1)} fusion(bf16[512,3072]{1,0:T(8,128)(2,1)S(1)} %copy-done.4, bf16[512,1024]{1,0:T(8,128)(2,1)S(1)} %copy-done.6), kind=kOutput, calls=%fused_computation.1 | convolution fusion | flops 3224371200 | bytes 10485760 | tf_op jit(solution)/shard_map/dot_general | solution.py:414
  115.4 1.6 %collective-permute-start.31 = (bf16[144,384]{1,0:T(8,128)(2,1)S(1)}, bf16[144,384]{1,0:T(8,128)(2,1)S(1)}, u32[]{:S(2)}, u32[]{:S(2)}) collective-permute-start(bf16[144,384]{1,0:T(8,128)(2,1)S(1)} %get-tuple-element.162), channel_id=1, source_target_pairs={{0,1},{1,0},{2,3},{3,2},{4,5},{5,4},{6,7},{7,6},{8,9},{9,8},{10,11... | collective-permute-start | bytes 331784 | tf_op jit(solution)/shard_map/ppermute | solution.py:56
  117.0 5.4 %convolution_convert_fusion = bf16[3072,1024]{1,0:T(8,128)(2,1)} fusion(bf16[512,3072]{1,0:T(8,128)(2,1)S(1)} %copy-done.4, bf16[512,1024]{1,0:T(8,128)(2,1)S(1)} %copy-done.5), kind=kOutput, calls=%fused_computation | convolution fusion | flops 3224371200 | bytes 10485760 | tf_op jit(solution)/shard_map/dot_general | solution.py:414
  122.6 3.0 %collective-permute-start.35 = (bf16[128,384]{1,0:T(8,128)(2,1)S(1)}, bf16[128,384]{1,0:T(8,128)(2,1)S(1)}, u32[]{:S(2)}, u32[]{:S(2)}) collective-permute-start(bf16[128,384]{1,0:T(8,128)(2,1)S(1)} %step.9.refs_0_), channel_id=1, source_target_pairs={{0,2},{1,3},{2,0},{3,1},{4,6},{5,7},{6,4},{7,5},{8,10},{9,11},{10,... | collective-permute-start | bytes 294920 | tf_op jit(solution)/shard_map/ppermute | solution.py:56
  126.4 8.9 %collective-permute-done.35.refs_1_ = bf16[128,384]{1,0:T(8,128)(2,1)S(1)} collective-permute-done((bf16[128,384]{1,0:T(8,128)(2,1)S(1)}, bf16[128,384]{1,0:T(8,128)(2,1)S(1)}, u32[]{:S(2)}, u32[]{:S(2)}) %collective-permute-start.35) | collective-permute-done | bytes 98336 | tf_op jit(solution)/shard_map/ppermute | solution.py:56
  135.7 2.0 %collective-permute-start.36 = (bf16[144,384]{1,0:T(8,128)(2,1)S(1)}, bf16[144,384]{1,0:T(8,128)(2,1)S(1)}, u32[]{:S(2)}, u32[]{:S(2)}) collective-permute-start(bf16[144,384]{1,0:T(8,128)(2,1)S(1)} %get-tuple-element.173.refs_0_), channel_id=1, source_target_pairs={{0,1},{1,0},{2,3},{3,2},{4,5},{5,4},{6,7},{7,6},{8,9},{9,8},{10,11... | collective-permute-start | bytes 331784 | tf_op jit(solution)/shard_map/ppermute | solution.py:56
  138.0 2.4 %fusion.2 = f32[3072,12]{0,1:T(8,128)S(1)} fusion(bf16[512,3072]{1,0:T(8,128)(2,1)} %get-tuple-element.164, bf16[512,4]{0,1:T(4,128)(2,1)S(1)} %get-tuple-element.189, bf16[512,4]{0,1:T(4,128)(2,1)S(1)} %get-tuple-element.190, bf16[512,4]{0,1:T(4,128)(2,1)S(1)} %get-tuple-element.188), kind=kOutput, calls=%fused_computation.14 | convolution fusion | flops 37785600 | bytes 3305472 | tf_op jit(solution)/shard_map/rd,re->de/dot_general | solution.py:785
  (142 shorter events, 34.3 us)
Async XLA Ops:
  0.6 12.7 %collective-permute-start.3 = (bf16[64,3072]{1,0:T(8,128)(2,1)}, bf16[64,3072]{1,0:T(8,128)(2,1)S(1)}, u32[]{:S(2)}, u32[]{:S(2)}) collective-permute-start(bf16[64,3072]{1,0:T(8,128)(2,1)} %refs_0_), channel_id=1, source_target_pairs={{0,4},{4,0},{8,12},{12,8},{16,24},{20,28},{24,16},{28,20},{1,5},{5... | collective-permute-start | bytes 1179656 | tf_op jit(solution)/shard_map/ppermute | solution.py:442
  3.6 19.5 %collective-permute-start.4 = (bf16[64,3072]{1,0:T(8,128)(2,1)}, bf16[64,3072]{1,0:T(8,128)(2,1)S(1)}, u32[]{:S(2)}, u32[]{:S(2)}) collective-permute-start(bf16[64,3072]{1,0:T(8,128)(2,1)} %refs_0_), channel_id=1, source_target_pairs={{0,8},{4,12},{8,0},{12,4},{16,20},{20,16},{24,28},{28,24},{1,9},{5... | collective-permute-start | bytes 1179656 | tf_op jit(solution)/shard_map/ppermute | solution.py:442
  13.4 9.9 %collective-permute-start.5 = (bf16[64,3072]{1,0:T(8,128)(2,1)S(1)}, bf16[64,3072]{1,0:T(8,128)(2,1)S(1)}, u32[]{:S(2)}, u32[]{:S(2)}) collective-permute-start(bf16[64,3072]{1,0:T(8,128)(2,1)S(1)} %collective-permute-done.3.refs_1_), channel_id=1, source_target_pairs={{0,8},{4,12},{8,0},{12,4},{16,20},{20,16},{24,28},{28,24},{1,9},{5... | collective-permute-start | bytes 1179656 | tf_op jit(solution)/shard_map/ppermute | solution.py:442
  24.1 24.1 %collective-permute-start.12 = (bf16[64,3072]{1,0:T(8,128)(2,1)}, bf16[64,3072]{1,0:T(8,128)(2,1)}, u32[]{:S(2)}, u32[]{:S(2)}) collective-permute-start(bf16[64,3072]{1,0:T(8,128)(2,1)} %refs_0_.1), channel_id=1, source_target_pairs={{0,12},{4,8},{8,4},{12,0},{16,28},{20,24},{24,20},{28,16},{1,13},{... | collective-permute-start | bytes 1179656 | tf_op jit(solution)/shard_map/ppermute | solution.py:442
  26.5 21.8 %collective-permute-start.11 = (bf16[64,3072]{1,0:T(8,128)(2,1)}, bf16[64,3072]{1,0:T(8,128)(2,1)}, u32[]{:S(2)}, u32[]{:S(2)}) collective-permute-start(bf16[64,3072]{1,0:T(8,128)(2,1)} %refs_0_.1), channel_id=1, source_target_pairs={{0,8},{4,12},{8,0},{12,4},{16,20},{20,16},{24,28},{28,24},{1,9},{5... | collective-permute-start | bytes 1179656 | tf_op jit(solution)/shard_map/ppermute | solution.py:442
  27.4 20.9 %collective-permute-start.10 = (bf16[64,3072]{1,0:T(8,128)(2,1)}, bf16[64,3072]{1,0:T(8,128)(2,1)}, u32[]{:S(2)}, u32[]{:S(2)}) collective-permute-start(bf16[64,3072]{1,0:T(8,128)(2,1)} %refs_0_.1), channel_id=1, source_target_pairs={{0,4},{4,0},{8,12},{12,8},{16,24},{20,28},{24,16},{28,20},{1,5},{5... | collective-permute-start | bytes 1179656 | tf_op jit(solution)/shard_map/ppermute | solution.py:442
  48.3 9.4 %collective-permute-start.16 = (bf16[64,3072]{1,0:T(8,128)(2,1)}, bf16[64,3072]{1,0:T(8,128)(2,1)}, u32[]{:S(2)}, u32[]{:S(2)}) collective-permute-start(bf16[64,3072]{1,0:T(8,128)(2,1)} %refs_0_.1), channel_id=1, source_target_pairs={{0,16},{4,20},{8,24},{12,28},{16,0},{20,4},{24,8},{28,12},{1,17},{... | collective-permute-start | bytes 1179656 | tf_op jit(solution)/shard_map/ppermute | solution.py:442
  48.8 10.0 %collective-permute-start.18 = (bf16[64,3072]{1,0:T(8,128)(2,1)}, bf16[64,3072]{1,0:T(8,128)(2,1)}, u32[]{:S(2)}, u32[]{:S(2)}) collective-permute-start(bf16[64,3072]{1,0:T(8,128)(2,1)} %collective-permute-done.10.refs_1_), channel_id=1, source_target_pairs={{0,16},{4,20},{8,24},{12,28},{16,0},{20,4},{24,8},{28,12},{1,17},{... | collective-permute-start | bytes 1179656 | tf_op jit(solution)/shard_map/ppermute | solution.py:442
  48.9 10.0 %collective-permute-start.17 = (bf16[64,3072]{1,0:T(8,128)(2,1)}, bf16[64,3072]{1,0:T(8,128)(2,1)}, u32[]{:S(2)}, u32[]{:S(2)}) collective-permute-start(bf16[64,3072]{1,0:T(8,128)(2,1)} %collective-permute-done.11.refs_2_), channel_id=1, source_target_pairs={{0,16},{4,20},{8,24},{12,28},{16,0},{20,4},{24,8},{28,12},{1,17},{... | collective-permute-start | bytes 1179656 | tf_op jit(solution)/shard_map/ppermute | solution.py:442
  49.4 9.5 %collective-permute-start.19 = (bf16[64,3072]{1,0:T(8,128)(2,1)}, bf16[64,3072]{1,0:T(8,128)(2,1)}, u32[]{:S(2)}, u32[]{:S(2)}) collective-permute-start(bf16[64,3072]{1,0:T(8,128)(2,1)} %collective-permute-done.12.refs_3_), channel_id=1, source_target_pairs={{0,16},{4,20},{8,24},{12,28},{16,0},{20,4},{24,8},{28,12},{1,17},{... | collective-permute-start | bytes 1179656 | tf_op jit(solution)/shard_map/ppermute | solution.py:442
  56.0 13.2 %collective-permute-start.14 = (bf16[256,768]{1,0:T(8,128)(2,1)}, bf16[256,768]{1,0:T(8,128)(2,1)S(1)}, u32[]{:S(2)}, u32[]{:S(2)}) collective-permute-start(bf16[256,768]{1,0:T(8,128)(2,1)} %get-tuple-element.107), channel_id=1, source_target_pairs={{0,4},{4,0},{8,12},{12,8},{16,24},{20,28},{24,16},{28,20},{1,5},{5... | collective-permute-start | bytes 1179656 | tf_op jit(solution)/shard_map/ppermute | solution.py:442
  57.7 11.4 %collective-permute-start.15 = (bf16[256,768]{1,0:T(8,128)(2,1)S(1)}, bf16[256,768]{1,0:T(8,128)(2,1)S(1)}, u32[]{:S(2)}, u32[]{:S(2)}) collective-permute-start(bf16[256,768]{1,0:T(8,128)(2,1)S(1)} %get-tuple-element.108), channel_id=1, source_target_pairs={{0,8},{4,12},{8,0},{12,4},{16,20},{20,16},{24,28},{28,24},{1,9},{5... | collective-permute-start | bytes 1179656 | tf_op jit(solution)/shard_map/ppermute | solution.py:442
  69.4 10.0 %collective-permute-start.20 = (bf16[128,768]{1,0:T(8,128)(2,1)S(1)}, bf16[128,768]{1,0:T(8,128)(2,1)S(1)}, u32[]{:S(2)}, u32[]{:S(2)}) collective-permute-start(bf16[128,768]{1,0:T(8,128)(2,1)S(1)} %get-tuple-element.117), channel_id=1, source_target_pairs={{0,8},{4,12},{8,0},{12,4},{16,20},{20,16},{24,28},{28,24},{1,9},{5... | collective-permute-start | bytes 589832 | tf_op jit(solution)/shard_map/ppermute | solution.py:442
  70.3 9.0 %collective-permute-start.21 = (bf16[128,768]{1,0:T(8,128)(2,1)S(1)}, bf16[128,768]{1,0:T(8,128)(2,1)S(1)}, u32[]{:S(2)}, u32[]{:S(2)}) collective-permute-start(bf16[128,768]{1,0:T(8,128)(2,1)S(1)} %get-tuple-element.118), channel_id=1, source_target_pairs={{0,4},{4,0},{8,12},{12,8},{16,24},{20,28},{24,16},{28,20},{1,5},{5... | collective-permute-start | bytes 589832 | tf_op jit(solution)/shard_map/ppermute | solution.py:442
  79.6 10.2 %collective-permute-start.23 = (bf16[528,768]{1,0:T(8,128)(2,1)}, bf16[528,768]{1,0:T(8,128)(2,1)S(1)}, u32[]{:S(2)}, u32[]{:S(2)}) collective-permute-start(bf16[528,768]{1,0:T(8,128)(2,1)} %get-tuple-element.128), channel_id=1, source_target_pairs={{0,16},{4,20},{8,24},{12,28},{16,0},{20,4},{24,8},{28,12},{1,17},{... | collective-permute-start | bytes 2433032 | tf_op jit(solution)/shard_map/ppermute | solution.py:442
  79.6 10.1 %collective-permute-start.22 = (bf16[128,768]{1,0:T(8,128)(2,1)S(1)}, bf16[128,768]{1,0:T(8,128)(2,1)S(1)}, u32[]{:S(2)}, u32[]{:S(2)}) collective-permute-start(bf16[128,768]{1,0:T(8,128)(2,1)S(1)} %get-tuple-element.126), channel_id=1, source_target_pairs={{0,1},{1,0},{2,3},{3,2},{4,5},{5,4},{6,7},{7,6},{8,9},{9,8},{10,11... | collective-permute-start | bytes 589832 | tf_op jit(solution)/shard_map/ppermute | solution.py:56
  90.3 12.4 %collective-permute-start.27 = (bf16[128,768]{1,0:T(8,128)(2,1)S(1)}, bf16[128,768]{1,0:T(8,128)(2,1)S(1)}, u32[]{:S(2)}, u32[]{:S(2)}) collective-permute-start(bf16[128,768]{1,0:T(8,128)(2,1)S(1)} %step.6.refs_0_), channel_id=1, source_target_pairs={{0,2},{1,3},{2,0},{3,1},{4,6},{5,7},{6,4},{7,5},{8,10},{9,11},{10,... | collective-permute-start | bytes 589832 | tf_op jit(solution)/shard_map/ppermute | solution.py:56
  92.9 10.9 %collective-permute-start.24 = (bf16[272,768]{1,0:T(8,128)(2,1)S(1)}, bf16[272,768]{1,0:T(8,128)(2,1)S(1)}, u32[]{:S(2)}, u32[]{:S(2)}) collective-permute-start(bf16[272,768]{1,0:T(8,128)(2,1)S(1)} %get-tuple-element.135), channel_id=1, source_target_pairs={{0,4},{4,0},{8,12},{12,8},{16,24},{20,28},{24,16},{28,20},{1,5},{5... | collective-permute-start | bytes 1253384 | tf_op jit(solution)/shard_map/ppermute | solution.py:442
  95.7 8.6 %collective-permute-start.26 = (bf16[256,768]{1,0:T(8,128)(2,1)S(1)}, bf16[256,768]{1,0:T(8,128)(2,1)S(1)}, u32[]{:S(2)}, u32[]{:S(2)}) collective-permute-start(bf16[256,768]{1,0:T(8,128)(2,1)S(1)} %get-tuple-element.138), channel_id=1, source_target_pairs={{0,8},{4,12},{8,0},{12,4},{16,20},{20,16},{24,28},{28,24},{1,9},{5... | collective-permute-start | bytes 1179656 | tf_op jit(solution)/shard_map/ppermute | solution.py:442
  104.5 10.1 %collective-permute-start.30 = (bf16[128,768]{1,0:T(8,128)(2,1)S(1)}, bf16[128,768]{1,0:T(8,128)(2,1)S(1)}, u32[]{:S(2)}, u32[]{:S(2)}) collective-permute-start(bf16[128,768]{1,0:T(8,128)(2,1)S(1)} %step.7.refs_0_), channel_id=1, source_target_pairs={{0,1},{1,0},{2,3},{3,2},{4,5},{5,4},{6,7},{7,6},{8,9},{9,8},{10,11... | collective-permute-start | bytes 589832 | tf_op jit(solution)/shard_map/ppermute | solution.py:56
  105.8 8.8 %collective-permute-start.29 = (bf16[128,768]{1,0:T(8,128)(2,1)S(1)}, bf16[128,768]{1,0:T(8,128)(2,1)S(1)}, u32[]{:S(2)}, u32[]{:S(2)}) collective-permute-start(bf16[128,768]{1,0:T(8,128)(2,1)S(1)} %get-tuple-element.151), channel_id=1, source_target_pairs={{0,4},{4,0},{8,12},{12,8},{16,24},{20,28},{24,16},{28,20},{1,5},{5... | collective-permute-start | bytes 589832 | tf_op jit(solution)/shard_map/ppermute | solution.py:442
  117.0 8.5 %collective-permute-start.33 = (bf16[64,1536]{1,0:T(8,128)(2,1)S(1)}, bf16[64,1536]{1,0:T(8,128)(2,1)S(1)}, u32[]{:S(2)}, u32[]{:S(2)}) collective-permute-start(bf16[64,1536]{1,0:T(8,128)(2,1)S(1)} %get-tuple-element.170), channel_id=1, source_target_pairs={{0,16},{4,20},{8,24},{12,28},{16,0},{20,4},{24,8},{28,12},{1,17},{... | collective-permute-start | bytes 589832 | tf_op jit(solution)/shard_map/ppermute | solution.py:442
  122.5 12.9 %collective-permute-start.34 = (bf16[144,384]{1,0:T(8,128)(2,1)S(1)}, bf16[144,384]{1,0:T(8,128)(2,1)S(1)}, u32[]{:S(2)}, u32[]{:S(2)}) collective-permute-start(bf16[144,384]{1,0:T(8,128)(2,1)S(1)} %get-tuple-element.167.refs_0_), channel_id=1, source_target_pairs={{0,2},{1,3},{2,0},{3,1},{4,6},{5,7},{6,4},{7,5},{8,10},{9,11},{10,... | collective-permute-start | bytes 331784 | tf_op jit(solution)/shard_map/ppermute | solution.py:56
  122.6 12.8 %collective-permute-start.35 = (bf16[128,384]{1,0:T(8,128)(2,1)S(1)}, bf16[128,384]{1,0:T(8,128)(2,1)S(1)}, u32[]{:S(2)}, u32[]{:S(2)}) collective-permute-start(bf16[128,384]{1,0:T(8,128)(2,1)S(1)} %step.9.refs_0_), channel_id=1, source_target_pairs={{0,2},{1,3},{2,0},{3,1},{4,6},{5,7},{6,4},{7,5},{8,10},{9,11},{10,... | collective-permute-start | bytes 294920 | tf_op jit(solution)/shard_map/ppermute | solution.py:56
  (31 other events, 179.0 us)

commit v4 on v3

--- a/solution.py
+++ b/solution.py
@@ -262,7 +262,7 @@
     part = pltpu.VMEM((count, half), jnp.bfloat16)
     return pl.pallas_call(
         body,
-        out_shape=(in_hbm((count, half)),) * 2,
+        out_shape=(in_vmem((count, half)), in_hbm((count, half))),
         in_specs=[pl.BlockSpec(memory_space=pltpu.SMEM)] + [LEFT] * 2,
         out_specs=(LEFT,) * 2,
         scratch_shapes=[
@@ -398,7 +398,7 @@
     sent = (count + tail, last - first)
     return pl.pallas_call(
         body,
-        out_shape=(in_hbm((count, last - first)), in_hbm(sent)),
+        out_shape=((in_hbm if riders else in_vmem)((count, last - first)), in_hbm(sent)),
         in_specs=[pl.BlockSpec(memory_space=pltpu.SMEM)] + [LEFT] * 4 + [WHOLE] * len(riders),
         out_specs=(LEFT,) * 2,
         scratch_shapes=[flat, flat, weights, weights, part, pltpu.VMEM(sent, jnp.bfloat16)]

time: 146 us -> 145 us (level)
  starting transfers between devices: 38.6 us -> 36.8 us
  waiting for transfers between devices: 27.3 us -> 28.8 us
    unnamed x30 -> x38, local copies, waits for them, and re-layouts: 3.3 us -> 2.66 us
where the time goes in v4:
time: 145 us
  Pallas kernels  53.2 us (37%)
  starting transfers between devices  36.8 us (25%)
  waiting for transfers between devices  28.8 us (20%)
  matrix products  18.6 us (13%)
  local copies, waits for them, and re-layouts  5.24 us (4%)
    ppermute x31, starting transfers between devices, trade(): return lax.ppermute(values, ('dp', 'expert'), pairs)  24.7 us
    ppermute x31, waiting for transfers between devices, trade(): return lax.ppermute(values, ('dp', 'expert'), pairs)  16.9 us
    pallas_call x2, Pallas kernels, rows_back(): pl.pallas_call(body, out_shape=((in_hbm if riders else in_vmem)((count, l...  16.3 us
    dot_general x3, matrix products, outer(): lax.dot_general(left, right, TN, preferred_element_type=jnp.float32)  16.2 us
    pallas_call x1, Pallas kernels, forward(): pl.pallas_call(body, out_shape=(in_hbm((count, width)),) * 3 + (in_hbm((c...  12.2 us
    ppermute x9, starting transfers between devices, swap(): lax.ppermute(values, axis, [(place, place ^ flip) for place in range(size)])  12.1 us
    ppermute x9, waiting for transfers between devices, swap(): lax.ppermute(values, axis, [(place, place ^ flip) for place in range(size)])  11.9 us
    pallas_call x1, Pallas kernels, backward(): pl.pallas_call(body, out_shape=(in_hbm((count, width)),) * 3 + (shaped((c...  9.92 us
  transfers between devices with their start and end apart: 40, of which 12 were waited for; matrix products, arithmetic and copies ran while one was open for 15% of the time, Pallas kernels for 35%

profile of v4, /device:TPU:0, one launch (start us, length us, event | category | flops | bytes accessed | tf_op | source)
XLA Modules:
  0.0 144.8 jit_solution(1008018708461240880)
XLA Ops:
  0.6 3.0 %collective-permute-start.3 = (bf16[64,3072]{1,0:T(8,128)(2,1)}, bf16[64,3072]{1,0:T(8,128)(2,1)S(1)}, u32[]{:S(2)}, u32[]{:S(2)}) collective-permute-start(bf16[64,3072]{1,0:T(8,128)(2,1)} %refs_0_), channel_id=1, source_target_pairs={{0,4},{4,0},{8,12},{12,8},{16,24},{20,28},{24,16},{28,20},{1,5},{5... | collective-permute-start | bytes 1179656 | tf_op jit(solution)/shard_map/ppermute | solution.py:442
  5.2 2.1 %route.1 = f32[12,64]{1,0:T(8,128)} custom-call(bf16[64,3072]{1,0:T(8,128)(2,1)} %refs_0_, f32[4,3072]{1,0:T(4,128)} %bitcast.33, s32[2,64]{1,0:T(2,128)} %bitcast.47, s32[4]{0:T(128)} %partner.1), custom_call_target="tpu_custom_call" | custom-call | flops 1048576 | bytes 1048576 | tf_op jit(solution)/shard_map/route/pallas_call | solution.py:141
  7.2 6.1 %collective-permute-done.3.refs_1_ = bf16[64,3072]{1,0:T(8,128)(2,1)S(1)} collective-permute-done((bf16[64,3072]{1,0:T(8,128)(2,1)}, bf16[64,3072]{1,0:T(8,128)(2,1)S(1)}, u32[]{:S(2)}, u32[]{:S(2)}) %collective-permute-start.3) | collective-permute-done | bytes 393248 | tf_op jit(solution)/shard_map/ppermute | solution.py:442
  14.8 1.6 %collective-permute-start = (f32[12,64]{1,0:T(8,128)}, f32[12,64]{1,0:T(8,128)S(1)}, u32[]{:S(2)}, u32[]{:S(2)}) collective-permute-start(f32[12,64]{1,0:T(8,128)} %route.1), channel_id=1, source_target_pairs={{0,4},{4,0},{8,12},{12,8},{16,24},{20,28},{24,16},{28,20},{1,5},{5... | collective-permute-start | bytes 9224 | tf_op jit(solution)/shard_map/ppermute | solution.py:442
  17.2 1.5 %collective-permute-done = f32[12,64]{1,0:T(8,128)S(1)} collective-permute-done((f32[12,64]{1,0:T(8,128)}, f32[12,64]{1,0:T(8,128)S(1)}, u32[]{:S(2)}, u32[]{:S(2)}) %collective-permute-start) | collective-permute-done | bytes 3104 | tf_op jit(solution)/shard_map/ppermute | solution.py:442
  19.8 2.7 %collective-permute-done.1 = f32[2,12,64]{2,0,1:T(2,128)S(1)} collective-permute-done((f32[2,12,64]{2,0,1:T(2,128)S(1)}, f32[2,12,64]{2,0,1:T(2,128)S(1)}, u32[]{:S(2)}, u32[]{:S(2)}) %collective-permute-start.1) | collective-permute-done | bytes 6176 | tf_op jit(solution)/shard_map/ppermute | solution.py:442
  24.1 2.3 %collective-permute-start.12 = (bf16[64,3072]{1,0:T(8,128)(2,1)}, bf16[64,3072]{1,0:T(8,128)(2,1)}, u32[]{:S(2)}, u32[]{:S(2)}) collective-permute-start(bf16[64,3072]{1,0:T(8,128)(2,1)} %refs_0_.1), channel_id=1, source_target_pairs={{0,12},{4,8},{8,4},{12,0},{16,28},{20,24},{24,20},{28,16},{1,13},{... | collective-permute-start | bytes 1179656 | tf_op jit(solution)/shard_map/ppermute | solution.py:442
  28.5 12.2 %forward.1 = (bf16[512,1024]{1,0:T(8,128)(2,1)}, bf16[512,1024]{1,0:T(8,128)(2,1)}, bf16[512,1024]{1,0:T(8,128)(2,1)}, bf16[512,3072]{1,0:T(8,128)(2,1)}) custom-call(bf16[64,3072]{1,0:T(8,128)(2,1)} %refs_0_, bf16[64,3072]{1,0:T(8,128)(2,1)} %copy-done.12, bf16[64,3072]{1,0:T(8,128)(2,1)} %copy-done.13, bf16[64,3072]{1,0:T(8,128)(2,1)} %copy-done.14, ...), custom_call_target="tpu_custom_call" | custom-call | flops 6442450944 | bytes 18874368 | tf_op jit(solution)/shard_map/forward/pallas_call | solution.py:217
  40.8 7.6 %down.1 = (bf16[512,1536]{1,0:T(8,128)(2,1)S(1)}, bf16[512,1536]{1,0:T(8,128)(2,1)}) custom-call(s32[1]{0:T(128)} %bitcast.core_ref, bf16[512,1024]{1,0:T(8,128)(2,1)} %get-tuple-element.97.hid.refs_9_, bf16[1024,3072]{1,0:T(8,128)(2,1)} %bitcast.41), custom_call_target="tpu_custom_call" | custom-call | flops 3221225472 | bytes 6291456 | tf_op jit(solution)/shard_map/down/pallas_call | solution.py:263
  50.7 2.9 %collective-permute-done.13.refs_1_ = bf16[512,1536]{1,0:T(8,128)(2,1)S(1)} collective-permute-done((bf16[512,1536]{1,0:T(8,128)(2,1)}, bf16[512,1536]{1,0:T(8,128)(2,1)S(1)}, u32[]{:S(2)}, u32[]{:S(2)}) %collective-permute-start.13) | collective-permute-done | bytes 1572896 | tf_op jit(solution)/shard_map/ppermute | solution.py:442
  55.7 1.7 %collective-permute-start.14 = (bf16[256,768]{1,0:T(8,128)(2,1)}, bf16[256,768]{1,0:T(8,128)(2,1)S(1)}, u32[]{:S(2)}, u32[]{:S(2)}) collective-permute-start(bf16[256,768]{1,0:T(8,128)(2,1)} %get-tuple-element.107), channel_id=1, source_target_pairs={{0,4},{4,0},{8,12},{12,8},{16,24},{20,28},{24,16},{28,20},{1,5},{5... | collective-permute-start | bytes 1179656 | tf_op jit(solution)/shard_map/ppermute | solution.py:442
  58.6 9.9 %backward.1 = (bf16[512,1024]{1,0:T(8,128)(2,1)}, bf16[512,1024]{1,0:T(8,128)(2,1)}, bf16[512,1024]{1,0:T(8,128)(2,1)}, f32[512,1]{1,0:T(8,128)S(1)}, bf16[512,3072]{1,0:T(8,128)(2,1)}) custom-call(bf16[64,3072]{1,0:T(8,128)(2,1)} %refs_0_.1, bf16[64,3072]{1,0:T(8,128)(2,1)} %collective-permute-done.10.refs_1_, ...), custom_call_target="tpu_custom_call" | custom-call | flops 3221225472 | bytes 6291456 | tf_op jit(solution)/shard_map/backward/pallas_call | solution.py:327
  71.8 8.4 %rows_back.2 = (bf16[512,768]{1,0:T(8,128)(2,1)}, bf16[528,768]{1,0:T(8,128)(2,1)}) custom-call(s32[1]{0:T(128)} %bitcast.core_ref, bf16[512,1024]{1,0:T(8,128)(2,1)} %get-tuple-element.129.gate_in, bf16[512,1024]{1,0:T(8,128)(2,1)} %get-tuple-element.120.up_in, bf16[3072,1024]{1,0:T(8,128)(2,1)} %bitcast.36, bf16[3072,1024]{1,0:T(8,128)(2,1)} %bitcast.39, ...), custom_call_target="tpu_custom_call" | custom-call | flops 3221225472 | bytes 6291456 | tf_op jit(solution)/shard_map/rows_back/pallas_call | solution.py:399
  82.0 7.9 %rows_back.3 = (bf16[512,768]{1,0:T(8,128)(2,1)S(1)}, bf16[512,768]{1,0:T(8,128)(2,1)}) custom-call(s32[1]{0:T(128)} %bitcast.core_ref, bf16[512,1024]{1,0:T(8,128)(2,1)} %get-tuple-element.129.gate_in, bf16[512,1024]{1,0:T(8,128)(2,1)} %get-tuple-element.120.up_in, bf16[3072,1024]{1,0:T(8,128)(2,1)} %bitcast.37, bf16[3072,1024]{1,0:T(8,128)(2,1)} %bitcast.40), custom_call_target="tpu_custom_call" | custom-call | flops 3221225472 | bytes 6291456 | tf_op jit(solution)/shard_map/rows_back/pallas_call | solution.py:399
  90.4 2.6 %collective-permute-start.27 = (bf16[128,768]{1,0:T(8,128)(2,1)S(1)}, bf16[128,768]{1,0:T(8,128)(2,1)S(1)}, u32[]{:S(2)}, u32[]{:S(2)}) collective-permute-start(bf16[128,768]{1,0:T(8,128)(2,1)S(1)} %step.6.refs_0_), channel_id=1, source_target_pairs={{0,2},{1,3},{2,0},{3,1},{4,6},{5,7},{6,4},{7,5},{8,10},{9,11},{10,... | collective-permute-start | bytes 589832 | tf_op jit(solution)/shard_map/ppermute | solution.py:56
  96.0 5.4 %convolution_convert_fusion.2 = bf16[1024,3072]{1,0:T(8,128)(2,1)} fusion(bf16[512,1024]{1,0:T(8,128)(2,1)S(1)} %copy-done.11, bf16[512,3072]{1,0:T(8,128)(2,1)S(1)} %copy-done.10), kind=kOutput, calls=%fused_computation.2 | convolution fusion | flops 3224371200 | bytes 10485760 | tf_op jit(solution)/shard_map/dot_general | solution.py:414
  102.8 2.6 %collective-permute-done.24.refs_1_ = bf16[272,768]{1,0:T(8,128)(2,1)S(1)} collective-permute-done((bf16[272,768]{1,0:T(8,128)(2,1)S(1)}, bf16[272,768]{1,0:T(8,128)(2,1)S(1)}, u32[]{:S(2)}, u32[]{:S(2)}) %collective-permute-start.24) | collective-permute-done | bytes 417824 | tf_op jit(solution)/shard_map/ppermute | solution.py:442
  108.6 5.4 %convolution_convert_fusion.1 = bf16[3072,1024]{1,0:T(8,128)(2,1)} fusion(bf16[512,3072]{1,0:T(8,128)(2,1)S(1)} %copy-done.7, bf16[512,1024]{1,0:T(8,128)(2,1)S(1)} %copy-done.9), kind=kOutput, calls=%fused_computation.1 | convolution fusion | flops 3224371200 | bytes 10485760 | tf_op jit(solution)/shard_map/dot_general | solution.py:414
  114.3 1.6 %collective-permute-start.32 = (bf16[128,384]{1,0:T(8,128)(2,1)S(1)}, bf16[128,384]{1,0:T(8,128)(2,1)S(1)}, u32[]{:S(2)}, u32[]{:S(2)}) collective-permute-start(bf16[128,384]{1,0:T(8,128)(2,1)S(1)} %get-tuple-element.163), channel_id=1, source_target_pairs={{0,1},{1,0},{2,3},{3,2},{4,5},{5,4},{6,7},{7,6},{8,9},{9,8},{10,11... | collective-permute-start | bytes 294920 | tf_op jit(solution)/shard_map/ppermute | solution.py:56
  116.4 5.4 %convolution_convert_fusion = bf16[3072,1024]{1,0:T(8,128)(2,1)} fusion(bf16[512,3072]{1,0:T(8,128)(2,1)S(1)} %copy-done.7, bf16[512,1024]{1,0:T(8,128)(2,1)S(1)} %copy-done.8), kind=kOutput, calls=%fused_computation | convolution fusion | flops 3224371200 | bytes 10485760 | tf_op jit(solution)/shard_map/dot_general | solution.py:414
  122.1 2.8 %collective-permute-start.35 = (bf16[128,384]{1,0:T(8,128)(2,1)S(1)}, bf16[128,384]{1,0:T(8,128)(2,1)S(1)}, u32[]{:S(2)}, u32[]{:S(2)}) collective-permute-start(bf16[128,384]{1,0:T(8,128)(2,1)S(1)} %step.9.refs_0_), channel_id=1, source_target_pairs={{0,2},{1,3},{2,0},{3,1},{4,6},{5,7},{6,4},{7,5},{8,10},{9,11},{10,... | collective-permute-start | bytes 294920 | tf_op jit(solution)/shard_map/ppermute | solution.py:56
  125.7 9.1 %collective-permute-done.35.refs_1_ = bf16[128,384]{1,0:T(8,128)(2,1)S(1)} collective-permute-done((bf16[128,384]{1,0:T(8,128)(2,1)S(1)}, bf16[128,384]{1,0:T(8,128)(2,1)S(1)}, u32[]{:S(2)}, u32[]{:S(2)}) %collective-permute-start.35) | collective-permute-done | bytes 98336 | tf_op jit(solution)/shard_map/ppermute | solution.py:56
  135.2 2.0 %collective-permute-start.36 = (bf16[144,384]{1,0:T(8,128)(2,1)S(1)}, bf16[144,384]{1,0:T(8,128)(2,1)S(1)}, u32[]{:S(2)}, u32[]{:S(2)}) collective-permute-start(bf16[144,384]{1,0:T(8,128)(2,1)S(1)} %get-tuple-element.173.refs_0_), channel_id=1, source_target_pairs={{0,1},{1,0},{2,3},{3,2},{4,5},{5,4},{6,7},{7,6},{8,9},{9,8},{10,11... | collective-permute-start | bytes 331784 | tf_op jit(solution)/shard_map/ppermute | solution.py:56
  137.5 2.4 %fusion.2 = f32[3072,12]{0,1:T(8,128)S(1)} fusion(bf16[512,3072]{1,0:T(8,128)(2,1)} %get-tuple-element.164, bf16[512,4]{0,1:T(4,128)(2,1)S(1)} %get-tuple-element.189, bf16[512,4]{0,1:T(4,128)(2,1)S(1)} %get-tuple-element.190, bf16[512,4]{0,1:T(4,128)(2,1)S(1)} %get-tuple-element.188), kind=kOutput, calls=%fused_computation.14 | convolution fusion | flops 37785600 | bytes 3305472 | tf_op jit(solution)/shard_map/rd,re->de/dot_general | solution.py:785
  (150 shorter events, 34.4 us)
Async XLA Ops:
  0.6 12.7 %collective-permute-start.3 = (bf16[64,3072]{1,0:T(8,128)(2,1)}, bf16[64,3072]{1,0:T(8,128)(2,1)S(1)}, u32[]{:S(2)}, u32[]{:S(2)}) collective-permute-start(bf16[64,3072]{1,0:T(8,128)(2,1)} %refs_0_), channel_id=1, source_target_pairs={{0,4},{4,0},{8,12},{12,8},{16,24},{20,28},{24,16},{28,20},{1,5},{5... | collective-permute-start | bytes 1179656 | tf_op jit(solution)/shard_map/ppermute | solution.py:442
  3.6 19.5 %collective-permute-start.4 = (bf16[64,3072]{1,0:T(8,128)(2,1)}, bf16[64,3072]{1,0:T(8,128)(2,1)S(1)}, u32[]{:S(2)}, u32[]{:S(2)}) collective-permute-start(bf16[64,3072]{1,0:T(8,128)(2,1)} %refs_0_), channel_id=1, source_target_pairs={{0,8},{4,12},{8,0},{12,4},{16,20},{20,16},{24,28},{28,24},{1,9},{5... | collective-permute-start | bytes 1179656 | tf_op jit(solution)/shard_map/ppermute | solution.py:442
  13.4 9.9 %collective-permute-start.5 = (bf16[64,3072]{1,0:T(8,128)(2,1)S(1)}, bf16[64,3072]{1,0:T(8,128)(2,1)S(1)}, u32[]{:S(2)}, u32[]{:S(2)}) collective-permute-start(bf16[64,3072]{1,0:T(8,128)(2,1)S(1)} %collective-permute-done.3.refs_1_), channel_id=1, source_target_pairs={{0,8},{4,12},{8,0},{12,4},{16,20},{20,16},{24,28},{28,24},{1,9},{5... | collective-permute-start | bytes 1179656 | tf_op jit(solution)/shard_map/ppermute | solution.py:442
  24.1 24.3 %collective-permute-start.12 = (bf16[64,3072]{1,0:T(8,128)(2,1)}, bf16[64,3072]{1,0:T(8,128)(2,1)}, u32[]{:S(2)}, u32[]{:S(2)}) collective-permute-start(bf16[64,3072]{1,0:T(8,128)(2,1)} %refs_0_.1), channel_id=1, source_target_pairs={{0,12},{4,8},{8,4},{12,0},{16,28},{20,24},{24,20},{28,16},{1,13},{... | collective-permute-start | bytes 1179656 | tf_op jit(solution)/shard_map/ppermute | solution.py:442
  26.5 21.9 %collective-permute-start.11 = (bf16[64,3072]{1,0:T(8,128)(2,1)}, bf16[64,3072]{1,0:T(8,128)(2,1)}, u32[]{:S(2)}, u32[]{:S(2)}) collective-permute-start(bf16[64,3072]{1,0:T(8,128)(2,1)} %refs_0_.1), channel_id=1, source_target_pairs={{0,8},{4,12},{8,0},{12,4},{16,20},{20,16},{24,28},{28,24},{1,9},{5... | collective-permute-start | bytes 1179656 | tf_op jit(solution)/shard_map/ppermute | solution.py:442
  27.4 21.1 %collective-permute-start.10 = (bf16[64,3072]{1,0:T(8,128)(2,1)}, bf16[64,3072]{1,0:T(8,128)(2,1)}, u32[]{:S(2)}, u32[]{:S(2)}) collective-permute-start(bf16[64,3072]{1,0:T(8,128)(2,1)} %refs_0_.1), channel_id=1, source_target_pairs={{0,4},{4,0},{8,12},{12,8},{16,24},{20,28},{24,16},{28,20},{1,5},{5... | collective-permute-start | bytes 1179656 | tf_op jit(solution)/shard_map/ppermute | solution.py:442
  48.5 8.9 %collective-permute-start.16 = (bf16[64,3072]{1,0:T(8,128)(2,1)}, bf16[64,3072]{1,0:T(8,128)(2,1)}, u32[]{:S(2)}, u32[]{:S(2)}) collective-permute-start(bf16[64,3072]{1,0:T(8,128)(2,1)} %refs_0_.1), channel_id=1, source_target_pairs={{0,16},{4,20},{8,24},{12,28},{16,0},{20,4},{24,8},{28,12},{1,17},{... | collective-permute-start | bytes 1179656 | tf_op jit(solution)/shard_map/ppermute | solution.py:442
  49.0 9.6 %collective-permute-start.18 = (bf16[64,3072]{1,0:T(8,128)(2,1)}, bf16[64,3072]{1,0:T(8,128)(2,1)}, u32[]{:S(2)}, u32[]{:S(2)}) collective-permute-start(bf16[64,3072]{1,0:T(8,128)(2,1)} %collective-permute-done.10.refs_1_), channel_id=1, source_target_pairs={{0,16},{4,20},{8,24},{12,28},{16,0},{20,4},{24,8},{28,12},{1,17},{... | collective-permute-start | bytes 1179656 | tf_op jit(solution)/shard_map/ppermute | solution.py:442
  49.1 9.5 %collective-permute-start.17 = (bf16[64,3072]{1,0:T(8,128)(2,1)}, bf16[64,3072]{1,0:T(8,128)(2,1)}, u32[]{:S(2)}, u32[]{:S(2)}) collective-permute-start(bf16[64,3072]{1,0:T(8,128)(2,1)} %collective-permute-done.11.refs_2_), channel_id=1, source_target_pairs={{0,16},{4,20},{8,24},{12,28},{16,0},{20,4},{24,8},{28,12},{1,17},{... | collective-permute-start | bytes 1179656 | tf_op jit(solution)/shard_map/ppermute | solution.py:442
  49.5 9.1 %collective-permute-start.19 = (bf16[64,3072]{1,0:T(8,128)(2,1)}, bf16[64,3072]{1,0:T(8,128)(2,1)}, u32[]{:S(2)}, u32[]{:S(2)}) collective-permute-start(bf16[64,3072]{1,0:T(8,128)(2,1)} %collective-permute-done.12.refs_3_), channel_id=1, source_target_pairs={{0,16},{4,20},{8,24},{12,28},{16,0},{20,4},{24,8},{28,12},{1,17},{... | collective-permute-start | bytes 1179656 | tf_op jit(solution)/shard_map/ppermute | solution.py:442
  55.7 13.3 %collective-permute-start.14 = (bf16[256,768]{1,0:T(8,128)(2,1)}, bf16[256,768]{1,0:T(8,128)(2,1)S(1)}, u32[]{:S(2)}, u32[]{:S(2)}) collective-permute-start(bf16[256,768]{1,0:T(8,128)(2,1)} %get-tuple-element.107), channel_id=1, source_target_pairs={{0,4},{4,0},{8,12},{12,8},{16,24},{20,28},{24,16},{28,20},{1,5},{5... | collective-permute-start | bytes 1179656 | tf_op jit(solution)/shard_map/ppermute | solution.py:442
  57.4 11.5 %collective-permute-start.15 = (bf16[256,768]{1,0:T(8,128)(2,1)}, bf16[256,768]{1,0:T(8,128)(2,1)S(1)}, u32[]{:S(2)}, u32[]{:S(2)}) collective-permute-start(bf16[256,768]{1,0:T(8,128)(2,1)} %get-tuple-element.108), channel_id=1, source_target_pairs={{0,8},{4,12},{8,0},{12,4},{16,20},{20,16},{24,28},{28,24},{1,9},{5... | collective-permute-start | bytes 1179656 | tf_op jit(solution)/shard_map/ppermute | solution.py:442
  70.1 10.1 %collective-permute-start.20 = (bf16[128,768]{1,0:T(8,128)(2,1)S(1)}, bf16[128,768]{1,0:T(8,128)(2,1)S(1)}, u32[]{:S(2)}, u32[]{:S(2)}) collective-permute-start(bf16[128,768]{1,0:T(8,128)(2,1)S(1)} %get-tuple-element.117), channel_id=1, source_target_pairs={{0,8},{4,12},{8,0},{12,4},{16,20},{20,16},{24,28},{28,24},{1,9},{5... | collective-permute-start | bytes 589832 | tf_op jit(solution)/shard_map/ppermute | solution.py:442
  71.1 9.2 %collective-permute-start.21 = (bf16[128,768]{1,0:T(8,128)(2,1)S(1)}, bf16[128,768]{1,0:T(8,128)(2,1)S(1)}, u32[]{:S(2)}, u32[]{:S(2)}) collective-permute-start(bf16[128,768]{1,0:T(8,128)(2,1)S(1)} %get-tuple-element.118), channel_id=1, source_target_pairs={{0,4},{4,0},{8,12},{12,8},{16,24},{20,28},{24,16},{28,20},{1,5},{5... | collective-permute-start | bytes 589832 | tf_op jit(solution)/shard_map/ppermute | solution.py:442
  80.4 9.5 %collective-permute-start.23 = (bf16[528,768]{1,0:T(8,128)(2,1)}, bf16[528,768]{1,0:T(8,128)(2,1)S(1)}, u32[]{:S(2)}, u32[]{:S(2)}) collective-permute-start(bf16[528,768]{1,0:T(8,128)(2,1)} %get-tuple-element.128), channel_id=1, source_target_pairs={{0,16},{4,20},{8,24},{12,28},{16,0},{20,4},{24,8},{28,12},{1,17},{... | collective-permute-start | bytes 2433032 | tf_op jit(solution)/shard_map/ppermute | solution.py:442
  80.5 9.4 %collective-permute-start.22 = (bf16[128,768]{1,0:T(8,128)(2,1)S(1)}, bf16[128,768]{1,0:T(8,128)(2,1)S(1)}, u32[]{:S(2)}, u32[]{:S(2)}) collective-permute-start(bf16[128,768]{1,0:T(8,128)(2,1)S(1)} %get-tuple-element.126), channel_id=1, source_target_pairs={{0,1},{1,0},{2,3},{3,2},{4,5},{5,4},{6,7},{7,6},{8,9},{9,8},{10,11... | collective-permute-start | bytes 589832 | tf_op jit(solution)/shard_map/ppermute | solution.py:56
  90.4 12.3 %collective-permute-start.27 = (bf16[128,768]{1,0:T(8,128)(2,1)S(1)}, bf16[128,768]{1,0:T(8,128)(2,1)S(1)}, u32[]{:S(2)}, u32[]{:S(2)}) collective-permute-start(bf16[128,768]{1,0:T(8,128)(2,1)S(1)} %step.6.refs_0_), channel_id=1, source_target_pairs={{0,2},{1,3},{2,0},{3,1},{4,6},{5,7},{6,4},{7,5},{8,10},{9,11},{10,... | collective-permute-start | bytes 589832 | tf_op jit(solution)/shard_map/ppermute | solution.py:56
  93.1 12.3 %collective-permute-start.24 = (bf16[272,768]{1,0:T(8,128)(2,1)S(1)}, bf16[272,768]{1,0:T(8,128)(2,1)S(1)}, u32[]{:S(2)}, u32[]{:S(2)}) collective-permute-start(bf16[272,768]{1,0:T(8,128)(2,1)S(1)} %get-tuple-element.135), channel_id=1, source_target_pairs={{0,4},{4,0},{8,12},{12,8},{16,24},{20,28},{24,16},{28,20},{1,5},{5... | collective-permute-start | bytes 1253384 | tf_op jit(solution)/shard_map/ppermute | solution.py:442
  94.6 10.8 %collective-permute-start.26 = (bf16[256,768]{1,0:T(8,128)(2,1)S(1)}, bf16[256,768]{1,0:T(8,128)(2,1)S(1)}, u32[]{:S(2)}, u32[]{:S(2)}) collective-permute-start(bf16[256,768]{1,0:T(8,128)(2,1)S(1)} %get-tuple-element.138), channel_id=1, source_target_pairs={{0,8},{4,12},{8,0},{12,4},{16,20},{20,16},{24,28},{28,24},{1,9},{5... | collective-permute-start | bytes 1179656 | tf_op jit(solution)/shard_map/ppermute | solution.py:442
  105.6 8.3 %collective-permute-start.30 = (bf16[128,768]{1,0:T(8,128)(2,1)S(1)}, bf16[128,768]{1,0:T(8,128)(2,1)S(1)}, u32[]{:S(2)}, u32[]{:S(2)}) collective-permute-start(bf16[128,768]{1,0:T(8,128)(2,1)S(1)} %step.7.refs_0_), channel_id=1, source_target_pairs={{0,1},{1,0},{2,3},{3,2},{4,5},{5,4},{6,7},{7,6},{8,9},{9,8},{10,11... | collective-permute-start | bytes 589832 | tf_op jit(solution)/shard_map/ppermute | solution.py:56
  106.3 7.6 %collective-permute-start.29 = (bf16[128,768]{1,0:T(8,128)(2,1)S(1)}, bf16[128,768]{1,0:T(8,128)(2,1)S(1)}, u32[]{:S(2)}, u32[]{:S(2)}) collective-permute-start(bf16[128,768]{1,0:T(8,128)(2,1)S(1)} %get-tuple-element.151), channel_id=1, source_target_pairs={{0,4},{4,0},{8,12},{12,8},{16,24},{20,28},{24,16},{28,20},{1,5},{5... | collective-permute-start | bytes 589832 | tf_op jit(solution)/shard_map/ppermute | solution.py:442
  116.4 8.5 %collective-permute-start.33 = (bf16[64,1536]{1,0:T(8,128)(2,1)S(1)}, bf16[64,1536]{1,0:T(8,128)(2,1)S(1)}, u32[]{:S(2)}, u32[]{:S(2)}) collective-permute-start(bf16[64,1536]{1,0:T(8,128)(2,1)S(1)} %get-tuple-element.170), channel_id=1, source_target_pairs={{0,16},{4,20},{8,24},{12,28},{16,0},{20,4},{24,8},{28,12},{1,17},{... | collective-permute-start | bytes 589832 | tf_op jit(solution)/shard_map/ppermute | solution.py:442
  121.8 13.0 %collective-permute-start.34 = (bf16[144,384]{1,0:T(8,128)(2,1)S(1)}, bf16[144,384]{1,0:T(8,128)(2,1)S(1)}, u32[]{:S(2)}, u32[]{:S(2)}) collective-permute-start(bf16[144,384]{1,0:T(8,128)(2,1)S(1)} %get-tuple-element.167.refs_0_), channel_id=1, source_target_pairs={{0,2},{1,3},{2,0},{3,1},{4,6},{5,7},{6,4},{7,5},{8,10},{9,11},{10,... | collective-permute-start | bytes 331784 | tf_op jit(solution)/shard_map/ppermute | solution.py:56
  122.1 12.7 %collective-permute-start.35 = (bf16[128,384]{1,0:T(8,128)(2,1)S(1)}, bf16[128,384]{1,0:T(8,128)(2,1)S(1)}, u32[]{:S(2)}, u32[]{:S(2)}) collective-permute-start(bf16[128,384]{1,0:T(8,128)(2,1)S(1)} %step.9.refs_0_), channel_id=1, source_target_pairs={{0,2},{1,3},{2,0},{3,1},{4,6},{5,7},{6,4},{7,5},{8,10},{9,11},{10,... | collective-permute-start | bytes 294920 | tf_op jit(solution)/shard_map/ppermute | solution.py:56
  (35 other events, 202.9 us)
